TPU v7x, 32 devices: a whole 2x2x4 slice. The times are simulated.
32 devices in a mesh: plane: 4 (over y, x), tile: 8 (over z, core).
Axes of the slice: x: 2, y: 2, z: 4, core: 2. Of those that a mesh axis runs over, the one named last changes fastest.
Arguments:
- recording: bfloat16 [4, 8, 3, 4, 256, 128], P('plane', 'tile'), may hold values from -8 to 8
- start_vectors: float32 [4, 16, 32, 128], P('plane', 'tile'), may hold values from -5 to 5
- footprints: bfloat16 [4, 1024, 256], P('plane', 'tile'), may hold values from 0.00019931793 to 0.029907227
- source_row: int32 [4, 1024, 1], P('plane', 'tile'), may hold values from 0 to 5; in each aligned block of 128 rows (0 to 127, 128 to 255, ..., all dimensions but the last counted through in order) at most 32 rows name the same one
- footprint_block: int32 [4, 1024], P('plane', 'tile'), may hold values from 0 to 3
Outputs:
- temporal_factors: float32 [4, 16, 32, 128], P('plane', 'tile')
- traces: float32 [4, 1024, 128], P('plane', 'tile')
Inputs may be any that keep to these rules, and one draw needn't show every extreme that they name: `source_row`: among the 128 sources of one device at most 32 share a value, and some value is shared by exactly 32 of them.
All inputs are finite; a program needn't handle non-finite values.
Results may differ from a plain program's by a relative error of at most 0.0069.
Values may be sent and summed in bfloat16 or wider, within the bound.
No kernel may reach another device: no remote copies, remote signals or barrier semaphores. Data moves between devices by JAX's collectives and lax.ppermute only.
A program may use at most 64 MiB of HBM per device.

v0:
```python
import jax
import jax.numpy as jnp
from jax import lax
from jax.sharding import PartitionSpec as P

ITERS = 3


def from_behind(block, axis, distance):
    devices = range(lax.axis_size(axis))
    route = [(i - distance, i) for i in devices if i - distance in devices]
    return lax.ppermute(block, axis, route)


def compress_patches(patches, start_block):
    temporal = start_block
    spatial = None
    for step_index in range(ITERS):
        projection = jnp.einsum(
            "prf,pkf->prk",
            temporal.astype(jnp.bfloat16),
            patches,
            preferred_element_type=jnp.float32,
        )
        gram_matrix = jnp.einsum(
            "prk,psk->prs", projection, projection, precision=lax.Precision.HIGHEST
        )
        cholesky_factor = jnp.linalg.cholesky(gram_matrix)
        spatial = jax.scipy.linalg.solve_triangular(cholesky_factor, projection, lower=True).astype(
            jnp.bfloat16
        )
        temporal = jnp.einsum("prk,pkf->prf", spatial, patches, preferred_element_type=jnp.float32)
    return (spatial, temporal)


def on_device(recording, start_vectors, footprints, source_row, footprint_block):
    tile_count = lax.axis_size("tile")
    own_strip = recording[0, 0]
    cell_count = own_strip.shape[0]
    patch_count = cell_count - 1
    block_pixels = own_strip.shape[2]
    frame_count = own_strip.shape[3]
    pixel_total = lax.axis_size("plane") * tile_count * cell_count * 4 * block_pixels
    frame_sum = jnp.sum(own_strip, axis=(0, 1, 2), dtype=jnp.float32)
    background = lax.psum(frame_sum, ("plane", "tile")) / pixel_total
    centered = (own_strip.astype(jnp.float32) - background).astype(jnp.bfloat16)
    lower_strip = from_behind(centered, "tile", -2)
    stacked = jnp.stack([centered, lower_strip])
    patches = jnp.stack(
        [
            stacked[:, column_index : column_index + 2].reshape(16 * block_pixels, frame_count)
            for column_index in range(patch_count)
        ]
    )
    spatial, temporal = compress_patches(patches, start_vectors[0])
    rank_width = spatial.shape[1]
    temporal_rounded = temporal.astype(jnp.bfloat16)
    source_rows = source_row[0, :, 0]
    block_value = footprint_block[0]
    footprint_rows = footprints[0]
    source_count = source_rows.shape[0]
    row_span = tile_count - 2
    capacity = max(2, (3 * source_count + 2 * row_span - 1) // (2 * row_span))
    row_match = (source_rows[:, None] == jnp.arange(tile_count)[None, :]).astype(jnp.int32)
    position = jnp.sum(jnp.cumsum(row_match, axis=0) * row_match, axis=1) - 1
    slot_upper = source_rows * capacity + position
    slot_lower = (source_rows + 2) * capacity + position
    footprint_send = jnp.zeros((tile_count * capacity, 2, block_pixels), jnp.bfloat16)
    footprint_send = (
        footprint_send.at[slot_upper, 0].set(footprint_rows).at[slot_lower, 1].set(footprint_rows)
    )
    block_send = jnp.full((tile_count * capacity, 2), -1, jnp.int32)
    block_send = block_send.at[slot_upper, 0].set(block_value).at[slot_lower, 1].set(block_value)
    footprint_send = footprint_send.reshape(tile_count, capacity, 2, block_pixels)
    block_send = block_send.reshape(tile_count, capacity, 2)
    spatial_blocks = spatial.reshape(patch_count, rank_width, 16, block_pixels)
    patch_axis = jnp.arange(patch_count)[None, None, :, None]
    block_axis = jnp.arange(8)[None, None, None, :]
    footprint_in = lax.all_to_all(footprint_send, "tile", split_axis=0, concat_axis=0, tiled=True)
    codes_in = lax.all_to_all(block_send, "tile", split_axis=0, concat_axis=0, tiled=True)
    role_terms = []
    for half_index in range(2):
        strip_offset = 1 - half_index
        block_range = spatial_blocks[:, :, strip_offset * 8 : strip_offset * 8 + 8]
        projected = jnp.einsum(
            "nkb,prgb->nkpgr",
            footprint_in[:, :, half_index],
            block_range,
            preferred_element_type=jnp.float32,
        )
        block_codes = codes_in[:, :, half_index]
        column_cell = (block_codes // 4 + 1)[:, :, None, None]
        quarter = (block_codes % 4)[:, :, None, None]
        filled = (block_codes >= 0)[:, :, None, None]
        from_left = (patch_axis == column_cell - 1) & (block_axis == quarter + 4)
        from_right = (patch_axis == column_cell) & (block_axis == quarter)
        selector = ((from_left | from_right) & filled).astype(jnp.float32)
        coefficient = jnp.sum(selector[..., None] * projected, axis=3)
        role_terms.append(
            coefficient.reshape(
                coefficient.shape[0], coefficient.shape[1], patch_count * rank_width
            )
        )
    coefficient = jnp.stack(role_terms, 2).astype(jnp.bfloat16)
    replies = lax.all_to_all(coefficient, "tile", split_axis=0, concat_axis=0, tiled=True)
    reply_rows = replies.reshape(tile_count * capacity, 2, patch_count * rank_width)
    upper_coefs = reply_rows[slot_upper, 0].reshape(source_count, patch_count, rank_width)
    lower_coefs = reply_rows[slot_lower, 1].reshape(source_count, patch_count, rank_width)
    coef_table = jnp.concatenate(
        [upper_coefs, lower_coefs, jnp.zeros((source_count, 1, rank_width), jnp.bfloat16)], 1
    )
    shard_rows = lax.all_gather(temporal_rounded, "tile", axis=0, tiled=True)
    patch_number = shard_rows.shape[0]
    patch_index = jnp.arange(patch_number)
    owner_row = patch_index // patch_count
    patch_column = patch_index % patch_count
    lookup = jnp.where(
        owner_row[None, :] == source_rows[:, None],
        patch_column[None, :],
        jnp.where(
            owner_row[None, :] == source_rows[:, None] + 2,
            patch_count + patch_column[None, :],
            2 * patch_count,
        ),
    )
    weights = jnp.take_along_axis(coef_table, lookup[:, :, None], axis=1)
    weights = weights.reshape(source_count, patch_number * rank_width)
    summed = jnp.dot(
        weights,
        shard_rows.reshape(patch_number * rank_width, frame_count),
        preferred_element_type=jnp.float32,
    )
    traces = 0.25 * summed
    return (temporal[None], traces[None])


def solution(mesh):
    placed = (
        P("plane", "tile", None, None, None, None),
        P("plane", "tile", None, None),
        P("plane", "tile", None),
        P("plane", "tile", None),
        P("plane", "tile"),
    )
    return jax.shard_map(
        on_device,
        mesh=mesh,
        in_specs=placed,
        out_specs=(P("plane", "tile", None, None), P("plane", "tile", None)),
        check_vma=False,
    )
```

profile of v0, /device:TPU:0, one launch (start us, length us, event | category | flops | bytes accessed | tf_op | source)
XLA Modules:
  0.0 174.9 jit_solution(6968167123436777132)
XLA Ops:
  0.6 1.6 convert_reduce_fusion
  2.3 42.0 %psum.7 = f32[128]{0:T(128)S(1)} all-reduce(f32[128]{0:T(128)S(1)} %convert_reduce_fusion), channel_id=1, replica_groups=mesh['plane'=4,'tile'=8] {'plane','tile'}, use_global_device_ids=true, to_apply=%region_1.0 | all-reduce | flops 128 | bytes 1024 | tf_op jit(solution)/shard_map/psum | solution.py:45
  44.3 0.2 fusion.5
  44.5 1.3 collective-permute-start
  45.9 0.2 reduce_window_sum.11
  46.1 0.2 select_reduce_fusion
  46.3 6.8 %scatter_fusion = s32[256,2]{0,1:T(2,128)S(1)} fusion(s32[256,2]{0,1:T(2,128)S(1)} %broadcast_in_dim.81, s32[128]{0:T(128)S(1)} %get-tuple-element.28, s32[128]{0:T(128)S(1)} %bitcast.186), kind=kCustom, calls=%fused_computation.3 | custom fusion | bytes 2560 | tf_op jit(solution)/shard_map/scatter | solution.py:73
  53.2 6.8 %scatter_fusion.1 = s32[256,2]{0,1:T(2,128)S(1)} fusion(s32[256,2]{0,1:T(2,128)S(1)} %scatter_fusion, s32[128]{0:T(128)S(1)} %get-tuple-element.29, s32[128]{0:T(128)S(1)} %bitcast.187), kind=kCustom, calls=%fused_computation.4 | custom fusion | bytes 2560 | tf_op jit(solution)/shard_map/scatter | solution.py:73
  60.1 0.6 copy.50
  60.7 5.7 %all-to-all-start = ((s32[8,32,2]{1,2,0:T(2,128)}), s32[8,32,2]{1,2,0:T(2,128)S(1)}, u32[]{:S(2)}, u32[]{:S(2)}) async-start(s32[8,32,2]{1,2,0:T(2,128)} %copy.50), calls=%async_computation | async-start | bytes 16384 | tf_op jit(solution)/shard_map/all_to_all | solution.py:80
  66.5 0.2 fusion.3
  66.9 0.1 broadcast_in_dim.82
  67.1 6.8 %scatter_fusion.2 = bf16[256,2,256]{2,1,0:T(2,128)(2,1)S(1)} fusion(bf16[256,2,256]{2,1,0:T(2,128)(2,1)S(1)} %broadcast_in_dim.82, s32[128]{0:T(128)S(1)} %get-tuple-element.28, bf16[128,256]{1,0:T(8,128)(2,1)S(1)} %bitcast.172), kind=kCustom, calls=%fused_computation.5 | custom fusion | bytes 197632 | tf_op jit(solution)/shard_map/scatter | solution.py:70
  73.9 6.8 %scatter_fusion.3 = bf16[256,2,256]{2,1,0:T(2,128)(2,1)S(1)} fusion(bf16[256,2,256]{2,1,0:T(2,128)(2,1)S(1)} %scatter_fusion.2, s32[128]{0:T(128)S(1)} %get-tuple-element.29, bf16[128,256]{1,0:T(8,128)(2,1)S(1)} %bitcast.173), kind=kCustom, calls=%fused_computation.6 | custom fusion | bytes 197632 | tf_op jit(solution)/shard_map/scatter | solution.py:70
  80.7 0.8 copy.52
  81.6 5.1 %all-to-all-start.1 = ((bf16[8,32,2,256]{3,1,2,0:T(8,128)(2,1)}), bf16[8,32,2,256]{3,1,2,0:T(8,128)(2,1)}, u32[]{:S(2)}, u32[]{:S(2)}) async-start(bf16[8,32,2,256]{3,1,2,0:T(8,128)(2,1)} %copy.52), calls=%async_computation.1 | async-start | bytes 524288 | tf_op jit(solution)/shard_map/all_to_all | solution.py:79
  87.0 0.7 and_convert_fusion.1
  87.6 0.2 fusion.10
  87.8 0.6 copy-done.7
  88.4 0.8 fusion.25
  89.2 1.1 fusion.41
  90.4 5.9 %custom-call.24 = f32[2,32,32]{2,1,0:T(8,128)S(1)} custom-call(f32[2,32,32]{2,1,0:T(8,128)S(1)} %fusion.24), custom_call_target="Cholesky" | custom-call | tf_op jit(solution)/shard_map/jit(cholesky)/cholesky | solution.py:28
  96.5 4.9 %custom-call.25 = f32[2,1,32,32]{2,3,1,0:T(8,128)S(1)} custom-call(f32[2,1,32,32]{3,2,1,0:T(8,128)S(1)} %select_bitcast_fusion.2), custom_call_target="InvertDiagBlocksLowerTriangular" | custom-call | tf_op jit(solution)/shard_map/jit(_solve_triangular)/vmap()/triangular_solve | solution.py:29
  101.4 1.1 convolution_convert_fusion.2
  102.5 2.7 %fusion.8 = f32[2,32,4096]{2,1,0:T(8,128)S(1)} fusion(bf16[2,32,4096]{2,1,0:T(8,128)(2,1)S(1)} %convolution_convert_fusion.2, bf16[1,4096,128]{2,1,0:T(8,128)(2,1)} %bitcast.165, bf16[1,4096,128]{2,1,0:T(8,128)(2,1)S(1)} %bitcast.161), kind=kOutput, calls=%fused_computation.29 | convolution fusion | flops 136323072 | bytes 3670016 | tf_op jit(solution)/shard_map/prf,pkf->prk/dot_general | solution.py:19
  105.2 1.1 fusion.42
  106.4 5.9 %custom-call.26 = f32[2,32,32]{2,1,0:T(8,128)S(1)} custom-call(f32[2,32,32]{2,1,0:T(8,128)S(1)} %fusion.22), custom_call_target="Cholesky" | custom-call | tf_op jit(solution)/shard_map/jit(cholesky)/cholesky | solution.py:28
  112.5 4.9 %custom-call.27 = f32[2,1,32,32]{2,3,1,0:T(8,128)S(1)} custom-call(f32[2,1,32,32]{3,2,1,0:T(8,128)S(1)} %select_bitcast_fusion.1), custom_call_target="InvertDiagBlocksLowerTriangular" | custom-call | tf_op jit(solution)/shard_map/jit(_solve_triangular)/vmap()/triangular_solve | solution.py:29
  117.4 1.1 convolution_convert_fusion.1
  118.5 2.7 %fusion.9 = f32[2,32,4096]{2,1,0:T(8,128)S(1)} fusion(bf16[2,32,4096]{2,1,0:T(8,128)(2,1)S(1)} %convolution_convert_fusion.1, bf16[1,4096,128]{2,1,0:T(8,128)(2,1)} %bitcast.166, bf16[1,4096,128]{2,1,0:T(8,128)(2,1)S(1)} %bitcast.162), kind=kOutput, calls=%fused_computation.30 | convolution fusion | flops 136323072 | bytes 3670016 | tf_op jit(solution)/shard_map/prf,pkf->prk/dot_general | solution.py:19
  121.2 1.1 fusion.43
  122.4 5.9 %custom-call.28 = f32[2,32,32]{2,1,0:T(8,128)S(1)} custom-call(f32[2,32,32]{2,1,0:T(8,128)S(1)} %fusion.20), custom_call_target="Cholesky" | custom-call | tf_op jit(solution)/shard_map/jit(cholesky)/cholesky | solution.py:28
  128.5 5.1 %custom-call.29 = f32[2,1,32,32]{2,3,1,0:T(8,128)S(1)} custom-call(f32[2,1,32,32]{3,2,1,0:T(8,128)S(1)} %select_bitcast_fusion), custom_call_target="InvertDiagBlocksLowerTriangular" | custom-call | tf_op jit(solution)/shard_map/jit(_solve_triangular)/vmap()/triangular_solve | solution.py:29
  133.6 1.0 convolution_convert_fusion
  134.8 1.7 fusion
  136.5 0.1 copy.71
  136.7 1.8 %fusion.1 = bf16[8,32,2,32]{1,0,3,2:T(8,128)(2,1)S(1)} fusion(f32[8,32,2,8]{1,3,0,2:T(8,128)S(1)} %copy-done.4, bf16[2,32,16,256]{3,2,1,0:T(8,128)(2,1)S(1)} %bitcast.170, bf16[8,32,2,256]{3,1,2,0:T(8,128)(2,1)} %all-to-all-done.1), kind=kOutput, calls=%fused_computation.17 | convolution fusion | flops 67354624 | bytes 491520 | tf_op jit(solution)/shard_map/nkb,prgb->nkpgr/dot_general | solution.py:85
  138.7 0.8 reshape.613
  139.5 5.1 %all-to-all-start.2 = ((bf16[8,2,2048]{2,1,0:T(2,128)(2,1)}), bf16[8,2,2048]{2,1,0:T(2,128)(2,1)S(1)}, u32[]{:S(2)}, u32[]{:S(2)}) async-start(bf16[8,2,2048]{2,1,0:T(2,128)(2,1)} %reshape.613), calls=%async_computation.2 | async-start | bytes 131072 | tf_op jit(solution)/shard_map/all_to_all | solution.py:105
  144.6 1.1 fusion.40
  145.7 14.5 %all_gather.3 = bf16[16,32,128]{2,1,0:T(8,128)(2,1)S(1)} all-gather(bf16[2,32,128]{2,1,0:T(8,128)(2,1)S(1)} %get-tuple-element.26), channel_id=1, replica_groups=mesh['plane'=4,'tile'=8] {'tile'}, dimensions={0}, use_global_device_ids=true | all-gather | bytes 147456 | tf_op jit(solution)/shard_map/all_gather | solution.py:112
  160.2 0.1 reshape.614
  160.4 1.0 gather_fusion.1
  161.6 1.0 gather_fusion
  162.8 0.2 copy.61
  163.0 10.6 %gather_fusion.2 = bf16[2048,32]{1,0:T(8,128)(2,1)S(1)} fusion(bf16[128,5,32]{2,0,1:T(8,128)(2,1)S(1)} %copy.61, s32[2048]{0:T(1024)S(1)} %reshape.577), kind=kCustom, calls=%fused_computation.2 | custom fusion | bytes 278528 | tf_op jit(solution)/shard_map/jit(take_along_axis)/gather | solution.py:126
  173.5 0.4 copy.62
  174.0 0.9 fusion.7
  (70 shorter events, 2.3 us)
Async XLA Ops:
  0.6 43.7 %copy-start = (bf16[1,1,3,4,256,128]{5,4,3,2,1,0:T(8,128)(2,1)S(1)}, bf16[1,1,3,4,256,128]{5,4,3,2,1,0:T(8,128)(2,1)}, u32[]{:S(2)}) copy-start(bf16[1,1,3,4,256,128]{5,4,3,2,1,0:T(8,128)(2,1)} %param.8) | copy-start | bytes 2359300
  0.6 45.2 %copy-start.5 = (s32[1,128,1]{1,2,0:T(1,128)S(1)}, s32[1,128,1]{1,2,0:T(1,128)}, u32[]{:S(2)}) copy-start(s32[1,128,1]{1,2,0:T(1,128)} %param.11) | copy-start | bytes 1540
  2.3 44.0 %copy-start.6 = (s32[1,128]{1,0:T(1,128)S(1)}, s32[1,128]{1,0:T(1,128)}, u32[]{:S(2)}) copy-start(s32[1,128]{1,0:T(1,128)} %param.12) | copy-start | bytes 1540
  44.5 43.1 %collective-permute-start = (bf16[3,4,256,128]{3,2,1,0:T(8,128)(2,1)S(1)}, bf16[3,4,256,128]{3,2,1,0:T(8,128)(2,1)S(1)}, u32[]{:S(2)}, u32[]{:S(2)}) collective-permute-start(bf16[3,4,256,128]{3,2,1,0:T(8,128)(2,1)S(1)} %fusion.5), channel_id=1, source_target_pairs={{2,0},{3,1},{4,2},{5,3},{6,4},{7,5},{10,8},{11,9},{12,10},{13,11},... | collective-permute-start | bytes 2359304 | tf_op jit(solution)/shard_map/ppermute | solution.py:12
  60.0 7.0 %copy-start.3 = (bf16[1,128,256]{2,1,0:T(8,128)(2,1)S(1)}, bf16[1,128,256]{2,1,0:T(8,128)(2,1)}, u32[]{:S(2)}) copy-start(bf16[1,128,256]{2,1,0:T(8,128)(2,1)} %param.10) | copy-start | bytes 196612
  60.7 20.9 %all-to-all-start = ((s32[8,32,2]{1,2,0:T(2,128)}), s32[8,32,2]{1,2,0:T(2,128)S(1)}, u32[]{:S(2)}, u32[]{:S(2)}) async-start(s32[8,32,2]{1,2,0:T(2,128)} %copy.50), calls=%async_computation | async-start | bytes 16384 | tf_op jit(solution)/shard_map/all_to_all | solution.py:80
  81.6 53.1 %all-to-all-start.1 = ((bf16[8,32,2,256]{3,1,2,0:T(8,128)(2,1)}), bf16[8,32,2,256]{3,1,2,0:T(8,128)(2,1)}, u32[]{:S(2)}, u32[]{:S(2)}) async-start(bf16[8,32,2,256]{3,1,2,0:T(8,128)(2,1)} %copy.52), calls=%async_computation.1 | async-start | bytes 524288 | tf_op jit(solution)/shard_map/all_to_all | solution.py:79
  87.6 0.8 copy-start.7
  87.8 1.4 copy-start.1
  134.8 1.9 %copy-start.4 = (f32[8,32,2,8]{1,3,0,2:T(8,128)S(1)}, f32[8,32,2,8]{1,3,0,2:T(8,128)}, u32[]{:S(2)}) copy-start(f32[8,32,2,8]{1,3,0,2:T(8,128)} %and_convert_fusion.1) | copy-start | bytes 49156
  136.7 7.9 %copy-start.2 = (bf16[2,2,4,256,128]{4,3,2,1,0:T(8,128)(2,1)S(1)}, bf16[2,2,4,256,128]{4,3,2,1,0:T(8,128)(2,1)}, u32[]{:S(2)}) copy-start(bf16[2,2,4,256,128]{4,3,2,1,0:T(8,128)(2,1)} %copy-done.1) | copy-start | bytes 3145732
  139.5 20.7 %all-to-all-start.2 = ((bf16[8,2,2048]{2,1,0:T(2,128)(2,1)}), bf16[8,2,2048]{2,1,0:T(2,128)(2,1)S(1)}, u32[]{:S(2)}, u32[]{:S(2)}) async-start(bf16[8,2,2048]{2,1,0:T(2,128)(2,1)} %reshape.613), calls=%async_computation.2 | async-start | bytes 131072 | tf_op jit(solution)/shard_map/all_to_all | solution.py:105
where the time goes:
time: 175 us
  blocking collectives  56.5 us (32%)
  local copies, waits for them, and re-layouts  44.8 us (26%)
  other arithmetic  37 us (21%)
  matrix products  18.2 us (10%)
  starting transfers between devices  17.2 us (10%)
    psum x1, blocking collectives, on_device(): background = lax.psum(frame_sum, ('plane', 'tile')) / pixel_total  42 us
    another operation x10, other arithmetic, compress_patches(): cholesky_factor = jnp.linalg.cholesky(gram_matrix)  18.1 us
    another operation x7, other arithmetic, compress_patches(): jax.scipy.linalg.solve_triangular(cholesky_factor, projection, lower=True)  15.2 us
    all_gather x1, blocking collectives, on_device(): shard_rows = lax.all_gather(temporal_rounded, 'tile', axis=0, tiled=True)  14.5 us
    scatter x2, local copies, waits for them, and re-layouts, on_device(): block_send.at[slot_upper, 0].set(block_value).at[slot_lower, 1]  13.7 us
    scatter x2, local copies, waits for them, and re-layouts, on_device(): footprint_send.at[slot_upper, 0].set(footprint_rows).at[slot_lower, 1]  13.6 us
    gather x3, local copies, waits for them, and re-layouts, on_device(): weights = jnp.take_along_axis(coef_table, lookup[:, :, None], axis=1)  11.1 us
    dot_general x3, matrix products, compress_patches(): jnp.einsum('prf,pkf->prk', temporal.astype(jnp.bfloat16), patches, prefer...  6.26 us
  transfers between devices with their start and end apart: 4, of which 0 were waited for; matrix products, arithmetic and copies ran while one was open for 45% of the time, Pallas kernels for 0%

commit v1 on v0

v1 whole, which is shorter than its diff:
```python
import jax
import jax.numpy as jnp
from jax import lax
from jax.experimental import pallas as pl
from jax.experimental.pallas import tpu as pltpu
from jax.sharding import PartitionSpec as P

ITERS = 3
CODE_ROWS = 16
EXACT = lax.Precision.HIGHEST


def from_behind(block, axis, distance):
    devices = range(lax.axis_size(axis))
    route = [(i - distance, i) for i in devices if i - distance in devices]
    return lax.ppermute(block, axis, route)


def vmem_call(body, outs, name, flops, nbytes, in_specs=None, limit=None):
    params = pltpu.CompilerParams() if limit is None else pltpu.CompilerParams(vmem_limit_bytes=limit)
    extra = {} if in_specs is None else {"in_specs": in_specs}
    return pl.pallas_call(
        body,
        out_shape=outs,
        name=name,
        compiler_params=params,
        cost_estimate=pl.CostEstimate(flops=flops, bytes_accessed=nbytes, transcendentals=0),
        **extra,
    )


def rows_dot(left, right, precision=None):
    return lax.dot_general(
        left, right, (((1,), (1,)), ((), ())), precision=precision, preferred_element_type=jnp.float32
    )


def columns_dot(left, right):
    return lax.dot_general(left, right, (((0,), (0,)), ((), ())), preferred_element_type=jnp.float32)


def sum_body(strip_ref, row_ref, block_ref, footprint_ref, sums_ref, middle_ref, shared_ref):
    rows = strip_ref.shape[0]
    ones = jnp.ones((8, rows), jnp.bfloat16)
    total = jnp.dot(ones, strip_ref[...], preferred_element_type=jnp.float32)
    sums_ref[...] = jnp.broadcast_to(total[0:1], sums_ref.shape)
    cell = middle_ref.shape[0]
    middle_ref[...] = strip_ref[cell : 2 * cell, :]
    sources = footprint_ref.shape[0]
    shared_ref[0:sources, :] = footprint_ref[...]
    codes = jnp.concatenate([row_ref[...], block_ref[...]], 1).astype(jnp.float32)
    shared_ref[sources:, :] = jnp.broadcast_to(codes, (CODE_ROWS, codes.shape[1])).astype(jnp.bfloat16)


def gram_body(pixel_total, sums_ref, strip_ref, gram_ref, middle_ref):
    background = jnp.sum(sums_ref[...], axis=0, keepdims=True) / pixel_total
    cell = middle_ref.shape[0]
    cells = strip_ref.shape[0] // cell
    grams = []
    for index in range(cells):
        raw = strip_ref[index * cell : (index + 1) * cell, :].astype(jnp.float32)
        centered = (raw - background).astype(jnp.bfloat16)
        if index == 1:
            middle_ref[...] = centered
        grams.append(columns_dot(centered, centered))
    for column in range(cells - 1):
        gram_ref[column] = grams[column] + grams[column + 1]


def forward_solve(grams, sides):
    rank = grams[0].shape[0]
    blocks = rank // 8
    width = 128
    sub = lax.broadcasted_iota(jnp.int32, (8, width), 0)
    pad = jnp.zeros((rank, width - rank), jnp.float32)
    grams = [jnp.concatenate([gram, pad], 1) for gram in grams]

    def split(matrix):
        return [matrix[8 * b : 8 * b + 8] for b in range(blocks)]

    grams = [split(gram) for gram in grams]
    sides = [[split(side) for side in group] for group in sides]
    inverse = [[None] * blocks for _ in grams]
    for block in range(blocks):
        columns = [
            {
                (j, b): jnp.broadcast_to(gram[b][:, 8 * block + j : 8 * block + j + 1], (8, width))
                for j in range(8)
                for b in range(block, blocks)
            }
            for gram in grams
        ]
        for j in range(8):
            for patch in range(len(grams)):
                column, gram = columns[patch], grams[patch]
                pivot = 1.0 / jnp.broadcast_to(column[(j, block)][j : j + 1, :], (8, width))
                known = inverse[patch][block]
                inverse[patch][block] = pivot if known is None else jnp.where(sub == j, pivot, known)
                factor = {b: column[(j, b)] * pivot for b in range(block, blocks)}
                factor[block] = jnp.where(sub > j, factor[block], 0.0)
                for later in range(j + 1, 8):
                    entry = jnp.broadcast_to(column[(j, block)][later : later + 1, :], (8, width))
                    for b in range(block, blocks):
                        column[(later, b)] = column[(later, b)] - factor[b] * entry
                for target in [gram] + sides[patch]:
                    row = jnp.broadcast_to(target[block][j : j + 1, :], (8, width))
                    for b in range(block, blocks):
                        target[b] = target[b] - factor[b] * row
    return [
        [
            jnp.concatenate([m * lax.sqrt(d) for m, d in zip(side, inverse[patch])], 0)
            for side in group
        ]
        for patch, group in enumerate(sides)
    ]


def three_parts(value):
    high = value.astype(jnp.bfloat16)
    rest = value - high.astype(jnp.float32)
    middle = rest.astype(jnp.bfloat16)
    low = (rest - middle.astype(jnp.float32)).astype(jnp.bfloat16)
    return [high, middle, low]


def patch_body(
    pixel_total, place_ref, own_gram_ref, low_gram_ref, sums_ref, own_ref, low_ref, start_ref,
    shared_ref, temporal_ref, reply_ref,
):
    patches, rank = start_ref.shape[0], start_ref.shape[1]
    grams = [own_gram_ref[p] + low_gram_ref[p] for p in range(patches)]
    temporal = [start_ref[p] for p in range(patches)]
    whitened = None
    for step in range(ITERS):
        rounded = [t.astype(jnp.bfloat16).astype(jnp.float32) for t in temporal]
        moved = [jnp.dot(t, g, precision=EXACT, preferred_element_type=jnp.float32) for t, g in zip(rounded, grams)]
        inner = [rows_dot(m, t, EXACT) for m, t in zip(moved, rounded)]
        last = step == ITERS - 1
        solved = forward_solve(inner, [[m, t] if last else [m] for m, t in zip(moved, rounded)])
        temporal = [s[0] for s in solved]
        if last:
            whitened = jnp.concatenate([s[1] for s in solved], 0)
    for p in range(patches):
        temporal_ref[p] = temporal[p]
    ranks = patches * rank
    temporal_rounded = jnp.concatenate(temporal, 0).astype(jnp.bfloat16)
    background = jnp.sum(sums_ref[...], axis=0, keepdims=True) / pixel_total
    lower = (low_ref[...].astype(jnp.float32) - background).astype(jnp.bfloat16)
    parts = jnp.concatenate(three_parts(whitened), 0)
    pixels = 256
    bands = []
    for centered in (lower, own_ref[...]):
        sums = rows_dot(parts, centered)
        spatial = (sums[:ranks] + sums[ranks : 2 * ranks] + sums[2 * ranks :]).astype(jnp.bfloat16)
        bands += [spatial[:, q * pixels : (q + 1) * pixels] for q in range(4)]
    stacked = jnp.concatenate(bands, 0)
    place = place_ref[0]
    owners, sources = reply_ref.shape[0], reply_ref.shape[2]

    def one_owner(owner):
        projected = rows_dot(stacked, shared_ref[owner, 0:sources, :])
        codes = shared_ref[owner, sources : sources + 1, :].astype(jnp.float32)
        code_row = codes[:, 0:sources].astype(jnp.int32)
        code_quarter = codes[:, sources : 2 * sources].astype(jnp.int32)
        total = jnp.zeros((ranks, sources), jnp.float32)
        for role in range(2):
            for quarter in range(4):
                start = (role * 4 + quarter) * ranks
                chosen = (code_row == place - 2 * role) & (code_quarter == quarter)
                total = total + jnp.where(chosen, projected[start : start + ranks], 0.0)
        reply_ref[owner, 0:ranks, :] = total.astype(jnp.bfloat16)
        reply_ref[owner, ranks:, :] = temporal_rounded

    if owners <= 8:
        for owner in range(owners):
            one_owner(owner)
    else:
        pl.loop(0, owners)(one_owner)


def trace_body(reply_ref, traces_ref):
    owners, rows = reply_ref.shape[0], reply_ref.shape[1]
    ranks = rows // 2
    group = min(owners, 8)

    def one_group(first):
        coefficient = reply_ref[pl.ds(first, group), 0:ranks, :].reshape(group * ranks, -1)
        temporal = reply_ref[pl.ds(first, group), ranks:, :].reshape(group * ranks, -1)
        return columns_dot(coefficient, temporal)

    if owners == group:
        traces_ref[...] = 0.25 * one_group(0)
    else:
        traces_ref[...] = lax.fori_loop(
            0, owners // group, lambda i, total: total + 0.25 * one_group(i * group), jnp.zeros_like(traces_ref[...])
        )


def on_device(recording, start_vectors, footprints, source_row, footprint_block):
    tile_count = lax.axis_size("tile")
    plane_count = lax.axis_size("plane")
    devices = tile_count * plane_count
    cells, quarters, pixels, frames = recording.shape[2:]
    cell = quarters * pixels
    strip = recording.reshape(cells * cell, frames)
    start = start_vectors[0]
    patches, rank = start.shape[0], start.shape[1]
    sources = footprints.shape[1]
    pixel_total = devices * cells * cell
    f32, bf16 = jnp.float32, jnp.bfloat16

    def shape(dims, kind):
        return jax.ShapeDtypeStruct(dims, kind)

    sums, middle, shared = vmem_call(
        sum_body,
        [shape((devices, frames), f32), shape((cell, frames), bf16), shape((sources + CODE_ROWS, pixels), bf16)],
        "frame_sums",
        2 * cells * cell * frames,
        2 * cells * cell * frames,
    )(strip, source_row.reshape(1, sources), footprint_block.reshape(1, sources), footprints[0])
    all_sums = lax.all_to_all(sums, ("plane", "tile"), 0, 0, tiled=True)
    shared_all = lax.all_gather(shared, "tile", axis=0)
    low_middle = from_behind(middle, "tile", -2)
    own_gram, own_middle = vmem_call(
        lambda *refs: gram_body(pixel_total, *refs),
        [shape((patches, frames, frames), f32), shape((cell, frames), bf16)],
        "own_grams",
        2 * cells * cell * frames * frames,
        2 * cells * cell * frames,
    )(all_sums, strip)
    low_gram = from_behind(own_gram, "tile", -2)
    place = lax.axis_index("tile").astype(jnp.int32).reshape(1)
    whole = pl.BlockSpec(memory_space=pltpu.VMEM)
    temporal, reply = vmem_call(
        lambda *refs: patch_body(pixel_total, *refs),
        [shape((patches, rank, frames), f32), shape((tile_count, 2 * patches * rank, sources), bf16)],
        "patch_factors",
        2 * 1024 * 512 * 256,
        4 << 20,
        in_specs=[pl.BlockSpec(memory_space=pltpu.SMEM)] + [whole] * 7,
        limit=None if tile_count <= 8 else 40 << 20,
    )(place, own_gram, low_gram, all_sums, own_middle, low_middle, start, shared_all)
    answers = lax.all_to_all(reply, "tile", 0, 0, tiled=True)
    traces = vmem_call(
        trace_body,
        shape((sources, frames), f32),
        "source_traces",
        2 * sources * frames * patches * rank * tile_count,
        2 * answers.size,
    )(answers)
    return (temporal[None], traces[None])


def solution(mesh):
    placed = (
        P("plane", "tile", None, None, None, None),
        P("plane", "tile", None, None),
        P("plane", "tile", None),
        P("plane", "tile", None),
        P("plane", "tile"),
    )
    return jax.shard_map(
        on_device,
        mesh=mesh,
        in_specs=placed,
        out_specs=(P("plane", "tile", None, None), P("plane", "tile", None)),
        check_vma=False,
    )
```

time: 175 us -> 61.9 us (0.35)
  local copies, waits for them, and re-layouts: 44.8 us -> 1.37 us
  other arithmetic: 37 us -> 0 us
  blocking collectives: 56.5 us -> 31.1 us
  matrix products: 18.2 us -> 0 us
  Pallas kernels: 0 us -> 12.8 us
  starting transfers between devices: 17.2 us -> 9.87 us
  waiting for transfers between devices: 0.01 us -> 5.77 us
    psum x1 -> x0, blocking collectives: 42 us -> none  [on_device(): background = lax.psum(frame_sum, ('plane', 'tile')) / pixel_total]
    another operation x19 -> x0, other arithmetic: 33.6 us -> none  [the longest x10 18.1 us: compress_patches(): cholesky_factor = jnp.linalg.cholesky(gram_matrix)]
    scatter x4 -> x0, local copies, waits for them, and re-layouts: 27.3 us -> none  [the longest x2 13.7 us: on_device(): block_send.at[slot_upper, 0].set(block_value).at[slot_lower, 1]]
    dot_general x10 -> x0, matrix products: 15 us -> none  [the longest x3 6.26 us: compress_patches(): jnp.einsum('prf,pkf->prk', temporal.astype(jnp.bfloat16), patches, prefer...]
    all_to_all x0 -> x1, blocking collectives: none -> 13.8 us  [on_device(): answers = lax.all_to_all(reply, 'tile', 0, 0, tiled=True)]
    gather x7 -> x0, local copies, waits for them, and re-layouts: 13.3 us -> none  [the longest x3 11.1 us: on_device(): weights = jnp.take_along_axis(coef_table, lookup[:, :, None], axis=1)]
    pallas_call x0 -> x4, Pallas kernels: none -> 12.8 us  [the longest x1 6.7 us: on_device(): vmem_call(lambda *refs: patch_body(pixel_total, *refs), [shape((patches,...]
    all_to_all x3 -> x1, starting transfers between devices: 15.9 us -> 7.3 us  [on_device(): all_sums = lax.all_to_all(sums, ('plane', 'tile'), 0, 0, tiled=True)]
  transfers between devices with their start and end apart: 4 -> 3, of which waited for: 0 -> 1; matrix products, arithmetic and copies ran while one was open for 45% -> 0% of each run, Pallas kernels for 0% -> 4%
where the time goes in v1:
time: 61.9 us; the launch traced here: 61.5 us
  blocking collectives  31.1 us (50%)
  Pallas kernels  12.8 us (21%)
  starting transfers between devices  9.87 us (16%)
  waiting for transfers between devices  5.77 us (9%)
  local copies, waits for them, and re-layouts  1.37 us (2%)
  between operations  0.68 us (1%)
    all_gather x1, blocking collectives, on_device(): shared_all = lax.all_gather(shared, 'tile', axis=0)  17.3 us
    all_to_all x1, blocking collectives, on_device(): answers = lax.all_to_all(reply, 'tile', 0, 0, tiled=True)  13.8 us
    all_to_all x1, starting transfers between devices, on_device(): all_sums = lax.all_to_all(sums, ('plane', 'tile'), 0, 0, tiled=True)  7.3 us
    pallas_call x1, Pallas kernels, on_device(): vmem_call(lambda *refs: patch_body(pixel_total, *refs), [shape((patches,...  6.7 us
    all_to_all x1, waiting for transfers between devices, on_device(): all_sums = lax.all_to_all(sums, ('plane', 'tile'), 0, 0, tiled=True)  5.77 us
    ppermute x2, starting transfers between devices, from_behind(): return lax.ppermute(block, axis, route)  2.57 us
    pallas_call x1, Pallas kernels, on_device(): vmem_call(lambda *refs: gram_body(pixel_total, *refs), [shape((patches, f...  2.25 us
    pallas_call x1, Pallas kernels, on_device(): vmem_call(sum_body, [shape((devices, frames), f32), shape((cell, frames),...  2.03 us
  transfers between devices with their start and end apart: 3, of which 1 were waited for; matrix products, arithmetic and copies ran while one was open for 0% of the time, Pallas kernels for 4%

profile of v1, /device:TPU:0, one launch (start us, length us, event | category | flops | bytes accessed | tf_op | source)
XLA Modules:
  0.0 61.5 jit_solution(10506015071446403907)
XLA Ops:
  0.6 2.0 %frame_sums.1 = (f32[32,128]{1,0:T(8,128)}, bf16[1024,128]{1,0:T(8,128)(2,1)}, bf16[144,256]{1,0:T(8,128)(2,1)}) custom-call(bf16[3072,128]{1,0:T(8,128)(2,1)} %bitcast.12, s32[1,128]{1,0:T(1,128)} %bitcast.21, s32[1,128]{1,0:T(1,128)} %block_ref.1, bf16[128,256]{1,0:T(8,128)(2,1)} %bitcast.18), custom_call_target="tpu_custom_call" | custom-call | flops 786432 | bytes 786432 | tf_op jit(solution)/shard_map/frame_sums/pallas_call | solution.py:215
  2.7 7.3 %all-to-all-start = ((f32[32,1,128]{2,1,0:T(1,128)}), f32[32,1,128]{2,1,0:T(1,128)S(1)}, u32[]{:S(2)}, u32[]{:S(2)}) async-start(f32[32,1,128]{2,1,0:T(1,128)} %bitcast.20), calls=%async_computation | async-start | bytes 32768 | tf_op jit(solution)/shard_map/all_to_all | solution.py:222
  10.0 1.3 %collective-permute-start.1 = (bf16[1024,128]{1,0:T(8,128)(2,1)}, bf16[1024,128]{1,0:T(8,128)(2,1)S(1)}, u32[]{:S(2)}, u32[]{:S(2)}) collective-permute-start(bf16[1024,128]{1,0:T(8,128)(2,1)} %get-tuple-element.12), channel_id=1, source_target_pairs={{2,0},{3,1},{4,2},{5,3},{6,4},{7,5},{10,8},{11,9},{12,10},{13,11},... | collective-permute-start | bytes 786440 | tf_op jit(solution)/shard_map/ppermute | solution.py:16
  11.3 5.8 %all-to-all-done = f32[32,1,128]{2,1,0:T(1,128)S(1)} async-done(((f32[32,1,128]{2,1,0:T(1,128)}), f32[32,1,128]{2,1,0:T(1,128)S(1)}, u32[]{:S(2)}, u32[]{:S(2)}) %all-to-all-start) | async-done | bytes 16416 | tf_op jit(solution)/shard_map/all_to_all | solution.py:222
  17.0 0.0 copy-start.1
  17.0 0.6 copy-done.1
  17.6 0.0 copy-start.3
  17.6 2.3 %own_grams.1 = (f32[2,128,128]{2,1,0:T(8,128)}, bf16[1024,128]{1,0:T(8,128)(2,1)}) custom-call(f32[32,128]{1,0:T(8,128)} %bitcast.15, bf16[3072,128]{1,0:T(8,128)(2,1)} %bitcast.13), custom_call_target="tpu_custom_call" | custom-call | flops 100663296 | bytes 786432 | tf_op jit(solution)/shard_map/own_grams/pallas_call | solution.py:225
  19.9 1.3 %collective-permute-start = (f32[2,128,128]{2,1,0:T(8,128)}, f32[2,128,128]{2,1,0:T(8,128)S(1)}, u32[]{:S(2)}, u32[]{:S(2)}) collective-permute-start(f32[2,128,128]{2,1,0:T(8,128)} %get-tuple-element.10.refs_1_), channel_id=1, source_target_pairs={{2,0},{3,1},{4,2},{5,3},{6,4},{7,5},{10,8},{11,9},{12,10},{13,11},... | collective-permute-start | bytes 393224 | tf_op jit(solution)/shard_map/ppermute | solution.py:16
  21.2 0.0 copy-done.3
  21.2 17.3 %all-gather = bf16[1152,256]{1,0:T(8,128)(2,1)} all-gather(bf16[144,256]{1,0:T(8,128)(2,1)S(1)} %copy-done.3), channel_id=2, replica_groups=mesh['plane'=4,'tile'=8] {'tile'}, dimensions={0}, use_global_device_ids=true | all-gather | bytes 663552 | tf_op jit(solution)/shard_map/all_gather | solution.py:223
  38.5 0.0 collective-permute-done.refs_2_
  38.5 0.0 copy-start.2
  38.5 0.0 collective-permute-done.1.refs_5_
  38.5 0.0 copy-start
  38.5 0.6 %copy-done.2 = f32[2,128,128]{2,1,0:T(8,128)} copy-done((f32[2,128,128]{2,1,0:T(8,128)}, f32[2,128,128]{2,1,0:T(8,128)S(1)}, u32[]{:S(2)}) %copy-start.2) | copy-done | bytes 131096
  39.1 0.1 copy-done
  39.2 6.7 %patch_factors.1 = (f32[2,32,128]{2,1,0:T(8,128)}, bf16[8,128,128]{2,1,0:T(8,128)(2,1)}) custom-call(s32[1]{0:T(128)} %bitcast.refs_0_, f32[2,128,128]{2,1,0:T(8,128)} %get-tuple-element.10.refs_1_, f32[2,128,128]{2,1,0:T(8,128)} %copy-done.2, f32[32,128]{1,0:T(8,128)} %bitcast.16, bf16[1024,128]{1,0:T(8,128)(2,1)} %get-tuple-element.11.refs_4_, ...), custom_call_target="tpu_custom_call" | custom-call | flops 268435456 | bytes 4194304 | tf_op jit(solution)/shard_map/patch_factors/pallas_call | solution.py:235
  46.0 13.8 %all_to_all.16.reply_ref = bf16[8,128,128]{2,1,0:T(8,128)(2,1)} all-to-all(bf16[8,128,128]{2,1,0:T(8,128)(2,1)} %get-tuple-element.15), channel_id=1, replica_groups=mesh['plane'=4,'tile'=8] {'tile'}, dimensions={0} | all-to-all | bytes 524288 | tf_op jit(solution)/shard_map/all_to_all | solution.py:244
  59.7 1.8 %source_traces.1 = f32[128,128]{1,0:T(8,128)} custom-call(bf16[8,128,128]{2,1,0:T(8,128)(2,1)} %all_to_all.16.reply_ref), custom_call_target="tpu_custom_call" | custom-call | flops 16777216 | bytes 262144 | tf_op jit(solution)/shard_map/source_traces/pallas_call | solution.py:245
Async XLA Ops:
  2.7 14.4 %all-to-all-start = ((f32[32,1,128]{2,1,0:T(1,128)}), f32[32,1,128]{2,1,0:T(1,128)S(1)}, u32[]{:S(2)}, u32[]{:S(2)}) async-start(f32[32,1,128]{2,1,0:T(1,128)} %bitcast.20), calls=%async_computation | async-start | bytes 32768 | tf_op jit(solution)/shard_map/all_to_all | solution.py:222
  10.0 28.5 %collective-permute-start.1 = (bf16[1024,128]{1,0:T(8,128)(2,1)}, bf16[1024,128]{1,0:T(8,128)(2,1)S(1)}, u32[]{:S(2)}, u32[]{:S(2)}) collective-permute-start(bf16[1024,128]{1,0:T(8,128)(2,1)} %get-tuple-element.12), channel_id=1, source_target_pairs={{2,0},{3,1},{4,2},{5,3},{6,4},{7,5},{10,8},{11,9},{12,10},{13,11},... | collective-permute-start | bytes 786440 | tf_op jit(solution)/shard_map/ppermute | solution.py:16
  17.0 0.6 copy-start.1
  17.6 3.5 %copy-start.3 = (bf16[144,256]{1,0:T(8,128)(2,1)S(1)}, bf16[144,256]{1,0:T(8,128)(2,1)}, u32[]{:S(2)}) copy-start(bf16[144,256]{1,0:T(8,128)(2,1)} %get-tuple-element.13) | copy-start | bytes 221188
  19.9 18.6 %collective-permute-start = (f32[2,128,128]{2,1,0:T(8,128)}, f32[2,128,128]{2,1,0:T(8,128)S(1)}, u32[]{:S(2)}, u32[]{:S(2)}) collective-permute-start(f32[2,128,128]{2,1,0:T(8,128)} %get-tuple-element.10.refs_1_), channel_id=1, source_target_pairs={{2,0},{3,1},{4,2},{5,3},{6,4},{7,5},{10,8},{11,9},{12,10},{13,11},... | collective-permute-start | bytes 393224 | tf_op jit(solution)/shard_map/ppermute | solution.py:16
  38.5 0.7 %copy-start.2 = (f32[2,128,128]{2,1,0:T(8,128)}, f32[2,128,128]{2,1,0:T(8,128)S(1)}, u32[]{:S(2)}) copy-start(f32[2,128,128]{2,1,0:T(8,128)S(1)} %collective-permute-done.refs_2_) | copy-start | bytes 393220
  38.5 0.8 %copy-start = (bf16[1024,128]{1,0:T(8,128)(2,1)}, bf16[1024,128]{1,0:T(8,128)(2,1)S(1)}, u32[]{:S(2)}) copy-start(bf16[1024,128]{1,0:T(8,128)(2,1)S(1)} %collective-permute-done.1.refs_5_) | copy-start | bytes 786436

commit v2 on v1

--- a/solution.py
+++ b/solution.py
@@ -17,7 +17,7 @@
 
 
 def vmem_call(body, outs, name, flops, nbytes, in_specs=None, limit=None):
-    params = pltpu.CompilerParams() if limit is None else pltpu.CompilerParams(vmem_limit_bytes=limit)
+    params = pltpu.CompilerParams(vmem_limit_bytes=12 << 20) if limit is None else pltpu.CompilerParams(vmem_limit_bytes=limit)
     extra = {} if in_specs is None else {"in_specs": in_specs}
     return pl.pallas_call(
         body,
@@ -123,11 +123,8 @@
     return [high, middle, low]
 
 
-def patch_body(
-    pixel_total, place_ref, own_gram_ref, low_gram_ref, sums_ref, own_ref, low_ref, start_ref,
-    shared_ref, temporal_ref, reply_ref,
-):
-    patches, rank = start_ref.shape[0], start_ref.shape[1]
+def patch_body(own_gram_ref, low_gram_ref, start_ref, temporal_ref, parts_ref, rounded_ref):
+    patches = start_ref.shape[0]
     grams = [own_gram_ref[p] + low_gram_ref[p] for p in range(patches)]
     temporal = [start_ref[p] for p in range(patches)]
     whitened = None
@@ -142,11 +139,17 @@
             whitened = jnp.concatenate([s[1] for s in solved], 0)
     for p in range(patches):
         temporal_ref[p] = temporal[p]
-    ranks = patches * rank
-    temporal_rounded = jnp.concatenate(temporal, 0).astype(jnp.bfloat16)
+    rounded_ref[...] = jnp.concatenate(temporal, 0).astype(jnp.bfloat16)
+    parts_ref[...] = jnp.concatenate(three_parts(whitened), 0)
+
+
+def reply_body(pixel_total, place_ref, parts_ref, rounded_ref, sums_ref, own_ref, low_ref, *refs):
+    shared_refs, reply_ref = refs[:-1], refs[-1]
+    parts = parts_ref[...]
+    temporal_rounded = rounded_ref[...]
+    ranks = temporal_rounded.shape[0]
     background = jnp.sum(sums_ref[...], axis=0, keepdims=True) / pixel_total
     lower = (low_ref[...].astype(jnp.float32) - background).astype(jnp.bfloat16)
-    parts = jnp.concatenate(three_parts(whitened), 0)
     pixels = 256
     bands = []
     for centered in (lower, own_ref[...]):
@@ -157,9 +160,13 @@
     place = place_ref[0]
     owners, sources = reply_ref.shape[0], reply_ref.shape[2]
 
-    def one_owner(owner):
-        projected = rows_dot(stacked, shared_ref[owner, 0:sources, :])
-        codes = shared_ref[owner, sources : sources + 1, :].astype(jnp.float32)
+    bits = owners.bit_length() - 1
+
+    def one_owner(shared_ref, entry, order):
+        offset = sum(((order >> t) & 1) << (bits - 1 - t) for t in range(bits))
+        owner = lax.bitwise_xor(place, jnp.int32(offset))
+        projected = rows_dot(stacked, shared_ref[entry, 0:sources, :])
+        codes = shared_ref[entry, sources : sources + 1, :].astype(jnp.float32)
         code_row = codes[:, 0:sources].astype(jnp.int32)
         code_quarter = codes[:, sources : 2 * sources].astype(jnp.int32)
         total = jnp.zeros((ranks, sources), jnp.float32)
@@ -171,11 +178,15 @@
         reply_ref[owner, 0:ranks, :] = total.astype(jnp.bfloat16)
         reply_ref[owner, ranks:, :] = temporal_rounded
 
-    if owners <= 8:
-        for owner in range(owners):
-            one_owner(owner)
-    else:
-        pl.loop(0, owners)(one_owner)
+    offset = 0
+    for shared_ref in shared_refs:
+        count = shared_ref.shape[0]
+        if owners <= 8:
+            for entry in range(count):
+                one_owner(shared_ref, entry, offset + entry)
+        else:
+            pl.loop(0, count)(lambda entry, ref=shared_ref, first=offset: one_owner(ref, entry, first + entry))
+        offset += count
 
 
 def trace_body(reply_ref, traces_ref):
@@ -220,7 +231,6 @@
         2 * cells * cell * frames,
     )(strip, source_row.reshape(1, sources), footprint_block.reshape(1, sources), footprints[0])
     all_sums = lax.all_to_all(sums, ("plane", "tile"), 0, 0, tiled=True)
-    shared_all = lax.all_gather(shared, "tile", axis=0)
     low_middle = from_behind(middle, "tile", -2)
     own_gram, own_middle = vmem_call(
         lambda *refs: gram_body(pixel_total, *refs),
@@ -230,17 +240,33 @@
         2 * cells * cell * frames,
     )(all_sums, strip)
     low_gram = from_behind(own_gram, "tile", -2)
+    held = [shared[None]]
+    bits = tile_count.bit_length() - 1
+    for bit in reversed(range(bits)):
+        route = [(i, i ^ (1 << bit)) for i in range(tile_count)]
+        everything = held[0] if len(held) == 1 else jnp.concatenate(held, 0)
+        if len(held) == 2:
+            everything, own_gram = lax.optimization_barrier((everything, own_gram))
+        held.append(lax.ppermute(everything, "tile", route))
     place = lax.axis_index("tile").astype(jnp.int32).reshape(1)
     whole = pl.BlockSpec(memory_space=pltpu.VMEM)
-    temporal, reply = vmem_call(
-        lambda *refs: patch_body(pixel_total, *refs),
-        [shape((patches, rank, frames), f32), shape((tile_count, 2 * patches * rank, sources), bf16)],
+    ranks = patches * rank
+    temporal, parts, rounded = vmem_call(
+        patch_body,
+        [shape((patches, rank, frames), f32), shape((3 * ranks, frames), bf16), shape((ranks, frames), bf16)],
         "patch_factors",
+        6 * 10**9,
+        1 << 20,
+    )(own_gram, low_gram, start)
+    (reply,) = vmem_call(
+        lambda *refs: reply_body(pixel_total, *refs),
+        [shape((tile_count, 2 * ranks, sources), bf16)],
+        "coefficients",
         2 * 1024 * 512 * 256,
-        4 << 20,
-        in_specs=[pl.BlockSpec(memory_space=pltpu.SMEM)] + [whole] * 7,
+        2 << 20,
+        in_specs=[pl.BlockSpec(memory_space=pltpu.SMEM)] + [whole] * (5 + len(held)),
         limit=None if tile_count <= 8 else 40 << 20,
-    )(place, own_gram, low_gram, all_sums, own_middle, low_middle, start, shared_all)
+    )(place, parts, rounded, all_sums, own_middle, low_middle, *held)
     answers = lax.all_to_all(reply, "tile", 0, 0, tiled=True)
     traces = vmem_call(
         trace_body,

time: 61.9 us -> 47.2 us (0.76)
  blocking collectives: 31.1 us -> 22.9 us
  Pallas kernels: 12.8 us -> 6.85 us
  starting transfers between devices: 9.87 us -> 7.33 us
  local copies, waits for them, and re-layouts: 1.37 us -> 2.63 us
    all_gather x1 -> x0, blocking collectives: 17.3 us -> none  [on_device(): shared_all = lax.all_gather(shared, 'tile', axis=0)]
    all_to_all x0 -> x1, blocking collectives: none -> 10.8 us  [on_device(): all_sums = lax.all_to_all(sums, ('plane', 'tile'), 0, 0, tiled=True)]
    all_to_all x1 -> x0, starting transfers between devices: 7.3 us -> none  [on_device(): all_sums = lax.all_to_all(sums, ('plane', 'tile'), 0, 0, tiled=True)]
    all_to_all x1 -> x0, waiting for transfers between devices: 5.77 us -> none  [on_device(): all_sums = lax.all_to_all(sums, ('plane', 'tile'), 0, 0, tiled=True)]
    ppermute x0 -> x3, starting transfers between devices: none -> 4.76 us  [on_device(): held.append(lax.ppermute(everything, 'tile', route))]
    ppermute x0 -> x3, waiting for transfers between devices: none -> 3.52 us  [on_device(): held.append(lax.ppermute(everything, 'tile', route))]
    ppermute x2, waiting for transfers between devices: 0.01 us -> 2.85 us  [from_behind(): return lax.ppermute(block, axis, route)]
    pallas_call x1, Pallas kernels: 2.25 us -> 0.41 us  [on_device(): vmem_call(lambda *refs: gram_body(pixel_total, *refs), [shape((patches, f...]
  transfers between devices with their start and end apart: 3 -> 5, of which waited for: 1 -> 3; matrix products, arithmetic and copies ran while one was open for 0% -> 0% of each run, Pallas kernels for 4% -> 10%
where the time goes in v2:
time: 47.2 us; the launch traced here: 46.9 us
  blocking collectives  22.9 us (49%)
  starting transfers between devices  7.33 us (16%)
  Pallas kernels  6.85 us (15%)
  waiting for transfers between devices  6.37 us (13%)
  local copies, waits for them, and re-layouts  2.63 us (6%)
  between operations  0.72 us (2%)
    all_to_all x1, blocking collectives, on_device(): answers = lax.all_to_all(reply, 'tile', 0, 0, tiled=True)  12.1 us
    all_to_all x1, blocking collectives, on_device(): all_sums = lax.all_to_all(sums, ('plane', 'tile'), 0, 0, tiled=True)  10.8 us
    ppermute x3, starting transfers between devices, on_device(): held.append(lax.ppermute(everything, 'tile', route))  4.76 us
    pallas_call x1, Pallas kernels, on_device(): vmem_call(patch_body, [shape((patches, rank, frames), f32), shape((3 * ra...  4.44 us
    ppermute x3, waiting for transfers between devices, on_device(): held.append(lax.ppermute(everything, 'tile', route))  3.52 us
    ppermute x2, waiting for transfers between devices, from_behind(): return lax.ppermute(block, axis, route)  2.85 us
    unnamed x10, local copies, waits for them, and re-layouts  2.63 us
    ppermute x2, starting transfers between devices, from_behind(): return lax.ppermute(block, axis, route)  2.57 us
  transfers between devices with their start and end apart: 5, of which 3 were waited for; matrix products, arithmetic and copies ran while one was open for 0% of the time, Pallas kernels for 10%

profile of v2, /device:TPU:0, one launch (start us, length us, event | category | flops | bytes accessed | tf_op | source)
XLA Modules:
  0.0 46.9 jit_solution(14745581075438271900)
XLA Ops:
  0.6 0.0 copy-start.2
  0.6 0.0 copy-start.3
  0.7 0.6 %copy-done.2 = s32[1,128,1]{1,2,0:T(1,128)S(1)} copy-done((s32[1,128,1]{1,2,0:T(1,128)S(1)}, s32[1,128,1]{1,2,0:T(1,128)}, u32[]{:S(2)}) %copy-start.2) | copy-done | bytes 536
  1.3 0.0 copy-done.3
  1.3 0.0 copy-start
  1.3 1.1 %copy-done = bf16[1,1,3,4,256,128]{5,4,3,2,1,0:T(8,128)(2,1)S(1)} copy-done((bf16[1,1,3,4,256,128]{5,4,3,2,1,0:T(8,128)(2,1)S(1)}, bf16[1,1,3,4,256,128]{5,4,3,2,1,0:T(8,128)(2,1)}, u32[]{:S(2)}) %copy-start) | copy-done | bytes 786456
  2.4 0.0 copy-start.1
  2.4 0.8 %copy-done.1 = bf16[1,128,256]{2,1,0:T(8,128)(2,1)S(1)} copy-done((bf16[1,128,256]{2,1,0:T(8,128)(2,1)S(1)}, bf16[1,128,256]{2,1,0:T(8,128)(2,1)}, u32[]{:S(2)}) %copy-start.1) | copy-done | bytes 65560
  3.3 0.2 frame_sums.1
  3.5 4.1 %collective-permute-start = (bf16[1,144,256]{2,1,0:T(8,128)(2,1)S(1)}, bf16[1,144,256]{2,1,0:T(8,128)(2,1)S(1)}, u32[]{:S(2)}, u32[]{:S(2)}) collective-permute-start(bf16[1,144,256]{2,1,0:T(8,128)(2,1)S(1)} %bitcast.14), channel_id=1, source_target_pairs={{0,4},{1,5},{2,6},{3,7},{4,0},{5,1},{6,2},{7,3},{8,12},{9,13},{10,... | collective-permute-start | bytes 221192 | tf_op jit(solution)/shard_map/ppermute | solution.py:250
  7.6 10.8 %all_to_all.16 = f32[32,1,128]{2,1,0:T(1,128)S(1)} all-to-all(f32[32,1,128]{2,1,0:T(1,128)S(1)} %bitcast.21), channel_id=1, replica_groups=mesh['plane'=4,'tile'=8] {'plane','tile'}, dimensions={0} | all-to-all | bytes 32768 | tf_op jit(solution)/shard_map/all_to_all | solution.py:233
  18.3 0.4 own_grams.1
  18.8 0.0 collective-permute-done.refs_7_
  18.8 0.6 %collective-permute-start.3 = (bf16[2,144,256]{2,1,0:T(8,128)(2,1)S(1)}, bf16[2,144,256]{2,1,0:T(8,128)(2,1)S(1)}, u32[]{:S(2)}, u32[]{:S(2)}) collective-permute-start(bf16[2,144,256]{2,1,0:T(8,128)(2,1)S(1)} %pad_maximum_fusion.1), channel_id=1, source_target_pairs={{0,2},{1,3},{2,0},{3,1},{4,6},{5,7},{6,4},{7,5},{8,10},{9,11},{10,... | collective-permute-start | bytes 442376 | tf_op jit(solution)/shard_map/ppermute | solution.py:250
  19.4 1.3 %collective-permute-start.1 = (f32[2,128,128]{2,1,0:T(8,128)S(1)}, f32[2,128,128]{2,1,0:T(8,128)S(1)}, u32[]{:S(2)}, u32[]{:S(2)}) collective-permute-start(f32[2,128,128]{2,1,0:T(8,128)S(1)} %get-tuple-element.15.own_gram_ref), channel_id=1, source_target_pairs={{2,0},{3,1},{4,2},{5,3},{6,4},{7,5},{10,8},{11,9},{12,10},{13,11},... | collective-permute-start | bytes 393224 | tf_op jit(solution)/shard_map/ppermute | solution.py:16
  20.7 1.3 %collective-permute-start.2 = (bf16[1024,128]{1,0:T(8,128)(2,1)S(1)}, bf16[1024,128]{1,0:T(8,128)(2,1)S(1)}, u32[]{:S(2)}, u32[]{:S(2)}) collective-permute-start(bf16[1024,128]{1,0:T(8,128)(2,1)S(1)} %get-tuple-element.20), channel_id=1, source_target_pairs={{2,0},{3,1},{4,2},{5,3},{6,4},{7,5},{10,8},{11,9},{12,10},{13,11},... | collective-permute-start | bytes 786440 | tf_op jit(solution)/shard_map/ppermute | solution.py:16
  22.0 0.0 copy-start.4
  22.0 3.5 %collective-permute-done.3.refs_8_ = bf16[2,144,256]{2,1,0:T(8,128)(2,1)S(1)} collective-permute-done((bf16[2,144,256]{2,1,0:T(8,128)(2,1)S(1)}, bf16[2,144,256]{2,1,0:T(8,128)(2,1)S(1)}, u32[]{:S(2)}, u32[]{:S(2)}) %collective-permute-start.3) | collective-permute-done | bytes 147488 | tf_op jit(solution)/shard_map/ppermute | solution.py:250
  25.6 0.1 collective-permute-start.4
  25.6 2.7 %collective-permute-done.1.low_gram_ref = f32[2,128,128]{2,1,0:T(8,128)S(1)} collective-permute-done((f32[2,128,128]{2,1,0:T(8,128)S(1)}, f32[2,128,128]{2,1,0:T(8,128)S(1)}, u32[]{:S(2)}, u32[]{:S(2)}) %collective-permute-start.1) | collective-permute-done | bytes 131104 | tf_op jit(solution)/shard_map/ppermute | solution.py:16
  28.3 0.0 copy-done.4
  28.3 4.4 %patch_factors.1 = (f32[2,32,128]{2,1,0:T(8,128)}, bf16[192,128]{1,0:T(8,128)(2,1)S(1)}, bf16[64,128]{1,0:T(8,128)(2,1)S(1)}) custom-call(f32[2,128,128]{2,1,0:T(8,128)S(1)} %get-tuple-element.15.own_gram_ref, f32[2,128,128]{2,1,0:T(8,128)S(1)} %collective-permute-done.1.low_gram_ref, f32[2,32,128]{2,1,0:T(8,128)S(1)} %bitcast.23), custom_call_target="tpu_custom_call" | custom-call | flops 6000000000 | bytes 1048576 | tf_op jit(solution)/shard_map/patch_factors/pallas_call | solution.py:254
  32.8 0.2 collective-permute-done.2.refs_5_
  32.9 0.0 collective-permute-done.4.refs_9_
  32.9 0.9 %coefficients.1 = bf16[8,128,128]{2,1,0:T(8,128)(2,1)S(1)} custom-call(s32[1]{0:T(128)} %bitcast.9.refs_0_, bf16[192,128]{1,0:T(8,128)(2,1)S(1)} %get-tuple-element.17.refs_1_, bf16[64,128]{1,0:T(8,128)(2,1)S(1)} %get-tuple-element.18.refs_2_, f32[32,128]{1,0:T(8,128)S(1)} %bitcast.19, bf16[1024,128]{1,0:T(8,128)(2,1)S(1)} %get-tuple-element.19.refs_4_, ...), custom_call_target="tpu_custom_call" | custom-call | flops 268435456 | bytes 2097152 | tf_op jit(solution)/shard_map/coefficients/pallas_call | solution.py:261
  33.9 12.1 %all_to_all.17.reply_ref = bf16[8,128,128]{2,1,0:T(8,128)(2,1)S(1)} all-to-all(bf16[8,128,128]{2,1,0:T(8,128)(2,1)S(1)} %coefficients.1), channel_id=1, replica_groups=mesh['plane'=4,'tile'=8] {'tile'}, dimensions={0} | all-to-all | bytes 524288 | tf_op jit(solution)/shard_map/all_to_all | solution.py:270
  46.0 0.9 %source_traces.1 = f32[128,128]{1,0:T(8,128)} custom-call(bf16[8,128,128]{2,1,0:T(8,128)(2,1)S(1)} %all_to_all.17.reply_ref), custom_call_target="tpu_custom_call" | custom-call | flops 16777216 | bytes 262144 | tf_op jit(solution)/shard_map/source_traces/pallas_call | solution.py:271
  (2 shorter events, 0.0 us)
Async XLA Ops:
  0.6 0.7 %copy-start.2 = (s32[1,128,1]{1,2,0:T(1,128)S(1)}, s32[1,128,1]{1,2,0:T(1,128)}, u32[]{:S(2)}) copy-start(s32[1,128,1]{1,2,0:T(1,128)} %param.8) | copy-start | bytes 1540
  0.6 0.7 %copy-start.3 = (s32[1,128]{1,0:T(1,128)S(1)}, s32[1,128]{1,0:T(1,128)}, u32[]{:S(2)}) copy-start(s32[1,128]{1,0:T(1,128)} %block_ref.1) | copy-start | bytes 1540
  1.3 1.1 %copy-start = (bf16[1,1,3,4,256,128]{5,4,3,2,1,0:T(8,128)(2,1)S(1)}, bf16[1,1,3,4,256,128]{5,4,3,2,1,0:T(8,128)(2,1)}, u32[]{:S(2)}) copy-start(bf16[1,1,3,4,256,128]{5,4,3,2,1,0:T(8,128)(2,1)} %param.5) | copy-start | bytes 2359300
  2.4 0.8 %copy-start.1 = (bf16[1,128,256]{2,1,0:T(8,128)(2,1)S(1)}, bf16[1,128,256]{2,1,0:T(8,128)(2,1)}, u32[]{:S(2)}) copy-start(bf16[1,128,256]{2,1,0:T(8,128)(2,1)} %param.7) | copy-start | bytes 196612
  3.5 15.3 %collective-permute-start = (bf16[1,144,256]{2,1,0:T(8,128)(2,1)S(1)}, bf16[1,144,256]{2,1,0:T(8,128)(2,1)S(1)}, u32[]{:S(2)}, u32[]{:S(2)}) collective-permute-start(bf16[1,144,256]{2,1,0:T(8,128)(2,1)S(1)} %bitcast.14), channel_id=1, source_target_pairs={{0,4},{1,5},{2,6},{3,7},{4,0},{5,1},{6,2},{7,3},{8,12},{9,13},{10,... | collective-permute-start | bytes 221192 | tf_op jit(solution)/shard_map/ppermute | solution.py:250
  18.8 6.7 %collective-permute-start.3 = (bf16[2,144,256]{2,1,0:T(8,128)(2,1)S(1)}, bf16[2,144,256]{2,1,0:T(8,128)(2,1)S(1)}, u32[]{:S(2)}, u32[]{:S(2)}) collective-permute-start(bf16[2,144,256]{2,1,0:T(8,128)(2,1)S(1)} %pad_maximum_fusion.1), channel_id=1, source_target_pairs={{0,2},{1,3},{2,0},{3,1},{4,6},{5,7},{6,4},{7,5},{8,10},{9,11},{10,... | collective-permute-start | bytes 442376 | tf_op jit(solution)/shard_map/ppermute | solution.py:250
  19.4 8.9 %collective-permute-start.1 = (f32[2,128,128]{2,1,0:T(8,128)S(1)}, f32[2,128,128]{2,1,0:T(8,128)S(1)}, u32[]{:S(2)}, u32[]{:S(2)}) collective-permute-start(f32[2,128,128]{2,1,0:T(8,128)S(1)} %get-tuple-element.15.own_gram_ref), channel_id=1, source_target_pairs={{2,0},{3,1},{4,2},{5,3},{6,4},{7,5},{10,8},{11,9},{12,10},{13,11},... | collective-permute-start | bytes 393224 | tf_op jit(solution)/shard_map/ppermute | solution.py:16
  20.7 12.2 %collective-permute-start.2 = (bf16[1024,128]{1,0:T(8,128)(2,1)S(1)}, bf16[1024,128]{1,0:T(8,128)(2,1)S(1)}, u32[]{:S(2)}, u32[]{:S(2)}) collective-permute-start(bf16[1024,128]{1,0:T(8,128)(2,1)S(1)} %get-tuple-element.20), channel_id=1, source_target_pairs={{2,0},{3,1},{4,2},{5,3},{6,4},{7,5},{10,8},{11,9},{12,10},{13,11},... | collective-permute-start | bytes 786440 | tf_op jit(solution)/shard_map/ppermute | solution.py:16
  22.0 6.3 %copy-start.4 = (f32[1,2,32,128]{3,2,1,0:T(8,128)S(1)}, f32[1,2,32,128]{3,2,1,0:T(8,128)}, u32[]{:S(2)}) copy-start(f32[1,2,32,128]{3,2,1,0:T(8,128)} %param.6) | copy-start | bytes 98308
  25.6 7.4 %collective-permute-start.4 = (bf16[4,144,256]{2,1,0:T(8,128)(2,1)S(1)}, bf16[4,144,256]{2,1,0:T(8,128)(2,1)S(1)}, u32[]{:S(2)}, u32[]{:S(2)}) collective-permute-start(bf16[4,144,256]{2,1,0:T(8,128)(2,1)S(1)} %pad_maximum_fusion), channel_id=1, source_target_pairs={{0,1},{1,0},{2,3},{3,2},{4,5},{5,4},{6,7},{7,6},{8,9},{9,8},{10,11... | collective-permute-start | bytes 884744 | tf_op jit(solution)/shard_map/ppermute | solution.py:250

commit v3 on v2

--- a/solution.py
+++ b/solution.py
@@ -6,7 +6,6 @@
 from jax.sharding import PartitionSpec as P
 
 ITERS = 3
-CODE_ROWS = 16
 EXACT = lax.Precision.HIGHEST
 
 
@@ -39,21 +38,20 @@
     return lax.dot_general(left, right, (((0,), (0,)), ((), ())), preferred_element_type=jnp.float32)
 
 
-def sum_body(strip_ref, row_ref, block_ref, footprint_ref, sums_ref, middle_ref, shared_ref):
+def sum_body(strip_ref, sums_ref, middle_ref):
     rows = strip_ref.shape[0]
     ones = jnp.ones((8, rows), jnp.bfloat16)
-    total = jnp.dot(ones, strip_ref[...], preferred_element_type=jnp.float32)
-    sums_ref[...] = jnp.broadcast_to(total[0:1], sums_ref.shape)
+    sums_ref[...] = jnp.dot(ones, strip_ref[...], preferred_element_type=jnp.float32)
     cell = middle_ref.shape[0]
     middle_ref[...] = strip_ref[cell : 2 * cell, :]
-    sources = footprint_ref.shape[0]
-    shared_ref[0:sources, :] = footprint_ref[...]
-    codes = jnp.concatenate([row_ref[...], block_ref[...]], 1).astype(jnp.float32)
-    shared_ref[sources:, :] = jnp.broadcast_to(codes, (CODE_ROWS, codes.shape[1])).astype(jnp.bfloat16)
-
-
-def gram_body(pixel_total, sums_ref, strip_ref, gram_ref, middle_ref):
-    background = jnp.sum(sums_ref[...], axis=0, keepdims=True) / pixel_total
+
+
+def background_of(notes_ref, frames, pixel_total):
+    return jnp.sum(notes_ref[:, 0:frames], axis=0, keepdims=True) / pixel_total
+
+
+def gram_body(pixel_total, notes_ref, strip_ref, gram_ref, middle_ref):
+    background = background_of(notes_ref, strip_ref.shape[1], pixel_total)
     cell = middle_ref.shape[0]
     cells = strip_ref.shape[0] // cell
     grams = []
@@ -143,12 +141,15 @@
     parts_ref[...] = jnp.concatenate(three_parts(whitened), 0)
 
 
-def reply_body(pixel_total, place_ref, parts_ref, rounded_ref, sums_ref, own_ref, low_ref, *refs):
-    shared_refs, reply_ref = refs[:-1], refs[-1]
+def reply_body(pixel_total, place_ref, parts_ref, rounded_ref, notes_ref, own_ref, low_ref, *refs):
+    tile_count, paired = refs[0], refs[1]
+    refs = refs[2:]
+    held_count = tile_count.bit_length()
+    held_refs, reply_refs = refs[:held_count], refs[held_count:]
     parts = parts_ref[...]
     temporal_rounded = rounded_ref[...]
-    ranks = temporal_rounded.shape[0]
-    background = jnp.sum(sums_ref[...], axis=0, keepdims=True) / pixel_total
+    ranks, frames = temporal_rounded.shape
+    background = background_of(notes_ref, frames, pixel_total)
     lower = (low_ref[...].astype(jnp.float32) - background).astype(jnp.bfloat16)
     pixels = 256
     bands = []
@@ -158,35 +159,53 @@
         bands += [spatial[:, q * pixels : (q + 1) * pixels] for q in range(4)]
     stacked = jnp.concatenate(bands, 0)
     place = place_ref[0]
-    owners, sources = reply_ref.shape[0], reply_ref.shape[2]
-
-    bits = owners.bit_length() - 1
-
-    def one_owner(shared_ref, entry, order):
-        offset = sum(((order >> t) & 1) << (bits - 1 - t) for t in range(bits))
-        owner = lax.bitwise_xor(place, jnp.int32(offset))
-        projected = rows_dot(stacked, shared_ref[entry, 0:sources, :])
-        codes = shared_ref[entry, sources : sources + 1, :].astype(jnp.float32)
-        code_row = codes[:, 0:sources].astype(jnp.int32)
-        code_quarter = codes[:, sources : 2 * sources].astype(jnp.int32)
+    plane_start = place_ref[1] * tile_count
+    sources = held_refs[0].shape[1]
+    bits = tile_count.bit_length() - 1
+
+    def turned(order):
+        return sum(((order >> t) & 1) << (bits - 1 - t) for t in range(bits))
+
+    def coefficients(held_ref, entry, owner):
+        projected = rows_dot(stacked, held_ref[entry])
+        codes = notes_ref[pl.ds(plane_start + owner, 1), :][:, frames : frames + sources].astype(jnp.int32)
         total = jnp.zeros((ranks, sources), jnp.float32)
         for role in range(2):
             for quarter in range(4):
                 start = (role * 4 + quarter) * ranks
-                chosen = (code_row == place - 2 * role) & (code_quarter == quarter)
+                chosen = codes == 4 * (place - 2 * role) + quarter
                 total = total + jnp.where(chosen, projected[start : start + ranks], 0.0)
-        reply_ref[owner, 0:ranks, :] = total.astype(jnp.bfloat16)
-        reply_ref[owner, ranks:, :] = temporal_rounded
-
-    offset = 0
-    for shared_ref in shared_refs:
-        count = shared_ref.shape[0]
-        if owners <= 8:
+        return total.astype(jnp.bfloat16)
+
+    first = 0
+    for held_ref in held_refs:
+        count = held_ref.shape[0]
+        if paired:
             for entry in range(count):
-                one_owner(shared_ref, entry, offset + entry)
+                offset = turned(first + entry)
+                owner = lax.bitwise_xor(place, jnp.int32(offset))
+                row = (offset % 2) * ranks
+                reply_refs[offset // 2][row : row + ranks, :] = coefficients(held_ref, entry, owner)
         else:
-            pl.loop(0, count)(lambda entry, ref=shared_ref, first=offset: one_owner(ref, entry, first + entry))
-        offset += count
+
+            def one_owner(entry, held_ref=held_ref, first=first):
+                owner = lax.bitwise_xor(place, turned(first + entry))
+                reply_refs[0][owner, 0:ranks, :] = coefficients(held_ref, entry, owner)
+                reply_refs[0][owner, ranks:, :] = temporal_rounded
+
+            pl.loop(0, count)(one_owner)
+        first += count
+    if paired:
+        for reply_ref in reply_refs:
+            reply_ref[2 * ranks :, :] = temporal_rounded
+
+
+def paired_trace_body(*refs):
+    own_refs, mate_ref, traces_ref = refs[:-2], refs[-2], refs[-1]
+    ranks = own_refs[0].shape[0] // 3
+    coefficient = [r[0:ranks] for r in own_refs] + [mate_ref[i, 0:ranks] for i in range(len(own_refs))]
+    temporal = [r[2 * ranks :] for r in own_refs] + [mate_ref[i, ranks:] for i in range(len(own_refs))]
+    traces_ref[...] = 0.25 * columns_dot(jnp.concatenate(coefficient, 0), jnp.concatenate(temporal, 0))
 
 
 def trace_body(reply_ref, traces_ref):
@@ -223,14 +242,16 @@
     def shape(dims, kind):
         return jax.ShapeDtypeStruct(dims, kind)
 
-    sums, middle, shared = vmem_call(
+    sums, middle = vmem_call(
         sum_body,
-        [shape((devices, frames), f32), shape((cell, frames), bf16), shape((sources + CODE_ROWS, pixels), bf16)],
+        [shape((8, frames), f32), shape((cell, frames), bf16)],
         "frame_sums",
         2 * cells * cell * frames,
         2 * cells * cell * frames,
-    )(strip, source_row.reshape(1, sources), footprint_block.reshape(1, sources), footprints[0])
-    all_sums = lax.all_to_all(sums, ("plane", "tile"), 0, 0, tiled=True)
+    )(strip)
+    codes = (source_row.reshape(1, sources) * 4 + footprint_block.reshape(1, sources)).astype(f32)
+    notes = jnp.broadcast_to(jnp.concatenate([sums[0:1], codes], 1), (devices, frames + sources))
+    notes = lax.all_to_all(notes, ("plane", "tile"), 0, 0, tiled=True)
     low_middle = from_behind(middle, "tile", -2)
     own_gram, own_middle = vmem_call(
         lambda *refs: gram_body(pixel_total, *refs),
@@ -238,17 +259,14 @@
         "own_grams",
         2 * cells * cell * frames * frames,
         2 * cells * cell * frames,
-    )(all_sums, strip)
-    low_gram = from_behind(own_gram, "tile", -2)
-    held = [shared[None]]
-    bits = tile_count.bit_length() - 1
-    for bit in reversed(range(bits)):
+    )(notes, strip)
+    held = [footprints]
+    for bit in reversed(range(tile_count.bit_length() - 1)):
         route = [(i, i ^ (1 << bit)) for i in range(tile_count)]
         everything = held[0] if len(held) == 1 else jnp.concatenate(held, 0)
-        if len(held) == 2:
-            everything, own_gram = lax.optimization_barrier((everything, own_gram))
         held.append(lax.ppermute(everything, "tile", route))
-    place = lax.axis_index("tile").astype(jnp.int32).reshape(1)
+    low_gram = from_behind(own_gram, "tile", -2)
+    place = jnp.stack([lax.axis_index("tile"), lax.axis_index("plane")]).astype(jnp.int32)
     whole = pl.BlockSpec(memory_space=pltpu.VMEM)
     ranks = patches * rank
     temporal, parts, rounded = vmem_call(
@@ -258,23 +276,31 @@
         6 * 10**9,
         1 << 20,
     )(own_gram, low_gram, start)
-    (reply,) = vmem_call(
-        lambda *refs: reply_body(pixel_total, *refs),
-        [shape((tile_count, 2 * ranks, sources), bf16)],
+    chips = tile_count // 2
+    paired = chips <= 4
+    replies = vmem_call(
+        lambda *refs: reply_body(pixel_total, *refs[:6], tile_count, paired, *refs[6:]),
+        [shape((3 * ranks, sources), bf16)] * chips if paired else [shape((tile_count, 2 * ranks, sources), bf16)],
         "coefficients",
         2 * 1024 * 512 * 256,
         2 << 20,
         in_specs=[pl.BlockSpec(memory_space=pltpu.SMEM)] + [whole] * (5 + len(held)),
-        limit=None if tile_count <= 8 else 40 << 20,
-    )(place, parts, rounded, all_sums, own_middle, low_middle, *held)
-    answers = lax.all_to_all(reply, "tile", 0, 0, tiled=True)
-    traces = vmem_call(
-        trace_body,
-        shape((sources, frames), f32),
-        "source_traces",
-        2 * sources * frames * patches * rank * tile_count,
-        2 * answers.size,
-    )(answers)
+        limit=None if paired else 40 << 20,
+    )(place, parts, rounded, notes, own_middle, low_middle, *held)
+    flops = 2 * sources * frames * ranks * tile_count
+    if paired:
+        arrived = [replies[0]]
+        for offset in range(1, chips):
+            route = [(i, i ^ (2 * offset)) for i in range(tile_count)]
+            arrived.append(lax.ppermute(replies[offset], "tile", route))
+        handed = jnp.stack([block[ranks:] for block in arrived])
+        mate = lax.ppermute(handed, "tile", [(i, i ^ 1) for i in range(tile_count)])
+        traces = vmem_call(
+            paired_trace_body, shape((sources, frames), f32), "source_traces", flops, 1 << 19
+        )(*arrived, mate)
+    else:
+        answers = lax.all_to_all(replies[0], "tile", 0, 0, tiled=True)
+        traces = vmem_call(trace_body, shape((sources, frames), f32), "source_traces", flops, 2 * answers.size)(answers)
     return (temporal[None], traces[None])
 
 

time: 47.2 us -> 42.7 us (0.905)
  blocking collectives: 22.9 us -> 0 us
  starting transfers between devices: 7.33 us -> 17 us
  waiting for transfers between devices: 6.37 us -> 14.9 us
  Pallas kernels: 6.85 us -> 7.4 us
    all_to_all x2 -> x0, blocking collectives: 22.9 us -> none  [the longest x1 12.1 us: on_device(): answers = lax.all_to_all(reply, 'tile', 0, 0, tiled=True)]
    ppermute x0 -> x4, waiting for transfers between devices: none -> 4.92 us  [the longest x3 3.59 us: on_device(): arrived.append(lax.ppermute(replies[offset], 'tile', route))]
    ppermute x0 -> x4, starting transfers between devices: none -> 4.52 us  [the longest x3 4.45 us: on_device(): arrived.append(lax.ppermute(replies[offset], 'tile', route))]
    all_to_all x0 -> x1, waiting for transfers between devices: none -> 4.14 us  [on_device(): notes = lax.all_to_all(notes, ('plane', 'tile'), 0, 0, tiled=True)]
    all_to_all x0 -> x1, starting transfers between devices: none -> 3.82 us  [on_device(): notes = lax.all_to_all(notes, ('plane', 'tile'), 0, 0, tiled=True)]
    ppermute x3, waiting for transfers between devices: 3.52 us -> 0.01 us  [on_device(): held.append(lax.ppermute(everything, 'tile', route))]
    ppermute x2, waiting for transfers between devices: 2.85 us -> 5.82 us  [from_behind(): return lax.ppermute(block, axis, route)]
    ppermute x3, starting transfers between devices: 4.76 us -> 6.11 us  [on_device(): held.append(lax.ppermute(everything, 'tile', route))]
  transfers between devices with their start and end apart: 5 -> 10, of which waited for: 3 -> 6; matrix products, arithmetic and copies ran while one was open for 0% -> 2% of each run, Pallas kernels for 10% -> 12%
where the time goes in v3:
time: 42.7 us; the launch traced here: 42.5 us
  starting transfers between devices  17 us (40%)
  waiting for transfers between devices  14.9 us (35%)
  Pallas kernels  7.4 us (17%)
  local copies, waits for them, and re-layouts  2.25 us (5%)
  between operations  0.73 us (2%)
    ppermute x3, starting transfers between devices, on_device(): held.append(lax.ppermute(everything, 'tile', route))  6.11 us
    ppermute x2, waiting for transfers between devices, from_behind(): return lax.ppermute(block, axis, route)  5.82 us
    ppermute x3, starting transfers between devices, on_device(): arrived.append(lax.ppermute(replies[offset], 'tile', route))  4.45 us
    pallas_call x1, Pallas kernels, on_device(): vmem_call(patch_body, [shape((patches, rank, frames), f32), shape((3 * ra...  4.44 us
    all_to_all x1, waiting for transfers between devices, on_device(): notes = lax.all_to_all(notes, ('plane', 'tile'), 0, 0, tiled=True)  4.14 us
    all_to_all x1, starting transfers between devices, on_device(): notes = lax.all_to_all(notes, ('plane', 'tile'), 0, 0, tiled=True)  3.82 us
    ppermute x3, waiting for transfers between devices, on_device(): arrived.append(lax.ppermute(replies[offset], 'tile', route))  3.59 us
    ppermute x2, starting transfers between devices, from_behind(): return lax.ppermute(block, axis, route)  2.57 us
  transfers between devices with their start and end apart: 10, of which 6 were waited for; matrix products, arithmetic and copies ran while one was open for 2% of the time, Pallas kernels for 12%

profile of v3, /device:TPU:0, one launch (start us, length us, event | category | flops | bytes accessed | tf_op | source)
XLA Modules:
  0.0 42.5 jit_solution(15214991272710620843)
XLA Ops:
  0.6 4.1 %collective-permute-start.2 = (bf16[1,128,256]{2,1,0:T(8,128)(2,1)}, bf16[1,128,256]{2,1,0:T(8,128)(2,1)S(1)}, u32[]{:S(2)}, u32[]{:S(2)}) collective-permute-start(bf16[1,128,256]{2,1,0:T(8,128)(2,1)} %refs_6_.1), channel_id=1, source_target_pairs={{0,4},{1,5},{2,6},{3,7},{4,0},{5,1},{6,2},{7,3},{8,12},{9,13},{10,... | collective-permute-start | bytes 196616 | tf_op jit(solution)/shard_map/ppermute | solution.py:267
  4.7 0.0 copy-start
  4.7 1.1 %copy-done = bf16[1,1,3,4,256,128]{5,4,3,2,1,0:T(8,128)(2,1)S(1)} copy-done((bf16[1,1,3,4,256,128]{5,4,3,2,1,0:T(8,128)(2,1)S(1)}, bf16[1,1,3,4,256,128]{5,4,3,2,1,0:T(8,128)(2,1)}, u32[]{:S(2)}) %copy-start) | copy-done | bytes 786456
  5.9 0.0 copy-start.4
  5.9 0.0 copy-start.5
  5.9 0.0 copy-start.1
  5.9 0.2 frame_sums.1
  6.1 0.0 copy-start.2
  6.1 0.4 %copy-done.4 = s32[1,128]{1,0:T(1,128)S(1)} copy-done((s32[1,128]{1,0:T(1,128)S(1)}, s32[1,128]{1,0:T(1,128)}, u32[]{:S(2)}) %copy-start.4) | copy-done | bytes 536
  6.5 0.0 copy-done.5
  6.5 0.6 %broadcast_in_dim.11 = f32[32,1,256]{2,1,0:T(1,128)} broadcast(f32[256]{0:T(256)S(1)} %bitcast.28), dimensions={2} | broadcast | bytes 33792 | tf_op jit(solution)/shard_map/broadcast_in_dim | solution.py:253
  7.2 3.8 %all-to-all-start = ((f32[32,1,256]{2,1,0:T(1,128)}), f32[32,1,256]{2,1,0:T(1,128)S(1)}, u32[]{:S(2)}, u32[]{:S(2)}) async-start(f32[32,1,256]{2,1,0:T(1,128)} %broadcast_in_dim.11), calls=%async_computation | async-start | bytes 65536 | tf_op jit(solution)/shard_map/all_to_all | solution.py:254
  11.0 0.0 collective-permute-done.2.refs_7_
  11.0 0.0 copy-done.2
  11.1 1.8 %collective-permute-start.3 = (bf16[2,128,256]{2,1,0:T(8,128)(2,1)S(1)}, bf16[2,128,256]{2,1,0:T(8,128)(2,1)S(1)}, u32[]{:S(2)}, u32[]{:S(2)}) collective-permute-start(bf16[2,128,256]{2,1,0:T(8,128)(2,1)S(1)} %pad_maximum_fusion.1), channel_id=1, source_target_pairs={{0,2},{1,3},{2,0},{3,1},{4,6},{5,7},{6,4},{7,5},{8,10},{9,11},{10,... | collective-permute-start | bytes 393224 | tf_op jit(solution)/shard_map/ppermute | solution.py:267
  12.9 1.3 %collective-permute-start.1 = (bf16[1024,128]{1,0:T(8,128)(2,1)S(1)}, bf16[1024,128]{1,0:T(8,128)(2,1)S(1)}, u32[]{:S(2)}, u32[]{:S(2)}) collective-permute-start(bf16[1024,128]{1,0:T(8,128)(2,1)S(1)} %get-tuple-element.19), channel_id=1, source_target_pairs={{2,0},{3,1},{4,2},{5,3},{6,4},{7,5},{10,8},{11,9},{12,10},{13,11},... | collective-permute-start | bytes 786440 | tf_op jit(solution)/shard_map/ppermute | solution.py:15
  14.2 4.1 %all-to-all-done = f32[32,1,256]{2,1,0:T(1,128)S(1)} async-done(((f32[32,1,256]{2,1,0:T(1,128)}), f32[32,1,256]{2,1,0:T(1,128)S(1)}, u32[]{:S(2)}, u32[]{:S(2)}) %all-to-all-start) | async-done | bytes 32800 | tf_op jit(solution)/shard_map/all_to_all | solution.py:254
  18.3 0.0 copy-done.1
  18.3 0.4 own_grams.1
  18.8 1.3 %collective-permute-start = (f32[2,128,128]{2,1,0:T(8,128)S(1)}, f32[2,128,128]{2,1,0:T(8,128)S(1)}, u32[]{:S(2)}, u32[]{:S(2)}) collective-permute-start(f32[2,128,128]{2,1,0:T(8,128)S(1)} %get-tuple-element.14.own_gram_ref), channel_id=1, source_target_pairs={{2,0},{3,1},{4,2},{5,3},{6,4},{7,5},{10,8},{11,9},{12,10},{13,11},... | collective-permute-start | bytes 393224 | tf_op jit(solution)/shard_map/ppermute | solution.py:15
  20.1 0.1 pad_add_fusion.refs_0_
  20.1 0.0 copy-start.3
  20.1 0.0 collective-permute-done.3.refs_8_
  20.2 0.2 collective-permute-start.4
  20.4 5.8 %collective-permute-done.low_gram_ref = f32[2,128,128]{2,1,0:T(8,128)S(1)} collective-permute-done((f32[2,128,128]{2,1,0:T(8,128)S(1)}, f32[2,128,128]{2,1,0:T(8,128)S(1)}, u32[]{:S(2)}, u32[]{:S(2)}) %collective-permute-start) | collective-permute-done | bytes 131104 | tf_op jit(solution)/shard_map/ppermute | solution.py:15
  26.2 0.0 copy-done.3
  26.2 4.4 %patch_factors.1 = (f32[2,32,128]{2,1,0:T(8,128)}, bf16[192,128]{1,0:T(8,128)(2,1)S(1)}, bf16[64,128]{1,0:T(8,128)(2,1)S(1)}) custom-call(f32[2,128,128]{2,1,0:T(8,128)S(1)} %get-tuple-element.14.own_gram_ref, f32[2,128,128]{2,1,0:T(8,128)S(1)} %collective-permute-done.low_gram_ref, f32[2,32,128]{2,1,0:T(8,128)S(1)} %bitcast.26), custom_call_target="tpu_custom_call" | custom-call | flops 6000000000 | bytes 1048576 | tf_op jit(solution)/shard_map/patch_factors/pallas_call | solution.py:272
  30.6 0.0 collective-permute-done.1.refs_5_
  30.6 0.0 collective-permute-done.4.refs_9_
  30.6 1.5 %coefficients.1 = (bf16[192,128]{1,0:T(8,128)(2,1)S(1)}, bf16[192,128]{1,0:T(8,128)(2,1)S(1)}, bf16[192,128]{1,0:T(8,128)(2,1)S(1)}, bf16[192,128]{1,0:T(8,128)(2,1)S(1)}) custom-call(s32[2]{0:T(128)S(1)} %pad_add_fusion.refs_0_, bf16[192,128]{1,0:T(8,128)(2,1)S(1)} %get-tuple-element.16.refs_1_, bf16[64,128]{1,0:T(8,128)(2,1)S(1)} %get-tuple-element.17.refs_2_, ...), custom_call_target="tpu_custom_call" | custom-call | flops 268435456 | bytes 2097152 | tf_op jit(solution)/shard_map/coefficients/pallas_call | solution.py:281
  32.1 0.8 %collective-permute-start.5 = (bf16[192,128]{1,0:T(8,128)(2,1)S(1)}, bf16[192,128]{1,0:T(8,128)(2,1)S(1)}, u32[]{:S(2)}, u32[]{:S(2)}) collective-permute-start(bf16[192,128]{1,0:T(8,128)(2,1)S(1)} %get-tuple-element.21), channel_id=1, source_target_pairs={{0,2},{1,3},{2,0},{3,1},{4,6},{5,7},{6,4},{7,5},{8,10},{9,11},{10,... | collective-permute-start | bytes 147464 | tf_op jit(solution)/shard_map/ppermute | solution.py:295
  32.9 1.3 %collective-permute-start.6 = (bf16[192,128]{1,0:T(8,128)(2,1)S(1)}, bf16[192,128]{1,0:T(8,128)(2,1)S(1)}, u32[]{:S(2)}, u32[]{:S(2)}) collective-permute-start(bf16[192,128]{1,0:T(8,128)(2,1)S(1)} %get-tuple-element.22), channel_id=1, source_target_pairs={{0,4},{1,5},{2,6},{3,7},{4,0},{5,1},{6,2},{7,3},{8,12},{9,13},{10,... | collective-permute-start | bytes 147464 | tf_op jit(solution)/shard_map/ppermute | solution.py:295
  34.2 2.4 %collective-permute-start.7 = (bf16[192,128]{1,0:T(8,128)(2,1)S(1)}, bf16[192,128]{1,0:T(8,128)(2,1)S(1)}, u32[]{:S(2)}, u32[]{:S(2)}) collective-permute-start(bf16[192,128]{1,0:T(8,128)(2,1)S(1)} %get-tuple-element.23), channel_id=1, source_target_pairs={{0,6},{1,7},{2,4},{3,5},{4,2},{5,3},{6,0},{7,1},{8,14},{9,15},{10,... | collective-permute-start | bytes 147464 | tf_op jit(solution)/shard_map/ppermute | solution.py:295
  36.6 0.2 collective-permute-done.5.refs_1_
  36.7 2.2 %collective-permute-done.6.refs_2_ = bf16[192,128]{1,0:T(8,128)(2,1)S(1)} collective-permute-done((bf16[192,128]{1,0:T(8,128)(2,1)S(1)}, bf16[192,128]{1,0:T(8,128)(2,1)S(1)}, u32[]{:S(2)}, u32[]{:S(2)}) %collective-permute-start.6) | collective-permute-done | bytes 49184 | tf_op jit(solution)/shard_map/ppermute | solution.py:295
  38.9 1.2 %collective-permute-done.7.refs_3_ = bf16[192,128]{1,0:T(8,128)(2,1)S(1)} collective-permute-done((bf16[192,128]{1,0:T(8,128)(2,1)S(1)}, bf16[192,128]{1,0:T(8,128)(2,1)S(1)}, u32[]{:S(2)}, u32[]{:S(2)}) %collective-permute-start.7) | collective-permute-done | bytes 49184 | tf_op jit(solution)/shard_map/ppermute | solution.py:295
  40.2 0.1 collective-permute-start.8
  40.3 1.3 %collective-permute-done.8.refs_4_ = bf16[4,128,128]{2,1,0:T(8,128)(2,1)S(1)} collective-permute-done((bf16[4,128,128]{2,1,0:T(8,128)(2,1)S(1)}, bf16[4,128,128]{2,1,0:T(8,128)(2,1)S(1)}, u32[]{:S(2)}, u32[]{:S(2)}) %collective-permute-start.8) | collective-permute-done | bytes 131104 | tf_op jit(solution)/shard_map/ppermute | solution.py:297
  41.6 0.9 %source_traces.1 = f32[128,128]{1,0:T(8,128)} custom-call(bf16[192,128]{1,0:T(8,128)(2,1)S(1)} %get-tuple-element.20.refs_0_, bf16[192,128]{1,0:T(8,128)(2,1)S(1)} %collective-permute-done.5.refs_1_, bf16[192,128]{1,0:T(8,128)(2,1)S(1)} %collective-permute-done.6.refs_2_, bf16[192,128]{1,0:T(8,128)(2,1)S(1)} %collective-permute-done.7.refs_3_, ...), custom_call_target="tpu_custom_call" | custom-call | flops 16777216 | bytes 524288 | tf_op jit(solution)/shard_map/source_traces/pallas_call | solution.py:298
  (11 shorter events, 0.1 us)
Async XLA Ops:
  0.6 10.4 %collective-permute-start.2 = (bf16[1,128,256]{2,1,0:T(8,128)(2,1)}, bf16[1,128,256]{2,1,0:T(8,128)(2,1)S(1)}, u32[]{:S(2)}, u32[]{:S(2)}) collective-permute-start(bf16[1,128,256]{2,1,0:T(8,128)(2,1)} %refs_6_.1), channel_id=1, source_target_pairs={{0,4},{1,5},{2,6},{3,7},{4,0},{5,1},{6,2},{7,3},{8,12},{9,13},{10,... | collective-permute-start | bytes 196616 | tf_op jit(solution)/shard_map/ppermute | solution.py:267
  4.7 1.1 %copy-start = (bf16[1,1,3,4,256,128]{5,4,3,2,1,0:T(8,128)(2,1)S(1)}, bf16[1,1,3,4,256,128]{5,4,3,2,1,0:T(8,128)(2,1)}, u32[]{:S(2)}) copy-start(bf16[1,1,3,4,256,128]{5,4,3,2,1,0:T(8,128)(2,1)} %param.5) | copy-start | bytes 2359300
  5.9 0.7 %copy-start.4 = (s32[1,128]{1,0:T(1,128)S(1)}, s32[1,128]{1,0:T(1,128)}, u32[]{:S(2)}) copy-start(s32[1,128]{1,0:T(1,128)} %param.9) | copy-start | bytes 1540
  5.9 0.7 %copy-start.5 = (s32[1,128,1]{1,2,0:T(1,128)S(1)}, s32[1,128,1]{1,2,0:T(1,128)}, u32[]{:S(2)}) copy-start(s32[1,128,1]{1,2,0:T(1,128)} %param.8) | copy-start | bytes 1540
  5.9 12.5 %copy-start.1 = (bf16[1,1,3,4,256,128]{5,4,3,2,1,0:T(8,128)(2,1)S(1)}, bf16[1,1,3,4,256,128]{5,4,3,2,1,0:T(8,128)(2,1)}, u32[]{:S(2)}) copy-start(bf16[1,1,3,4,256,128]{5,4,3,2,1,0:T(8,128)(2,1)} %param.5) | copy-start | bytes 2359300
  6.1 5.0 %copy-start.2 = (bf16[1,128,256]{2,1,0:T(8,128)(2,1)S(1)}, bf16[1,128,256]{2,1,0:T(8,128)(2,1)}, u32[]{:S(2)}) copy-start(bf16[1,128,256]{2,1,0:T(8,128)(2,1)} %refs_6_.1) | copy-start | bytes 196612
  7.2 11.1 %all-to-all-start = ((f32[32,1,256]{2,1,0:T(1,128)}), f32[32,1,256]{2,1,0:T(1,128)S(1)}, u32[]{:S(2)}, u32[]{:S(2)}) async-start(f32[32,1,256]{2,1,0:T(1,128)} %broadcast_in_dim.11), calls=%async_computation | async-start | bytes 65536 | tf_op jit(solution)/shard_map/all_to_all | solution.py:254
  11.1 9.1 %collective-permute-start.3 = (bf16[2,128,256]{2,1,0:T(8,128)(2,1)S(1)}, bf16[2,128,256]{2,1,0:T(8,128)(2,1)S(1)}, u32[]{:S(2)}, u32[]{:S(2)}) collective-permute-start(bf16[2,128,256]{2,1,0:T(8,128)(2,1)S(1)} %pad_maximum_fusion.1), channel_id=1, source_target_pairs={{0,2},{1,3},{2,0},{3,1},{4,6},{5,7},{6,4},{7,5},{8,10},{9,11},{10,... | collective-permute-start | bytes 393224 | tf_op jit(solution)/shard_map/ppermute | solution.py:267
  12.9 17.7 %collective-permute-start.1 = (bf16[1024,128]{1,0:T(8,128)(2,1)S(1)}, bf16[1024,128]{1,0:T(8,128)(2,1)S(1)}, u32[]{:S(2)}, u32[]{:S(2)}) collective-permute-start(bf16[1024,128]{1,0:T(8,128)(2,1)S(1)} %get-tuple-element.19), channel_id=1, source_target_pairs={{2,0},{3,1},{4,2},{5,3},{6,4},{7,5},{10,8},{11,9},{12,10},{13,11},... | collective-permute-start | bytes 786440 | tf_op jit(solution)/shard_map/ppermute | solution.py:15
  18.8 7.4 %collective-permute-start = (f32[2,128,128]{2,1,0:T(8,128)S(1)}, f32[2,128,128]{2,1,0:T(8,128)S(1)}, u32[]{:S(2)}, u32[]{:S(2)}) collective-permute-start(f32[2,128,128]{2,1,0:T(8,128)S(1)} %get-tuple-element.14.own_gram_ref), channel_id=1, source_target_pairs={{2,0},{3,1},{4,2},{5,3},{6,4},{7,5},{10,8},{11,9},{12,10},{13,11},... | collective-permute-start | bytes 393224 | tf_op jit(solution)/shard_map/ppermute | solution.py:15
  20.1 6.0 %copy-start.3 = (f32[1,2,32,128]{3,2,1,0:T(8,128)S(1)}, f32[1,2,32,128]{3,2,1,0:T(8,128)}, u32[]{:S(2)}) copy-start(f32[1,2,32,128]{3,2,1,0:T(8,128)} %param.6) | copy-start | bytes 98308
  20.2 10.4 %collective-permute-start.4 = (bf16[4,128,256]{2,1,0:T(8,128)(2,1)S(1)}, bf16[4,128,256]{2,1,0:T(8,128)(2,1)S(1)}, u32[]{:S(2)}, u32[]{:S(2)}) collective-permute-start(bf16[4,128,256]{2,1,0:T(8,128)(2,1)S(1)} %pad_maximum_fusion), channel_id=1, source_target_pairs={{0,1},{1,0},{2,3},{3,2},{4,5},{5,4},{6,7},{7,6},{8,9},{9,8},{10,11... | collective-permute-start | bytes 786440 | tf_op jit(solution)/shard_map/ppermute | solution.py:267
  32.1 4.6 %collective-permute-start.5 = (bf16[192,128]{1,0:T(8,128)(2,1)S(1)}, bf16[192,128]{1,0:T(8,128)(2,1)S(1)}, u32[]{:S(2)}, u32[]{:S(2)}) collective-permute-start(bf16[192,128]{1,0:T(8,128)(2,1)S(1)} %get-tuple-element.21), channel_id=1, source_target_pairs={{0,2},{1,3},{2,0},{3,1},{4,6},{5,7},{6,4},{7,5},{8,10},{9,11},{10,... | collective-permute-start | bytes 147464 | tf_op jit(solution)/shard_map/ppermute | solution.py:295
  32.9 6.0 %collective-permute-start.6 = (bf16[192,128]{1,0:T(8,128)(2,1)S(1)}, bf16[192,128]{1,0:T(8,128)(2,1)S(1)}, u32[]{:S(2)}, u32[]{:S(2)}) collective-permute-start(bf16[192,128]{1,0:T(8,128)(2,1)S(1)} %get-tuple-element.22), channel_id=1, source_target_pairs={{0,4},{1,5},{2,6},{3,7},{4,0},{5,1},{6,2},{7,3},{8,12},{9,13},{10,... | collective-permute-start | bytes 147464 | tf_op jit(solution)/shard_map/ppermute | solution.py:295
  34.2 6.0 %collective-permute-start.7 = (bf16[192,128]{1,0:T(8,128)(2,1)S(1)}, bf16[192,128]{1,0:T(8,128)(2,1)S(1)}, u32[]{:S(2)}, u32[]{:S(2)}) collective-permute-start(bf16[192,128]{1,0:T(8,128)(2,1)S(1)} %get-tuple-element.23), channel_id=1, source_target_pairs={{0,6},{1,7},{2,4},{3,5},{4,2},{5,3},{6,0},{7,1},{8,14},{9,15},{10,... | collective-permute-start | bytes 147464 | tf_op jit(solution)/shard_map/ppermute | solution.py:295
  40.2 1.4 %collective-permute-start.8 = (bf16[4,128,128]{2,1,0:T(8,128)(2,1)S(1)}, bf16[4,128,128]{2,1,0:T(8,128)(2,1)S(1)}, u32[]{:S(2)}, u32[]{:S(2)}) collective-permute-start(bf16[4,128,128]{2,1,0:T(8,128)(2,1)S(1)} %pad_maximum_fusion.2), channel_id=1, source_target_pairs={{0,1},{1,0},{2,3},{3,2},{4,5},{5,4},{6,7},{7,6},{8,9},{9,8},{10,11... | collective-permute-start | bytes 393224 | tf_op jit(solution)/shard_map/ppermute | solution.py:297

commit v4 on v3

--- a/solution.py
+++ b/solution.py
@@ -6,7 +6,6 @@
 from jax.sharding import PartitionSpec as P
 
 ITERS = 3
-EXACT = lax.Precision.HIGHEST
 
 
 def from_behind(block, axis, distance):
@@ -15,7 +14,7 @@
     return lax.ppermute(block, axis, route)
 
 
-def vmem_call(body, outs, name, flops, nbytes, in_specs=None, limit=None):
+def vmem_call(body, outs, name, flops, nbytes, in_specs=None, limit=None, scratch=()):
     params = pltpu.CompilerParams(vmem_limit_bytes=12 << 20) if limit is None else pltpu.CompilerParams(vmem_limit_bytes=limit)
     extra = {} if in_specs is None else {"in_specs": in_specs}
     return pl.pallas_call(
@@ -23,35 +22,58 @@
         out_shape=outs,
         name=name,
         compiler_params=params,
+        scratch_shapes=scratch,
         cost_estimate=pl.CostEstimate(flops=flops, bytes_accessed=nbytes, transcendentals=0),
         **extra,
     )
 
 
-def rows_dot(left, right, precision=None):
-    return lax.dot_general(
-        left, right, (((1,), (1,)), ((), ())), precision=precision, preferred_element_type=jnp.float32
-    )
+def rows_dot(left, right):
+    return lax.dot_general(left, right, (((1,), (1,)), ((), ())), preferred_element_type=jnp.float32)
 
 
 def columns_dot(left, right):
     return lax.dot_general(left, right, (((0,), (0,)), ((), ())), preferred_element_type=jnp.float32)
 
 
-def sum_body(strip_ref, sums_ref, middle_ref):
-    rows = strip_ref.shape[0]
-    ones = jnp.ones((8, rows), jnp.bfloat16)
-    sums_ref[...] = jnp.dot(ones, strip_ref[...], preferred_element_type=jnp.float32)
+def sum_body(strip_ref, row_ref, block_ref, notes_ref, middle_ref, held_ref, codes_ref, strip_sems, code_sems):
     cell = middle_ref.shape[0]
-    middle_ref[...] = strip_ref[cell : 2 * cell, :]
-
-
-def background_of(notes_ref, frames, pixel_total):
-    return jnp.sum(notes_ref[:, 0:frames], axis=0, keepdims=True) / pixel_total
+    cells = strip_ref.shape[0] // cell
+    copies = [
+        pltpu.make_async_copy(
+            strip_ref.at[pl.ds(i * cell, cell)], held_ref.at[pl.ds(i * cell, cell)], strip_sems.at[i]
+        )
+        for i in range(cells)
+    ]
+    code_copies = [
+        pltpu.make_async_copy(source, codes_ref.at[pl.ds(i, 1)], code_sems.at[i])
+        for i, source in enumerate((row_ref, block_ref))
+    ]
+    for copy in copies + code_copies:
+        copy.start()
+    ones = jnp.ones((8, cell), jnp.bfloat16)
+    total = jnp.zeros((8, strip_ref.shape[1]), jnp.float32)
+    for i in range(cells):
+        copies[i].wait()
+        piece = held_ref[i * cell : (i + 1) * cell, :]
+        total = total + jnp.dot(ones, piece, preferred_element_type=jnp.float32)
+        if i == 1:
+            middle_ref[...] = piece
+    for copy in code_copies:
+        copy.wait()
+    codes = (codes_ref[0:1, :] * 4 + codes_ref[1:2, :]).astype(jnp.float32)
+    odd = lax.broadcasted_iota(jnp.int32, notes_ref.shape, 0) % 2 == 1
+    notes_ref[...] = jnp.where(odd, codes, total[0:1])
+
+
+def background_of(notes_ref, pixel_total):
+    notes = notes_ref[...]
+    even = lax.broadcasted_iota(jnp.int32, notes.shape, 0) % 2 == 0
+    return jnp.sum(jnp.where(even, notes, 0.0), axis=0, keepdims=True) / pixel_total
 
 
 def gram_body(pixel_total, notes_ref, strip_ref, gram_ref, middle_ref):
-    background = background_of(notes_ref, strip_ref.shape[1], pixel_total)
+    background = background_of(notes_ref, pixel_total)
     cell = middle_ref.shape[0]
     cells = strip_ref.shape[0] // cell
     grams = []
@@ -65,43 +87,48 @@
         gram_ref[column] = grams[column] + grams[column + 1]
 
 
-def forward_solve(grams, sides):
+def forward_solve(grams, sides, band=16):
     rank = grams[0].shape[0]
     blocks = rank // 8
     width = 128
     sub = lax.broadcasted_iota(jnp.int32, (8, width), 0)
     pad = jnp.zeros((rank, width - rank), jnp.float32)
-    grams = [jnp.concatenate([gram, pad], 1) for gram in grams]
 
     def split(matrix):
         return [matrix[8 * b : 8 * b + 8] for b in range(blocks)]
 
-    grams = [split(gram) for gram in grams]
+    def spread(row_or_column):
+        return jnp.broadcast_to(row_or_column, (8, width))
+
+    grams = [split(jnp.concatenate([gram, pad], 1)) for gram in grams]
     sides = [[split(side) for side in group] for group in sides]
     inverse = [[None] * blocks for _ in grams]
-    for block in range(blocks):
+    for start in range(0, rank, band):
         columns = [
             {
-                (j, b): jnp.broadcast_to(gram[b][:, 8 * block + j : 8 * block + j + 1], (8, width))
-                for j in range(8)
-                for b in range(block, blocks)
+                (j, b): spread(gram[b][:, start + j : start + j + 1])
+                for j in range(band)
+                for b in range((start + j) // 8, blocks)
             }
             for gram in grams
         ]
-        for j in range(8):
+        for j in range(band):
+            block, line = divmod(start + j, 8)
             for patch in range(len(grams)):
                 column, gram = columns[patch], grams[patch]
-                pivot = 1.0 / jnp.broadcast_to(column[(j, block)][j : j + 1, :], (8, width))
+                pivot = 1.0 / spread(column[(j, block)][line : line + 1, :])
                 known = inverse[patch][block]
-                inverse[patch][block] = pivot if known is None else jnp.where(sub == j, pivot, known)
+                inverse[patch][block] = pivot if known is None else jnp.where(sub == line, pivot, known)
                 factor = {b: column[(j, b)] * pivot for b in range(block, blocks)}
-                factor[block] = jnp.where(sub > j, factor[block], 0.0)
-                for later in range(j + 1, 8):
-                    entry = jnp.broadcast_to(column[(j, block)][later : later + 1, :], (8, width))
-                    for b in range(block, blocks):
+                factor[block] = jnp.where(sub > line, factor[block], 0.0)
+                for later in range(j + 1, band):
+                    later_block, later_line = divmod(start + later, 8)
+                    entry = spread(column[(j, later_block)][later_line : later_line + 1, :])
+                    for b in range(later_block, blocks):
                         column[(later, b)] = column[(later, b)] - factor[b] * entry
-                for target in [gram] + sides[patch]:
-                    row = jnp.broadcast_to(target[block][j : j + 1, :], (8, width))
+                targets = sides[patch] if start + band == rank else [gram] + sides[patch]
+                for target in targets:
+                    row = spread(target[block][line : line + 1, :])
                     for b in range(block, blocks):
                         target[b] = target[b] - factor[b] * row
     return [
@@ -123,15 +150,24 @@
 
 def patch_body(own_gram_ref, low_gram_ref, start_ref, temporal_ref, parts_ref, rounded_ref):
     patches = start_ref.shape[0]
-    grams = [own_gram_ref[p] + low_gram_ref[p] for p in range(patches)]
+    grams = [
+        jnp.concatenate(three_parts(own_gram_ref[p] + low_gram_ref[p]), 1) for p in range(patches)
+    ]
+    rank, frames = start_ref.shape[1], start_ref.shape[2]
     temporal = [start_ref[p] for p in range(patches)]
     whitened = None
     for step in range(ITERS):
-        rounded = [t.astype(jnp.bfloat16).astype(jnp.float32) for t in temporal]
-        moved = [jnp.dot(t, g, precision=EXACT, preferred_element_type=jnp.float32) for t, g in zip(rounded, grams)]
-        inner = [rows_dot(m, t, EXACT) for m, t in zip(moved, rounded)]
+        rounded = [t.astype(jnp.bfloat16) for t in temporal]
+        moved, inner = [], []
+        for narrow, gram in zip(rounded, grams):
+            terms = jnp.dot(narrow, gram, preferred_element_type=jnp.float32)
+            image = terms[:, :frames] + terms[:, frames : 2 * frames] + terms[:, 2 * frames :]
+            terms = rows_dot(jnp.concatenate(three_parts(image), 0), narrow)
+            moved.append(image)
+            inner.append(terms[:rank] + terms[rank : 2 * rank] + terms[2 * rank :])
         last = step == ITERS - 1
-        solved = forward_solve(inner, [[m, t] if last else [m] for m, t in zip(moved, rounded)])
+        sides = [[m, t.astype(jnp.float32)] if last else [m] for m, t in zip(moved, rounded)]
+        solved = forward_solve(inner, sides)
         temporal = [s[0] for s in solved]
         if last:
             whitened = jnp.concatenate([s[1] for s in solved], 0)
@@ -149,7 +185,7 @@
     parts = parts_ref[...]
     temporal_rounded = rounded_ref[...]
     ranks, frames = temporal_rounded.shape
-    background = background_of(notes_ref, frames, pixel_total)
+    background = background_of(notes_ref, pixel_total)
     lower = (low_ref[...].astype(jnp.float32) - background).astype(jnp.bfloat16)
     pixels = 256
     bands = []
@@ -168,7 +204,7 @@
 
     def coefficients(held_ref, entry, owner):
         projected = rows_dot(stacked, held_ref[entry])
-        codes = notes_ref[pl.ds(plane_start + owner, 1), :][:, frames : frames + sources].astype(jnp.int32)
+        codes = notes_ref[pl.ds(2 * (plane_start + owner) + 1, 1), :].astype(jnp.int32)
         total = jnp.zeros((ranks, sources), jnp.float32)
         for role in range(2):
             for quarter in range(4):
@@ -242,15 +278,25 @@
     def shape(dims, kind):
         return jax.ShapeDtypeStruct(dims, kind)
 
-    sums, middle = vmem_call(
+    outside = pl.BlockSpec(memory_space=pltpu.HBM)
+    notes, middle, near_strip = vmem_call(
         sum_body,
-        [shape((8, frames), f32), shape((cell, frames), bf16)],
+        [shape((2 * devices, frames), f32), shape((cell, frames), bf16), shape(strip.shape, bf16)],
         "frame_sums",
         2 * cells * cell * frames,
         2 * cells * cell * frames,
-    )(strip)
-    codes = (source_row.reshape(1, sources) * 4 + footprint_block.reshape(1, sources)).astype(f32)
-    notes = jnp.broadcast_to(jnp.concatenate([sums[0:1], codes], 1), (devices, frames + sources))
+        in_specs=[outside] * 3,
+        scratch=[
+            pltpu.VMEM((8, sources), jnp.int32),
+            pltpu.SemaphoreType.DMA((cells,)),
+            pltpu.SemaphoreType.DMA((2,)),
+        ],
+    )(
+        *(
+            pltpu.with_memory_space_constraint(x, pltpu.HBM)
+            for x in (strip, source_row.reshape(1, sources), footprint_block.reshape(1, sources))
+        )
+    )
     notes = lax.all_to_all(notes, ("plane", "tile"), 0, 0, tiled=True)
     low_middle = from_behind(middle, "tile", -2)
     own_gram, own_middle = vmem_call(
@@ -259,7 +305,7 @@
         "own_grams",
         2 * cells * cell * frames * frames,
         2 * cells * cell * frames,
-    )(notes, strip)
+    )(notes, near_strip)
     held = [footprints]
     for bit in reversed(range(tile_count.bit_length() - 1)):
         route = [(i, i ^ (1 << bit)) for i in range(tile_count)]

time: 42.7 us -> 40.6 us (0.951)
  local copies, waits for them, and re-layouts: 2.25 us -> 0.02 us
  Pallas kernels: 7.4 us -> 8.55 us
  waiting for transfers between devices: 14.9 us -> 13.8 us
    pallas_call x1, Pallas kernels: 0.21 us -> 2.05 us  [on_device(): vmem_call(sum_body, [shape((2 * devices, frames), f32), shape((cell, fram...]
    unnamed x13 -> x4, local copies, waits for them, and re-layouts: 1.6 us -> 0.01 us
    ppermute x3, waiting for transfers between devices: 3.59 us -> 2.54 us  [on_device(): arrived.append(lax.ppermute(replies[offset], 'tile', route))]
    pallas_call x1, Pallas kernels: 4.44 us -> 3.74 us  [on_device(): vmem_call(patch_body, [shape((patches, rank, frames), f32), shape((3 * ra...]
    broadcast_in_dim x1 -> x0, local copies, waits for them, and re-layouts: 0.63 us -> none  [on_device(): jnp.broadcast_to(jnp.concatenate([sums[0:1], codes], 1), (devices, frames...]
  transfers between devices with their start and end apart: 10 -> 10, of which waited for: 6 -> 5; matrix products, arithmetic and copies ran while one was open for 2% -> 0% of each run, Pallas kernels for 12% -> 15%
where the time goes in v4:
time: 40.6 us; the launch traced here: 40.3 us
  starting transfers between devices  17 us (42%)
  waiting for transfers between devices  13.8 us (34%)
  Pallas kernels  8.55 us (21%)
  between operations  0.74 us (2%)
    ppermute x3, starting transfers between devices, on_device(): held.append(lax.ppermute(everything, 'tile', route))  6.12 us
    ppermute x2, waiting for transfers between devices, from_behind(): return lax.ppermute(block, axis, route)  5.82 us
    ppermute x3, starting transfers between devices, on_device(): arrived.append(lax.ppermute(replies[offset], 'tile', route))  4.45 us
    all_to_all x1, waiting for transfers between devices, on_device(): notes = lax.all_to_all(notes, ('plane', 'tile'), 0, 0, tiled=True)  4.14 us
    all_to_all x1, starting transfers between devices, on_device(): notes = lax.all_to_all(notes, ('plane', 'tile'), 0, 0, tiled=True)  3.83 us
    pallas_call x1, Pallas kernels, on_device(): vmem_call(patch_body, [shape((patches, rank, frames), f32), shape((3 * ra...  3.74 us
    ppermute x2, starting transfers between devices, from_behind(): return lax.ppermute(block, axis, route)  2.57 us
    ppermute x3, waiting for transfers between devices, on_device(): arrived.append(lax.ppermute(replies[offset], 'tile', route))  2.54 us
  transfers between devices with their start and end apart: 10, of which 5 were waited for; matrix products, arithmetic and copies ran while one was open for 0% of the time, Pallas kernels for 15%

profile of v4, /device:TPU:0, one launch (start us, length us, event | category | flops | bytes accessed | tf_op | source)
XLA Modules:
  0.0 40.3 jit_solution(4716807581400365139)
XLA Ops:
  0.6 4.1 %collective-permute-start.2 = (bf16[1,128,256]{2,1,0:T(8,128)(2,1)}, bf16[1,128,256]{2,1,0:T(8,128)(2,1)S(1)}, u32[]{:S(2)}, u32[]{:S(2)}) collective-permute-start(bf16[1,128,256]{2,1,0:T(8,128)(2,1)} %refs_6_.1), channel_id=1, source_target_pairs={{0,4},{1,5},{2,6},{3,7},{4,0},{5,1},{6,2},{7,3},{8,12},{9,13},{10,... | collective-permute-start | bytes 196616 | tf_op jit(solution)/shard_map/ppermute | solution.py:313
  4.7 2.1 %frame_sums.1 = (f32[64,128]{1,0:T(8,128)}, bf16[1024,128]{1,0:T(8,128)(2,1)S(1)}, bf16[3072,128]{1,0:T(8,128)(2,1)S(1)}) custom-call(bf16[3072,128]{1,0:T(8,128)(2,1)} %bitcast.20, s32[1,128]{1,0:T(1,128)} %bitcast.22, s32[1,128]{1,0:T(1,128)} %block_ref.1), custom_call_target="tpu_custom_call" | custom-call | flops 786432 | bytes 786432 | tf_op jit(solution)/shard_map/frame_sums/pallas_call | solution.py:282
  6.8 0.0 copy-start
  6.8 3.8 %all-to-all-start = ((f32[32,2,128]{2,1,0:T(2,128)}), f32[32,2,128]{2,1,0:T(2,128)S(1)}, u32[]{:S(2)}, u32[]{:S(2)}) async-start(f32[32,2,128]{2,1,0:T(2,128)} %bitcast.2), calls=%async_computation | async-start | bytes 65536 | tf_op jit(solution)/shard_map/all_to_all | solution.py:300
  10.6 0.0 collective-permute-done.2.refs_7_
  10.7 0.0 copy-done
  10.7 1.8 %collective-permute-start.3 = (bf16[2,128,256]{2,1,0:T(8,128)(2,1)S(1)}, bf16[2,128,256]{2,1,0:T(8,128)(2,1)S(1)}, u32[]{:S(2)}, u32[]{:S(2)}) collective-permute-start(bf16[2,128,256]{2,1,0:T(8,128)(2,1)S(1)} %pad_maximum_fusion.1), channel_id=1, source_target_pairs={{0,2},{1,3},{2,0},{3,1},{4,6},{5,7},{6,4},{7,5},{8,10},{9,11},{10,... | collective-permute-start | bytes 393224 | tf_op jit(solution)/shard_map/ppermute | solution.py:313
  12.5 1.3 %collective-permute-start.1 = (bf16[1024,128]{1,0:T(8,128)(2,1)S(1)}, bf16[1024,128]{1,0:T(8,128)(2,1)S(1)}, u32[]{:S(2)}, u32[]{:S(2)}) collective-permute-start(bf16[1024,128]{1,0:T(8,128)(2,1)S(1)} %get-tuple-element.21), channel_id=1, source_target_pairs={{2,0},{3,1},{4,2},{5,3},{6,4},{7,5},{10,8},{11,9},{12,10},{13,11},... | collective-permute-start | bytes 786440 | tf_op jit(solution)/shard_map/ppermute | solution.py:14
  13.8 4.1 %all-to-all-done = f32[32,2,128]{2,1,0:T(2,128)S(1)} async-done(((f32[32,2,128]{2,1,0:T(2,128)}), f32[32,2,128]{2,1,0:T(2,128)S(1)}, u32[]{:S(2)}, u32[]{:S(2)}) %all-to-all-start) | async-done | bytes 32800 | tf_op jit(solution)/shard_map/all_to_all | solution.py:300
  18.0 0.4 %own_grams.1 = (f32[2,128,128]{2,1,0:T(8,128)S(1)}, bf16[1024,128]{1,0:T(8,128)(2,1)S(1)}) custom-call(f32[64,128]{1,0:T(8,128)S(1)} %bitcast.17, bf16[3072,128]{1,0:T(8,128)(2,1)S(1)} %get-tuple-element.15.refs_1_), custom_call_target="tpu_custom_call" | custom-call | flops 100663296 | bytes 786432 | tf_op jit(solution)/shard_map/own_grams/pallas_call | solution.py:302
  18.4 1.3 %collective-permute-start = (f32[2,128,128]{2,1,0:T(8,128)S(1)}, f32[2,128,128]{2,1,0:T(8,128)S(1)}, u32[]{:S(2)}, u32[]{:S(2)}) collective-permute-start(f32[2,128,128]{2,1,0:T(8,128)S(1)} %get-tuple-element.16.own_gram_ref), channel_id=1, source_target_pairs={{2,0},{3,1},{4,2},{5,3},{6,4},{7,5},{10,8},{11,9},{12,10},{13,11},... | collective-permute-start | bytes 393224 | tf_op jit(solution)/shard_map/ppermute | solution.py:14
  19.7 0.1 pad_add_fusion.refs_0_
  19.8 0.0 copy-start.1
  19.8 0.0 collective-permute-done.3.refs_8_
  19.8 0.2 collective-permute-start.4
  20.0 5.8 %collective-permute-done.low_gram_ref = f32[2,128,128]{2,1,0:T(8,128)S(1)} collective-permute-done((f32[2,128,128]{2,1,0:T(8,128)S(1)}, f32[2,128,128]{2,1,0:T(8,128)S(1)}, u32[]{:S(2)}, u32[]{:S(2)}) %collective-permute-start) | collective-permute-done | bytes 131104 | tf_op jit(solution)/shard_map/ppermute | solution.py:14
  25.8 0.0 copy-done.1
  25.8 3.7 %patch_factors.1 = (f32[2,32,128]{2,1,0:T(8,128)}, bf16[192,128]{1,0:T(8,128)(2,1)S(1)}, bf16[64,128]{1,0:T(8,128)(2,1)S(1)}) custom-call(f32[2,128,128]{2,1,0:T(8,128)S(1)} %get-tuple-element.16.own_gram_ref, f32[2,128,128]{2,1,0:T(8,128)S(1)} %collective-permute-done.low_gram_ref, f32[2,32,128]{2,1,0:T(8,128)S(1)} %bitcast.19), custom_call_target="tpu_custom_call" | custom-call | flops 6000000000 | bytes 1048576 | tf_op jit(solution)/shard_map/patch_factors/pallas_call | solution.py:318
  29.5 0.0 collective-permute-done.1.refs_5_
  29.5 0.0 collective-permute-done.4.refs_9_
  29.5 1.5 %coefficients.1 = (bf16[192,128]{1,0:T(8,128)(2,1)S(1)}, bf16[192,128]{1,0:T(8,128)(2,1)S(1)}, bf16[192,128]{1,0:T(8,128)(2,1)S(1)}, bf16[192,128]{1,0:T(8,128)(2,1)S(1)}) custom-call(s32[2]{0:T(128)S(1)} %pad_add_fusion.refs_0_, bf16[192,128]{1,0:T(8,128)(2,1)S(1)} %get-tuple-element.18.refs_1_, bf16[64,128]{1,0:T(8,128)(2,1)S(1)} %get-tuple-element.19.refs_2_, ...), custom_call_target="tpu_custom_call" | custom-call | flops 268435456 | bytes 2097152 | tf_op jit(solution)/shard_map/coefficients/pallas_call | solution.py:327
  31.0 1.0 %collective-permute-start.7 = (bf16[192,128]{1,0:T(8,128)(2,1)S(1)}, bf16[192,128]{1,0:T(8,128)(2,1)S(1)}, u32[]{:S(2)}, u32[]{:S(2)}) collective-permute-start(bf16[192,128]{1,0:T(8,128)(2,1)S(1)} %get-tuple-element.25), channel_id=1, source_target_pairs={{0,6},{1,7},{2,4},{3,5},{4,2},{5,3},{6,0},{7,1},{8,14},{9,15},{10,... | collective-permute-start | bytes 147464 | tf_op jit(solution)/shard_map/ppermute | solution.py:341
  32.0 1.3 %collective-permute-start.6 = (bf16[192,128]{1,0:T(8,128)(2,1)S(1)}, bf16[192,128]{1,0:T(8,128)(2,1)S(1)}, u32[]{:S(2)}, u32[]{:S(2)}) collective-permute-start(bf16[192,128]{1,0:T(8,128)(2,1)S(1)} %get-tuple-element.24), channel_id=1, source_target_pairs={{0,4},{1,5},{2,6},{3,7},{4,0},{5,1},{6,2},{7,3},{8,12},{9,13},{10,... | collective-permute-start | bytes 147464 | tf_op jit(solution)/shard_map/ppermute | solution.py:341
  33.3 2.2 %collective-permute-start.5 = (bf16[192,128]{1,0:T(8,128)(2,1)S(1)}, bf16[192,128]{1,0:T(8,128)(2,1)S(1)}, u32[]{:S(2)}, u32[]{:S(2)}) collective-permute-start(bf16[192,128]{1,0:T(8,128)(2,1)S(1)} %get-tuple-element.23), channel_id=1, source_target_pairs={{0,2},{1,3},{2,0},{3,1},{4,6},{5,7},{6,4},{7,5},{8,10},{9,11},{10,... | collective-permute-start | bytes 147464 | tf_op jit(solution)/shard_map/ppermute | solution.py:341
  35.5 1.6 %collective-permute-done.7.refs_3_ = bf16[192,128]{1,0:T(8,128)(2,1)S(1)} collective-permute-done((bf16[192,128]{1,0:T(8,128)(2,1)S(1)}, bf16[192,128]{1,0:T(8,128)(2,1)S(1)}, u32[]{:S(2)}, u32[]{:S(2)}) %collective-permute-start.7) | collective-permute-done | bytes 49184 | tf_op jit(solution)/shard_map/ppermute | solution.py:341
  37.1 0.9 %collective-permute-done.6.refs_2_ = bf16[192,128]{1,0:T(8,128)(2,1)S(1)} collective-permute-done((bf16[192,128]{1,0:T(8,128)(2,1)S(1)}, bf16[192,128]{1,0:T(8,128)(2,1)S(1)}, u32[]{:S(2)}, u32[]{:S(2)}) %collective-permute-start.6) | collective-permute-done | bytes 49184 | tf_op jit(solution)/shard_map/ppermute | solution.py:341
  38.0 0.0 collective-permute-done.5.refs_1_
  38.1 0.1 collective-permute-start.8
  38.1 1.3 %collective-permute-done.8.refs_4_ = bf16[4,128,128]{2,1,0:T(8,128)(2,1)S(1)} collective-permute-done((bf16[4,128,128]{2,1,0:T(8,128)(2,1)S(1)}, bf16[4,128,128]{2,1,0:T(8,128)(2,1)S(1)}, u32[]{:S(2)}, u32[]{:S(2)}) %collective-permute-start.8) | collective-permute-done | bytes 131104 | tf_op jit(solution)/shard_map/ppermute | solution.py:343
  39.5 0.9 %source_traces.1 = f32[128,128]{1,0:T(8,128)} custom-call(bf16[192,128]{1,0:T(8,128)(2,1)S(1)} %get-tuple-element.22.refs_0_, bf16[192,128]{1,0:T(8,128)(2,1)S(1)} %collective-permute-done.5.refs_1_, bf16[192,128]{1,0:T(8,128)(2,1)S(1)} %collective-permute-done.6.refs_2_, bf16[192,128]{1,0:T(8,128)(2,1)S(1)} %collective-permute-done.7.refs_3_, ...), custom_call_target="tpu_custom_call" | custom-call | flops 16777216 | bytes 524288 | tf_op jit(solution)/shard_map/source_traces/pallas_call | solution.py:344
  (7 shorter events, 0.1 us)
Async XLA Ops:
  0.6 10.0 %collective-permute-start.2 = (bf16[1,128,256]{2,1,0:T(8,128)(2,1)}, bf16[1,128,256]{2,1,0:T(8,128)(2,1)S(1)}, u32[]{:S(2)}, u32[]{:S(2)}) collective-permute-start(bf16[1,128,256]{2,1,0:T(8,128)(2,1)} %refs_6_.1), channel_id=1, source_target_pairs={{0,4},{1,5},{2,6},{3,7},{4,0},{5,1},{6,2},{7,3},{8,12},{9,13},{10,... | collective-permute-start | bytes 196616 | tf_op jit(solution)/shard_map/ppermute | solution.py:313
  6.8 3.9 %copy-start = (bf16[1,128,256]{2,1,0:T(8,128)(2,1)S(1)}, bf16[1,128,256]{2,1,0:T(8,128)(2,1)}, u32[]{:S(2)}) copy-start(bf16[1,128,256]{2,1,0:T(8,128)(2,1)} %refs_6_.1) | copy-start | bytes 196612
  6.8 11.2 %all-to-all-start = ((f32[32,2,128]{2,1,0:T(2,128)}), f32[32,2,128]{2,1,0:T(2,128)S(1)}, u32[]{:S(2)}, u32[]{:S(2)}) async-start(f32[32,2,128]{2,1,0:T(2,128)} %bitcast.2), calls=%async_computation | async-start | bytes 65536 | tf_op jit(solution)/shard_map/all_to_all | solution.py:300
  10.7 9.1 %collective-permute-start.3 = (bf16[2,128,256]{2,1,0:T(8,128)(2,1)S(1)}, bf16[2,128,256]{2,1,0:T(8,128)(2,1)S(1)}, u32[]{:S(2)}, u32[]{:S(2)}) collective-permute-start(bf16[2,128,256]{2,1,0:T(8,128)(2,1)S(1)} %pad_maximum_fusion.1), channel_id=1, source_target_pairs={{0,2},{1,3},{2,0},{3,1},{4,6},{5,7},{6,4},{7,5},{8,10},{9,11},{10,... | collective-permute-start | bytes 393224 | tf_op jit(solution)/shard_map/ppermute | solution.py:313
  12.5 17.0 %collective-permute-start.1 = (bf16[1024,128]{1,0:T(8,128)(2,1)S(1)}, bf16[1024,128]{1,0:T(8,128)(2,1)S(1)}, u32[]{:S(2)}, u32[]{:S(2)}) collective-permute-start(bf16[1024,128]{1,0:T(8,128)(2,1)S(1)} %get-tuple-element.21), channel_id=1, source_target_pairs={{2,0},{3,1},{4,2},{5,3},{6,4},{7,5},{10,8},{11,9},{12,10},{13,11},... | collective-permute-start | bytes 786440 | tf_op jit(solution)/shard_map/ppermute | solution.py:14
  18.4 7.4 %collective-permute-start = (f32[2,128,128]{2,1,0:T(8,128)S(1)}, f32[2,128,128]{2,1,0:T(8,128)S(1)}, u32[]{:S(2)}, u32[]{:S(2)}) collective-permute-start(f32[2,128,128]{2,1,0:T(8,128)S(1)} %get-tuple-element.16.own_gram_ref), channel_id=1, source_target_pairs={{2,0},{3,1},{4,2},{5,3},{6,4},{7,5},{10,8},{11,9},{12,10},{13,11},... | collective-permute-start | bytes 393224 | tf_op jit(solution)/shard_map/ppermute | solution.py:14
  19.8 6.0 %copy-start.1 = (f32[1,2,32,128]{3,2,1,0:T(8,128)S(1)}, f32[1,2,32,128]{3,2,1,0:T(8,128)}, u32[]{:S(2)}) copy-start(f32[1,2,32,128]{3,2,1,0:T(8,128)} %param.6) | copy-start | bytes 98308
  19.8 9.7 %collective-permute-start.4 = (bf16[4,128,256]{2,1,0:T(8,128)(2,1)S(1)}, bf16[4,128,256]{2,1,0:T(8,128)(2,1)S(1)}, u32[]{:S(2)}, u32[]{:S(2)}) collective-permute-start(bf16[4,128,256]{2,1,0:T(8,128)(2,1)S(1)} %pad_maximum_fusion), channel_id=1, source_target_pairs={{0,1},{1,0},{2,3},{3,2},{4,5},{5,4},{6,7},{7,6},{8,9},{9,8},{10,11... | collective-permute-start | bytes 786440 | tf_op jit(solution)/shard_map/ppermute | solution.py:313
  31.0 6.1 %collective-permute-start.7 = (bf16[192,128]{1,0:T(8,128)(2,1)S(1)}, bf16[192,128]{1,0:T(8,128)(2,1)S(1)}, u32[]{:S(2)}, u32[]{:S(2)}) collective-permute-start(bf16[192,128]{1,0:T(8,128)(2,1)S(1)} %get-tuple-element.25), channel_id=1, source_target_pairs={{0,6},{1,7},{2,4},{3,5},{4,2},{5,3},{6,0},{7,1},{8,14},{9,15},{10,... | collective-permute-start | bytes 147464 | tf_op jit(solution)/shard_map/ppermute | solution.py:341
  32.0 6.0 %collective-permute-start.6 = (bf16[192,128]{1,0:T(8,128)(2,1)S(1)}, bf16[192,128]{1,0:T(8,128)(2,1)S(1)}, u32[]{:S(2)}, u32[]{:S(2)}) collective-permute-start(bf16[192,128]{1,0:T(8,128)(2,1)S(1)} %get-tuple-element.24), channel_id=1, source_target_pairs={{0,4},{1,5},{2,6},{3,7},{4,0},{5,1},{6,2},{7,3},{8,12},{9,13},{10,... | collective-permute-start | bytes 147464 | tf_op jit(solution)/shard_map/ppermute | solution.py:341
  33.3 4.7 %collective-permute-start.5 = (bf16[192,128]{1,0:T(8,128)(2,1)S(1)}, bf16[192,128]{1,0:T(8,128)(2,1)S(1)}, u32[]{:S(2)}, u32[]{:S(2)}) collective-permute-start(bf16[192,128]{1,0:T(8,128)(2,1)S(1)} %get-tuple-element.23), channel_id=1, source_target_pairs={{0,2},{1,3},{2,0},{3,1},{4,6},{5,7},{6,4},{7,5},{8,10},{9,11},{10,... | collective-permute-start | bytes 147464 | tf_op jit(solution)/shard_map/ppermute | solution.py:341
  38.1 1.4 %collective-permute-start.8 = (bf16[4,128,128]{2,1,0:T(8,128)(2,1)S(1)}, bf16[4,128,128]{2,1,0:T(8,128)(2,1)S(1)}, u32[]{:S(2)}, u32[]{:S(2)}) collective-permute-start(bf16[4,128,128]{2,1,0:T(8,128)(2,1)S(1)} %pad_maximum_fusion.2), channel_id=1, source_target_pairs={{0,1},{1,0},{2,3},{3,2},{4,5},{5,4},{6,7},{7,6},{8,9},{9,8},{10,11... | collective-permute-start | bytes 393224 | tf_op jit(solution)/shard_map/ppermute | solution.py:343

commit v5 on v4

--- a/solution.py
+++ b/solution.py
@@ -174,7 +174,7 @@
     for p in range(patches):
         temporal_ref[p] = temporal[p]
     rounded_ref[...] = jnp.concatenate(temporal, 0).astype(jnp.bfloat16)
-    parts_ref[...] = jnp.concatenate(three_parts(whitened), 0)
+    parts_ref[...] = jnp.concatenate(three_parts(whitened)[:2], 0)
 
 
 def reply_body(pixel_total, place_ref, parts_ref, rounded_ref, notes_ref, own_ref, low_ref, *refs):
@@ -191,7 +191,7 @@
     bands = []
     for centered in (lower, own_ref[...]):
         sums = rows_dot(parts, centered)
-        spatial = (sums[:ranks] + sums[ranks : 2 * ranks] + sums[2 * ranks :]).astype(jnp.bfloat16)
+        spatial = (sums[:ranks] + sums[ranks:]).astype(jnp.bfloat16)
         bands += [spatial[:, q * pixels : (q + 1) * pixels] for q in range(4)]
     stacked = jnp.concatenate(bands, 0)
     place = place_ref[0]
@@ -202,10 +202,12 @@
     def turned(order):
         return sum(((order >> t) & 1) << (bits - 1 - t) for t in range(bits))
 
-    def coefficients(held_ref, entry, owner):
-        projected = rows_dot(stacked, held_ref[entry])
-        codes = notes_ref[pl.ds(2 * (plane_start + owner) + 1, 1), :].astype(jnp.int32)
-        total = jnp.zeros((ranks, sources), jnp.float32)
+    def coefficients(weights, owners):
+        projected = rows_dot(stacked, weights)
+        codes = jnp.concatenate(
+            [notes_ref[pl.ds(2 * (plane_start + owner) + 1, 1), :] for owner in owners], 1
+        ).astype(jnp.int32)
+        total = jnp.zeros((ranks, codes.shape[1]), jnp.float32)
         for role in range(2):
             for quarter in range(4):
                 start = (role * 4 + quarter) * ranks
@@ -213,24 +215,26 @@
                 total = total + jnp.where(chosen, projected[start : start + ranks], 0.0)
         return total.astype(jnp.bfloat16)
 
-    first = 0
-    for held_ref in held_refs:
-        count = held_ref.shape[0]
-        if paired:
-            for entry in range(count):
-                offset = turned(first + entry)
-                owner = lax.bitwise_xor(place, jnp.int32(offset))
+    if paired:
+        listed = [(held_ref, entry) for held_ref in held_refs for entry in range(held_ref.shape[0])]
+        for first in range(0, tile_count, 2):
+            offsets = [turned(first), turned(first + 1)]
+            weights = jnp.concatenate([held_ref[entry] for held_ref, entry in listed[first : first + 2]], 0)
+            found = coefficients(weights, [lax.bitwise_xor(place, jnp.int32(offset)) for offset in offsets])
+            for i, offset in enumerate(offsets):
                 row = (offset % 2) * ranks
-                reply_refs[offset // 2][row : row + ranks, :] = coefficients(held_ref, entry, owner)
-        else:
+                reply_refs[offset // 2][row : row + ranks, :] = found[:, i * sources : (i + 1) * sources]
+    else:
+        first = 0
+        for held_ref in held_refs:
 
             def one_owner(entry, held_ref=held_ref, first=first):
                 owner = lax.bitwise_xor(place, turned(first + entry))
-                reply_refs[0][owner, 0:ranks, :] = coefficients(held_ref, entry, owner)
+                reply_refs[0][owner, 0:ranks, :] = coefficients(held_ref[entry], [owner])
                 reply_refs[0][owner, ranks:, :] = temporal_rounded
 
-            pl.loop(0, count)(one_owner)
-        first += count
+            pl.loop(0, held_ref.shape[0])(one_owner)
+            first += held_ref.shape[0]
     if paired:
         for reply_ref in reply_refs:
             reply_ref[2 * ranks :, :] = temporal_rounded
@@ -317,7 +321,7 @@
     ranks = patches * rank
     temporal, parts, rounded = vmem_call(
         patch_body,
-        [shape((patches, rank, frames), f32), shape((3 * ranks, frames), bf16), shape((ranks, frames), bf16)],
+        [shape((patches, rank, frames), f32), shape((2 * ranks, frames), bf16), shape((ranks, frames), bf16)],
         "patch_factors",
         6 * 10**9,
         1 << 20,

time: 40.6 us -> 40.3 us (level)
  transfers between devices with their start and end apart: 10 -> 10, of which waited for: 5 -> 5; matrix products, arithmetic and copies ran while one was open for 0% -> 0% of each run, Pallas kernels for 15% -> 16%
where the time goes in v5:
time: 40.3 us; the launch traced here: 40.1 us
  starting transfers between devices  17 us (42%)
  waiting for transfers between devices  13.8 us (34%)
  Pallas kernels  8.27 us (21%)
  between operations  0.75 us (2%)
    ppermute x3, starting transfers between devices, on_device(): held.append(lax.ppermute(everything, 'tile', route))  6.12 us
    ppermute x2, waiting for transfers between devices, from_behind(): return lax.ppermute(block, axis, route)  5.82 us
    ppermute x3, starting transfers between devices, on_device(): arrived.append(lax.ppermute(replies[offset], 'tile', route))  4.45 us
    all_to_all x1, waiting for transfers between devices, on_device(): notes = lax.all_to_all(notes, ('plane', 'tile'), 0, 0, tiled=True)  4.14 us
    all_to_all x1, starting transfers between devices, on_device(): notes = lax.all_to_all(notes, ('plane', 'tile'), 0, 0, tiled=True)  3.83 us
    pallas_call x1, Pallas kernels, on_device(): vmem_call(patch_body, [shape((patches, rank, frames), f32), shape((2 * ra...  3.74 us
    ppermute x2, starting transfers between devices, from_behind(): return lax.ppermute(block, axis, route)  2.57 us
    ppermute x3, waiting for transfers between devices, on_device(): arrived.append(lax.ppermute(replies[offset], 'tile', route))  2.53 us
  transfers between devices with their start and end apart: 10, of which 5 were waited for; matrix products, arithmetic and copies ran while one was open for 0% of the time, Pallas kernels for 16%

profile of v5, /device:TPU:0, one launch (start us, length us, event | category | flops | bytes accessed | tf_op | source)
XLA Modules:
  0.0 40.1 jit_solution(9206779165946053586)
XLA Ops:
  0.6 4.1 %collective-permute-start.2 = (bf16[1,128,256]{2,1,0:T(8,128)(2,1)}, bf16[1,128,256]{2,1,0:T(8,128)(2,1)S(1)}, u32[]{:S(2)}, u32[]{:S(2)}) collective-permute-start(bf16[1,128,256]{2,1,0:T(8,128)(2,1)} %refs_6_.1), channel_id=1, source_target_pairs={{0,4},{1,5},{2,6},{3,7},{4,0},{5,1},{6,2},{7,3},{8,12},{9,13},{10,... | collective-permute-start | bytes 196616 | tf_op jit(solution)/shard_map/ppermute | solution.py:317
  4.7 2.1 %frame_sums.1 = (f32[64,128]{1,0:T(8,128)}, bf16[1024,128]{1,0:T(8,128)(2,1)S(1)}, bf16[3072,128]{1,0:T(8,128)(2,1)S(1)}) custom-call(bf16[3072,128]{1,0:T(8,128)(2,1)} %bitcast.20, s32[1,128]{1,0:T(1,128)} %bitcast.22, s32[1,128]{1,0:T(1,128)} %block_ref.1), custom_call_target="tpu_custom_call" | custom-call | flops 786432 | bytes 786432 | tf_op jit(solution)/shard_map/frame_sums/pallas_call | solution.py:286
  6.8 0.0 copy-start
  6.8 3.8 %all-to-all-start = ((f32[32,2,128]{2,1,0:T(2,128)}), f32[32,2,128]{2,1,0:T(2,128)S(1)}, u32[]{:S(2)}, u32[]{:S(2)}) async-start(f32[32,2,128]{2,1,0:T(2,128)} %bitcast.2), calls=%async_computation | async-start | bytes 65536 | tf_op jit(solution)/shard_map/all_to_all | solution.py:304
  10.6 0.0 collective-permute-done.2.refs_7_
  10.7 0.0 copy-done
  10.7 1.8 %collective-permute-start.3 = (bf16[2,128,256]{2,1,0:T(8,128)(2,1)S(1)}, bf16[2,128,256]{2,1,0:T(8,128)(2,1)S(1)}, u32[]{:S(2)}, u32[]{:S(2)}) collective-permute-start(bf16[2,128,256]{2,1,0:T(8,128)(2,1)S(1)} %pad_maximum_fusion.1), channel_id=1, source_target_pairs={{0,2},{1,3},{2,0},{3,1},{4,6},{5,7},{6,4},{7,5},{8,10},{9,11},{10,... | collective-permute-start | bytes 393224 | tf_op jit(solution)/shard_map/ppermute | solution.py:317
  12.5 1.3 %collective-permute-start.1 = (bf16[1024,128]{1,0:T(8,128)(2,1)S(1)}, bf16[1024,128]{1,0:T(8,128)(2,1)S(1)}, u32[]{:S(2)}, u32[]{:S(2)}) collective-permute-start(bf16[1024,128]{1,0:T(8,128)(2,1)S(1)} %get-tuple-element.21), channel_id=1, source_target_pairs={{2,0},{3,1},{4,2},{5,3},{6,4},{7,5},{10,8},{11,9},{12,10},{13,11},... | collective-permute-start | bytes 786440 | tf_op jit(solution)/shard_map/ppermute | solution.py:14
  13.8 4.1 %all-to-all-done = f32[32,2,128]{2,1,0:T(2,128)S(1)} async-done(((f32[32,2,128]{2,1,0:T(2,128)}), f32[32,2,128]{2,1,0:T(2,128)S(1)}, u32[]{:S(2)}, u32[]{:S(2)}) %all-to-all-start) | async-done | bytes 32800 | tf_op jit(solution)/shard_map/all_to_all | solution.py:304
  18.0 0.4 %own_grams.1 = (f32[2,128,128]{2,1,0:T(8,128)S(1)}, bf16[1024,128]{1,0:T(8,128)(2,1)S(1)}) custom-call(f32[64,128]{1,0:T(8,128)S(1)} %bitcast.17, bf16[3072,128]{1,0:T(8,128)(2,1)S(1)} %get-tuple-element.15.refs_1_), custom_call_target="tpu_custom_call" | custom-call | flops 100663296 | bytes 786432 | tf_op jit(solution)/shard_map/own_grams/pallas_call | solution.py:306
  18.4 1.3 %collective-permute-start = (f32[2,128,128]{2,1,0:T(8,128)S(1)}, f32[2,128,128]{2,1,0:T(8,128)S(1)}, u32[]{:S(2)}, u32[]{:S(2)}) collective-permute-start(f32[2,128,128]{2,1,0:T(8,128)S(1)} %get-tuple-element.16.own_gram_ref), channel_id=1, source_target_pairs={{2,0},{3,1},{4,2},{5,3},{6,4},{7,5},{10,8},{11,9},{12,10},{13,11},... | collective-permute-start | bytes 393224 | tf_op jit(solution)/shard_map/ppermute | solution.py:14
  19.7 0.1 pad_add_fusion.refs_0_
  19.8 0.0 copy-start.1
  19.8 0.0 collective-permute-done.3.refs_8_
  19.8 0.2 collective-permute-start.4
  20.0 5.8 %collective-permute-done.low_gram_ref = f32[2,128,128]{2,1,0:T(8,128)S(1)} collective-permute-done((f32[2,128,128]{2,1,0:T(8,128)S(1)}, f32[2,128,128]{2,1,0:T(8,128)S(1)}, u32[]{:S(2)}, u32[]{:S(2)}) %collective-permute-start) | collective-permute-done | bytes 131104 | tf_op jit(solution)/shard_map/ppermute | solution.py:14
  25.8 0.0 copy-done.1
  25.8 3.7 %patch_factors.1 = (f32[2,32,128]{2,1,0:T(8,128)}, bf16[128,128]{1,0:T(8,128)(2,1)S(1)}, bf16[64,128]{1,0:T(8,128)(2,1)S(1)}) custom-call(f32[2,128,128]{2,1,0:T(8,128)S(1)} %get-tuple-element.16.own_gram_ref, f32[2,128,128]{2,1,0:T(8,128)S(1)} %collective-permute-done.low_gram_ref, f32[2,32,128]{2,1,0:T(8,128)S(1)} %bitcast.19), custom_call_target="tpu_custom_call" | custom-call | flops 6000000000 | bytes 1048576 | tf_op jit(solution)/shard_map/patch_factors/pallas_call | solution.py:322
  29.5 0.0 collective-permute-done.1.refs_5_
  29.5 0.0 collective-permute-done.4.refs_9_
  29.5 1.2 %coefficients.1 = (bf16[192,128]{1,0:T(8,128)(2,1)S(1)}, bf16[192,128]{1,0:T(8,128)(2,1)S(1)}, bf16[192,128]{1,0:T(8,128)(2,1)S(1)}, bf16[192,128]{1,0:T(8,128)(2,1)S(1)}) custom-call(s32[2]{0:T(128)S(1)} %pad_add_fusion.refs_0_, bf16[128,128]{1,0:T(8,128)(2,1)S(1)} %get-tuple-element.18.refs_1_, bf16[64,128]{1,0:T(8,128)(2,1)S(1)} %get-tuple-element.19.refs_2_, ...), custom_call_target="tpu_custom_call" | custom-call | flops 268435456 | bytes 2097152 | tf_op jit(solution)/shard_map/coefficients/pallas_call | solution.py:331
  30.8 0.9 %collective-permute-start.7 = (bf16[192,128]{1,0:T(8,128)(2,1)S(1)}, bf16[192,128]{1,0:T(8,128)(2,1)S(1)}, u32[]{:S(2)}, u32[]{:S(2)}) collective-permute-start(bf16[192,128]{1,0:T(8,128)(2,1)S(1)} %get-tuple-element.25), channel_id=1, source_target_pairs={{0,6},{1,7},{2,4},{3,5},{4,2},{5,3},{6,0},{7,1},{8,14},{9,15},{10,... | collective-permute-start | bytes 147464 | tf_op jit(solution)/shard_map/ppermute | solution.py:345
  31.7 1.3 %collective-permute-start.6 = (bf16[192,128]{1,0:T(8,128)(2,1)S(1)}, bf16[192,128]{1,0:T(8,128)(2,1)S(1)}, u32[]{:S(2)}, u32[]{:S(2)}) collective-permute-start(bf16[192,128]{1,0:T(8,128)(2,1)S(1)} %get-tuple-element.24), channel_id=1, source_target_pairs={{0,4},{1,5},{2,6},{3,7},{4,0},{5,1},{6,2},{7,3},{8,12},{9,13},{10,... | collective-permute-start | bytes 147464 | tf_op jit(solution)/shard_map/ppermute | solution.py:345
  33.0 2.2 %collective-permute-start.5 = (bf16[192,128]{1,0:T(8,128)(2,1)S(1)}, bf16[192,128]{1,0:T(8,128)(2,1)S(1)}, u32[]{:S(2)}, u32[]{:S(2)}) collective-permute-start(bf16[192,128]{1,0:T(8,128)(2,1)S(1)} %get-tuple-element.23), channel_id=1, source_target_pairs={{0,2},{1,3},{2,0},{3,1},{4,6},{5,7},{6,4},{7,5},{8,10},{9,11},{10,... | collective-permute-start | bytes 147464 | tf_op jit(solution)/shard_map/ppermute | solution.py:345
  35.2 1.6 %collective-permute-done.7.refs_3_ = bf16[192,128]{1,0:T(8,128)(2,1)S(1)} collective-permute-done((bf16[192,128]{1,0:T(8,128)(2,1)S(1)}, bf16[192,128]{1,0:T(8,128)(2,1)S(1)}, u32[]{:S(2)}, u32[]{:S(2)}) %collective-permute-start.7) | collective-permute-done | bytes 49184 | tf_op jit(solution)/shard_map/ppermute | solution.py:345
  36.8 0.9 %collective-permute-done.6.refs_2_ = bf16[192,128]{1,0:T(8,128)(2,1)S(1)} collective-permute-done((bf16[192,128]{1,0:T(8,128)(2,1)S(1)}, bf16[192,128]{1,0:T(8,128)(2,1)S(1)}, u32[]{:S(2)}, u32[]{:S(2)}) %collective-permute-start.6) | collective-permute-done | bytes 49184 | tf_op jit(solution)/shard_map/ppermute | solution.py:345
  37.7 0.0 collective-permute-done.5.refs_1_
  37.8 0.1 collective-permute-start.8
  37.9 1.3 %collective-permute-done.8.refs_4_ = bf16[4,128,128]{2,1,0:T(8,128)(2,1)S(1)} collective-permute-done((bf16[4,128,128]{2,1,0:T(8,128)(2,1)S(1)}, bf16[4,128,128]{2,1,0:T(8,128)(2,1)S(1)}, u32[]{:S(2)}, u32[]{:S(2)}) %collective-permute-start.8) | collective-permute-done | bytes 131104 | tf_op jit(solution)/shard_map/ppermute | solution.py:347
  39.2 0.9 %source_traces.1 = f32[128,128]{1,0:T(8,128)} custom-call(bf16[192,128]{1,0:T(8,128)(2,1)S(1)} %get-tuple-element.22.refs_0_, bf16[192,128]{1,0:T(8,128)(2,1)S(1)} %collective-permute-done.5.refs_1_, bf16[192,128]{1,0:T(8,128)(2,1)S(1)} %collective-permute-done.6.refs_2_, bf16[192,128]{1,0:T(8,128)(2,1)S(1)} %collective-permute-done.7.refs_3_, ...), custom_call_target="tpu_custom_call" | custom-call | flops 16777216 | bytes 524288 | tf_op jit(solution)/shard_map/source_traces/pallas_call | solution.py:348
  (7 shorter events, 0.1 us)
Async XLA Ops:
  0.6 10.0 %collective-permute-start.2 = (bf16[1,128,256]{2,1,0:T(8,128)(2,1)}, bf16[1,128,256]{2,1,0:T(8,128)(2,1)S(1)}, u32[]{:S(2)}, u32[]{:S(2)}) collective-permute-start(bf16[1,128,256]{2,1,0:T(8,128)(2,1)} %refs_6_.1), channel_id=1, source_target_pairs={{0,4},{1,5},{2,6},{3,7},{4,0},{5,1},{6,2},{7,3},{8,12},{9,13},{10,... | collective-permute-start | bytes 196616 | tf_op jit(solution)/shard_map/ppermute | solution.py:317
  6.8 3.9 %copy-start = (bf16[1,128,256]{2,1,0:T(8,128)(2,1)S(1)}, bf16[1,128,256]{2,1,0:T(8,128)(2,1)}, u32[]{:S(2)}) copy-start(bf16[1,128,256]{2,1,0:T(8,128)(2,1)} %refs_6_.1) | copy-start | bytes 196612
  6.8 11.2 %all-to-all-start = ((f32[32,2,128]{2,1,0:T(2,128)}), f32[32,2,128]{2,1,0:T(2,128)S(1)}, u32[]{:S(2)}, u32[]{:S(2)}) async-start(f32[32,2,128]{2,1,0:T(2,128)} %bitcast.2), calls=%async_computation | async-start | bytes 65536 | tf_op jit(solution)/shard_map/all_to_all | solution.py:304
  10.7 9.1 %collective-permute-start.3 = (bf16[2,128,256]{2,1,0:T(8,128)(2,1)S(1)}, bf16[2,128,256]{2,1,0:T(8,128)(2,1)S(1)}, u32[]{:S(2)}, u32[]{:S(2)}) collective-permute-start(bf16[2,128,256]{2,1,0:T(8,128)(2,1)S(1)} %pad_maximum_fusion.1), channel_id=1, source_target_pairs={{0,2},{1,3},{2,0},{3,1},{4,6},{5,7},{6,4},{7,5},{8,10},{9,11},{10,... | collective-permute-start | bytes 393224 | tf_op jit(solution)/shard_map/ppermute | solution.py:317
  12.5 17.0 %collective-permute-start.1 = (bf16[1024,128]{1,0:T(8,128)(2,1)S(1)}, bf16[1024,128]{1,0:T(8,128)(2,1)S(1)}, u32[]{:S(2)}, u32[]{:S(2)}) collective-permute-start(bf16[1024,128]{1,0:T(8,128)(2,1)S(1)} %get-tuple-element.21), channel_id=1, source_target_pairs={{2,0},{3,1},{4,2},{5,3},{6,4},{7,5},{10,8},{11,9},{12,10},{13,11},... | collective-permute-start | bytes 786440 | tf_op jit(solution)/shard_map/ppermute | solution.py:14
  18.4 7.4 %collective-permute-start = (f32[2,128,128]{2,1,0:T(8,128)S(1)}, f32[2,128,128]{2,1,0:T(8,128)S(1)}, u32[]{:S(2)}, u32[]{:S(2)}) collective-permute-start(f32[2,128,128]{2,1,0:T(8,128)S(1)} %get-tuple-element.16.own_gram_ref), channel_id=1, source_target_pairs={{2,0},{3,1},{4,2},{5,3},{6,4},{7,5},{10,8},{11,9},{12,10},{13,11},... | collective-permute-start | bytes 393224 | tf_op jit(solution)/shard_map/ppermute | solution.py:14
  19.8 6.0 %copy-start.1 = (f32[1,2,32,128]{3,2,1,0:T(8,128)S(1)}, f32[1,2,32,128]{3,2,1,0:T(8,128)}, u32[]{:S(2)}) copy-start(f32[1,2,32,128]{3,2,1,0:T(8,128)} %param.6) | copy-start | bytes 98308
  19.8 9.7 %collective-permute-start.4 = (bf16[4,128,256]{2,1,0:T(8,128)(2,1)S(1)}, bf16[4,128,256]{2,1,0:T(8,128)(2,1)S(1)}, u32[]{:S(2)}, u32[]{:S(2)}) collective-permute-start(bf16[4,128,256]{2,1,0:T(8,128)(2,1)S(1)} %pad_maximum_fusion), channel_id=1, source_target_pairs={{0,1},{1,0},{2,3},{3,2},{4,5},{5,4},{6,7},{7,6},{8,9},{9,8},{10,11... | collective-permute-start | bytes 786440 | tf_op jit(solution)/shard_map/ppermute | solution.py:317
  30.8 6.1 %collective-permute-start.7 = (bf16[192,128]{1,0:T(8,128)(2,1)S(1)}, bf16[192,128]{1,0:T(8,128)(2,1)S(1)}, u32[]{:S(2)}, u32[]{:S(2)}) collective-permute-start(bf16[192,128]{1,0:T(8,128)(2,1)S(1)} %get-tuple-element.25), channel_id=1, source_target_pairs={{0,6},{1,7},{2,4},{3,5},{4,2},{5,3},{6,0},{7,1},{8,14},{9,15},{10,... | collective-permute-start | bytes 147464 | tf_op jit(solution)/shard_map/ppermute | solution.py:345
  31.7 6.0 %collective-permute-start.6 = (bf16[192,128]{1,0:T(8,128)(2,1)S(1)}, bf16[192,128]{1,0:T(8,128)(2,1)S(1)}, u32[]{:S(2)}, u32[]{:S(2)}) collective-permute-start(bf16[192,128]{1,0:T(8,128)(2,1)S(1)} %get-tuple-element.24), channel_id=1, source_target_pairs={{0,4},{1,5},{2,6},{3,7},{4,0},{5,1},{6,2},{7,3},{8,12},{9,13},{10,... | collective-permute-start | bytes 147464 | tf_op jit(solution)/shard_map/ppermute | solution.py:345
  33.0 4.7 %collective-permute-start.5 = (bf16[192,128]{1,0:T(8,128)(2,1)S(1)}, bf16[192,128]{1,0:T(8,128)(2,1)S(1)}, u32[]{:S(2)}, u32[]{:S(2)}) collective-permute-start(bf16[192,128]{1,0:T(8,128)(2,1)S(1)} %get-tuple-element.23), channel_id=1, source_target_pairs={{0,2},{1,3},{2,0},{3,1},{4,6},{5,7},{6,4},{7,5},{8,10},{9,11},{10,... | collective-permute-start | bytes 147464 | tf_op jit(solution)/shard_map/ppermute | solution.py:345
  37.8 1.4 %collective-permute-start.8 = (bf16[4,128,128]{2,1,0:T(8,128)(2,1)S(1)}, bf16[4,128,128]{2,1,0:T(8,128)(2,1)S(1)}, u32[]{:S(2)}, u32[]{:S(2)}) collective-permute-start(bf16[4,128,128]{2,1,0:T(8,128)(2,1)S(1)} %pad_maximum_fusion.2), channel_id=1, source_target_pairs={{0,1},{1,0},{2,3},{3,2},{4,5},{5,4},{6,7},{7,6},{8,9},{9,8},{10,11... | collective-permute-start | bytes 393224 | tf_op jit(solution)/shard_map/ppermute | solution.py:347

commit v6 on v5

--- a/solution.py
+++ b/solution.py
@@ -240,8 +240,9 @@
             reply_ref[2 * ranks :, :] = temporal_rounded
 
 
-def paired_trace_body(*refs):
-    own_refs, mate_ref, traces_ref = refs[:-2], refs[-2], refs[-1]
+def paired_trace_body(near_temporal_ref, *refs):
+    own_refs, mate_ref, temporal_ref, traces_ref = refs[:-3], refs[-3], refs[-2], refs[-1]
+    temporal_ref[...] = near_temporal_ref[...]
     ranks = own_refs[0].shape[0] // 3
     coefficient = [r[0:ranks] for r in own_refs] + [mate_ref[i, 0:ranks] for i in range(len(own_refs))]
     temporal = [r[2 * ranks :] for r in own_refs] + [mate_ref[i, ranks:] for i in range(len(own_refs))]
@@ -345,9 +346,13 @@
             arrived.append(lax.ppermute(replies[offset], "tile", route))
         handed = jnp.stack([block[ranks:] for block in arrived])
         mate = lax.ppermute(handed, "tile", [(i, i ^ 1) for i in range(tile_count)])
-        traces = vmem_call(
-            paired_trace_body, shape((sources, frames), f32), "source_traces", flops, 1 << 19
-        )(*arrived, mate)
+        temporal, traces = vmem_call(
+            paired_trace_body,
+            [shape(temporal.shape, f32), shape((sources, frames), f32)],
+            "source_traces",
+            flops,
+            1 << 19,
+        )(temporal, *arrived, mate)
     else:
         answers = lax.all_to_all(replies[0], "tile", 0, 0, tiled=True)
         traces = vmem_call(trace_body, shape((sources, frames), f32), "source_traces", flops, 2 * answers.size)(answers)

time: 40.3 us -> 39.7 us (0.985)
  Pallas kernels: 8.27 us -> 7.67 us
    pallas_call x1, Pallas kernels: 3.74 us -> 3.13 us  [on_device(): vmem_call(patch_body, [shape((patches, rank, frames), f32), shape((2 * ra...]
  transfers between devices with their start and end apart: 10 -> 10, of which waited for: 5 -> 5; matrix products, arithmetic and copies ran while one was open for 0% -> 0% of each run, Pallas kernels for 16% -> 14%
where the time goes in v6:
time: 39.7 us; the launch traced here: 39.5 us
  starting transfers between devices  17 us (43%)
  waiting for transfers between devices  13.8 us (35%)
  Pallas kernels  7.67 us (19%)
  between operations  0.76 us (2%)
    ppermute x3, starting transfers between devices, on_device(): held.append(lax.ppermute(everything, 'tile', route))  6.12 us
    ppermute x2, waiting for transfers between devices, from_behind(): return lax.ppermute(block, axis, route)  5.82 us
    ppermute x3, starting transfers between devices, on_device(): arrived.append(lax.ppermute(replies[offset], 'tile', route))  4.45 us
    all_to_all x1, waiting for transfers between devices, on_device(): notes = lax.all_to_all(notes, ('plane', 'tile'), 0, 0, tiled=True)  4.14 us
    all_to_all x1, starting transfers between devices, on_device(): notes = lax.all_to_all(notes, ('plane', 'tile'), 0, 0, tiled=True)  3.83 us
    pallas_call x1, Pallas kernels, on_device(): vmem_call(patch_body, [shape((patches, rank, frames), f32), shape((2 * ra...  3.13 us
    ppermute x2, starting transfers between devices, from_behind(): return lax.ppermute(block, axis, route)  2.57 us
    ppermute x3, waiting for transfers between devices, on_device(): arrived.append(lax.ppermute(replies[offset], 'tile', route))  2.53 us
  transfers between devices with their start and end apart: 10, of which 5 were waited for; matrix products, arithmetic and copies ran while one was open for 0% of the time, Pallas kernels for 14%

profile of v6, /device:TPU:0, one launch (start us, length us, event | category | flops | bytes accessed | tf_op | source)
XLA Modules:
  0.0 39.5 jit_solution(9510244572357473138)
XLA Ops:
  0.6 4.1 %collective-permute-start.2 = (bf16[1,128,256]{2,1,0:T(8,128)(2,1)}, bf16[1,128,256]{2,1,0:T(8,128)(2,1)S(1)}, u32[]{:S(2)}, u32[]{:S(2)}) collective-permute-start(bf16[1,128,256]{2,1,0:T(8,128)(2,1)} %refs_6_.1), channel_id=1, source_target_pairs={{0,4},{1,5},{2,6},{3,7},{4,0},{5,1},{6,2},{7,3},{8,12},{9,13},{10,... | collective-permute-start | bytes 196616 | tf_op jit(solution)/shard_map/ppermute | solution.py:318
  4.7 2.1 %frame_sums.1 = (f32[64,128]{1,0:T(8,128)}, bf16[1024,128]{1,0:T(8,128)(2,1)S(1)}, bf16[3072,128]{1,0:T(8,128)(2,1)S(1)}) custom-call(bf16[3072,128]{1,0:T(8,128)(2,1)} %bitcast.20, s32[1,128]{1,0:T(1,128)} %bitcast.21, s32[1,128]{1,0:T(1,128)} %block_ref.1), custom_call_target="tpu_custom_call" | custom-call | flops 786432 | bytes 786432 | tf_op jit(solution)/shard_map/frame_sums/pallas_call | solution.py:287
  6.8 0.0 copy-start
  6.8 3.8 %all-to-all-start = ((f32[32,2,128]{2,1,0:T(2,128)}), f32[32,2,128]{2,1,0:T(2,128)S(1)}, u32[]{:S(2)}, u32[]{:S(2)}) async-start(f32[32,2,128]{2,1,0:T(2,128)} %bitcast.2), calls=%async_computation | async-start | bytes 65536 | tf_op jit(solution)/shard_map/all_to_all | solution.py:305
  10.6 0.0 collective-permute-done.2.refs_7_
  10.7 0.0 copy-done
  10.7 1.8 %collective-permute-start.3 = (bf16[2,128,256]{2,1,0:T(8,128)(2,1)S(1)}, bf16[2,128,256]{2,1,0:T(8,128)(2,1)S(1)}, u32[]{:S(2)}, u32[]{:S(2)}) collective-permute-start(bf16[2,128,256]{2,1,0:T(8,128)(2,1)S(1)} %pad_maximum_fusion.1), channel_id=1, source_target_pairs={{0,2},{1,3},{2,0},{3,1},{4,6},{5,7},{6,4},{7,5},{8,10},{9,11},{10,... | collective-permute-start | bytes 393224 | tf_op jit(solution)/shard_map/ppermute | solution.py:318
  12.5 1.3 %collective-permute-start.1 = (bf16[1024,128]{1,0:T(8,128)(2,1)S(1)}, bf16[1024,128]{1,0:T(8,128)(2,1)S(1)}, u32[]{:S(2)}, u32[]{:S(2)}) collective-permute-start(bf16[1024,128]{1,0:T(8,128)(2,1)S(1)} %get-tuple-element.23), channel_id=1, source_target_pairs={{2,0},{3,1},{4,2},{5,3},{6,4},{7,5},{10,8},{11,9},{12,10},{13,11},... | collective-permute-start | bytes 786440 | tf_op jit(solution)/shard_map/ppermute | solution.py:14
  13.8 4.1 %all-to-all-done = f32[32,2,128]{2,1,0:T(2,128)S(1)} async-done(((f32[32,2,128]{2,1,0:T(2,128)}), f32[32,2,128]{2,1,0:T(2,128)S(1)}, u32[]{:S(2)}, u32[]{:S(2)}) %all-to-all-start) | async-done | bytes 32800 | tf_op jit(solution)/shard_map/all_to_all | solution.py:305
  18.0 0.4 %own_grams.1 = (f32[2,128,128]{2,1,0:T(8,128)S(1)}, bf16[1024,128]{1,0:T(8,128)(2,1)S(1)}) custom-call(f32[64,128]{1,0:T(8,128)S(1)} %bitcast.17, bf16[3072,128]{1,0:T(8,128)(2,1)S(1)} %get-tuple-element.17.refs_1_), custom_call_target="tpu_custom_call" | custom-call | flops 100663296 | bytes 786432 | tf_op jit(solution)/shard_map/own_grams/pallas_call | solution.py:307
  18.4 1.3 %collective-permute-start = (f32[2,128,128]{2,1,0:T(8,128)S(1)}, f32[2,128,128]{2,1,0:T(8,128)S(1)}, u32[]{:S(2)}, u32[]{:S(2)}) collective-permute-start(f32[2,128,128]{2,1,0:T(8,128)S(1)} %get-tuple-element.18.own_gram_ref), channel_id=1, source_target_pairs={{2,0},{3,1},{4,2},{5,3},{6,4},{7,5},{10,8},{11,9},{12,10},{13,11},... | collective-permute-start | bytes 393224 | tf_op jit(solution)/shard_map/ppermute | solution.py:14
  19.7 0.1 pad_add_fusion.refs_0_
  19.8 0.0 copy-start.1
  19.8 0.0 collective-permute-done.3.refs_8_
  19.8 0.2 collective-permute-start.4
  20.0 5.8 %collective-permute-done.low_gram_ref = f32[2,128,128]{2,1,0:T(8,128)S(1)} collective-permute-done((f32[2,128,128]{2,1,0:T(8,128)S(1)}, f32[2,128,128]{2,1,0:T(8,128)S(1)}, u32[]{:S(2)}, u32[]{:S(2)}) %collective-permute-start) | collective-permute-done | bytes 131104 | tf_op jit(solution)/shard_map/ppermute | solution.py:14
  25.8 0.0 copy-done.1
  25.8 3.1 %patch_factors.1 = (f32[2,32,128]{2,1,0:T(8,128)S(1)}, bf16[128,128]{1,0:T(8,128)(2,1)S(1)}, bf16[64,128]{1,0:T(8,128)(2,1)S(1)}) custom-call(f32[2,128,128]{2,1,0:T(8,128)S(1)} %get-tuple-element.18.own_gram_ref, f32[2,128,128]{2,1,0:T(8,128)S(1)} %collective-permute-done.low_gram_ref, f32[2,32,128]{2,1,0:T(8,128)S(1)} %bitcast.19), custom_call_target="tpu_custom_call" | custom-call | flops 6000000000 | bytes 1048576 | tf_op jit(solution)/shard_map/patch_factors/pallas_call | solution.py:323
  28.9 0.0 collective-permute-done.1.refs_5_
  28.9 0.0 collective-permute-done.4.refs_9_
  29.0 1.2 %coefficients.1 = (bf16[192,128]{1,0:T(8,128)(2,1)S(1)}, bf16[192,128]{1,0:T(8,128)(2,1)S(1)}, bf16[192,128]{1,0:T(8,128)(2,1)S(1)}, bf16[192,128]{1,0:T(8,128)(2,1)S(1)}) custom-call(s32[2]{0:T(128)S(1)} %pad_add_fusion.refs_0_, bf16[128,128]{1,0:T(8,128)(2,1)S(1)} %get-tuple-element.20.refs_1_, bf16[64,128]{1,0:T(8,128)(2,1)S(1)} %get-tuple-element.21.refs_2_, ...), custom_call_target="tpu_custom_call" | custom-call | flops 268435456 | bytes 2097152 | tf_op jit(solution)/shard_map/coefficients/pallas_call | solution.py:332
  30.2 1.0 %collective-permute-start.7 = (bf16[192,128]{1,0:T(8,128)(2,1)S(1)}, bf16[192,128]{1,0:T(8,128)(2,1)S(1)}, u32[]{:S(2)}, u32[]{:S(2)}) collective-permute-start(bf16[192,128]{1,0:T(8,128)(2,1)S(1)} %get-tuple-element.27), channel_id=1, source_target_pairs={{0,6},{1,7},{2,4},{3,5},{4,2},{5,3},{6,0},{7,1},{8,14},{9,15},{10,... | collective-permute-start | bytes 147464 | tf_op jit(solution)/shard_map/ppermute | solution.py:346
  31.1 1.3 %collective-permute-start.6 = (bf16[192,128]{1,0:T(8,128)(2,1)S(1)}, bf16[192,128]{1,0:T(8,128)(2,1)S(1)}, u32[]{:S(2)}, u32[]{:S(2)}) collective-permute-start(bf16[192,128]{1,0:T(8,128)(2,1)S(1)} %get-tuple-element.26), channel_id=1, source_target_pairs={{0,4},{1,5},{2,6},{3,7},{4,0},{5,1},{6,2},{7,3},{8,12},{9,13},{10,... | collective-permute-start | bytes 147464 | tf_op jit(solution)/shard_map/ppermute | solution.py:346
  32.4 2.2 %collective-permute-start.5 = (bf16[192,128]{1,0:T(8,128)(2,1)S(1)}, bf16[192,128]{1,0:T(8,128)(2,1)S(1)}, u32[]{:S(2)}, u32[]{:S(2)}) collective-permute-start(bf16[192,128]{1,0:T(8,128)(2,1)S(1)} %get-tuple-element.25), channel_id=1, source_target_pairs={{0,2},{1,3},{2,0},{3,1},{4,6},{5,7},{6,4},{7,5},{8,10},{9,11},{10,... | collective-permute-start | bytes 147464 | tf_op jit(solution)/shard_map/ppermute | solution.py:346
  34.6 1.6 %collective-permute-done.7.refs_3_ = bf16[192,128]{1,0:T(8,128)(2,1)S(1)} collective-permute-done((bf16[192,128]{1,0:T(8,128)(2,1)S(1)}, bf16[192,128]{1,0:T(8,128)(2,1)S(1)}, u32[]{:S(2)}, u32[]{:S(2)}) %collective-permute-start.7) | collective-permute-done | bytes 49184 | tf_op jit(solution)/shard_map/ppermute | solution.py:346
  36.2 0.9 %collective-permute-done.6.refs_2_ = bf16[192,128]{1,0:T(8,128)(2,1)S(1)} collective-permute-done((bf16[192,128]{1,0:T(8,128)(2,1)S(1)}, bf16[192,128]{1,0:T(8,128)(2,1)S(1)}, u32[]{:S(2)}, u32[]{:S(2)}) %collective-permute-start.6) | collective-permute-done | bytes 49184 | tf_op jit(solution)/shard_map/ppermute | solution.py:346
  37.2 0.0 collective-permute-done.5.refs_1_
  37.2 0.1 collective-permute-start.8
  37.3 1.3 %collective-permute-done.8.refs_4_ = bf16[4,128,128]{2,1,0:T(8,128)(2,1)S(1)} collective-permute-done((bf16[4,128,128]{2,1,0:T(8,128)(2,1)S(1)}, bf16[4,128,128]{2,1,0:T(8,128)(2,1)S(1)}, u32[]{:S(2)}, u32[]{:S(2)}) %collective-permute-start.8) | collective-permute-done | bytes 131104 | tf_op jit(solution)/shard_map/ppermute | solution.py:348
  38.6 0.9 %source_traces.1 = (f32[2,32,128]{2,1,0:T(8,128)}, f32[128,128]{1,0:T(8,128)}) custom-call(f32[2,32,128]{2,1,0:T(8,128)S(1)} %get-tuple-element.19.near_temporal_ref, bf16[192,128]{1,0:T(8,128)(2,1)S(1)} %get-tuple-element.24.refs_0_, bf16[192,128]{1,0:T(8,128)(2,1)S(1)} %collective-permute-done.5.refs_1_, ...), custom_call_target="tpu_custom_call" | custom-call | flops 16777216 | bytes 524288 | tf_op jit(solution)/shard_map/source_traces/pallas_call | solution.py:349
  (7 shorter events, 0.1 us)
Async XLA Ops:
  0.6 10.0 %collective-permute-start.2 = (bf16[1,128,256]{2,1,0:T(8,128)(2,1)}, bf16[1,128,256]{2,1,0:T(8,128)(2,1)S(1)}, u32[]{:S(2)}, u32[]{:S(2)}) collective-permute-start(bf16[1,128,256]{2,1,0:T(8,128)(2,1)} %refs_6_.1), channel_id=1, source_target_pairs={{0,4},{1,5},{2,6},{3,7},{4,0},{5,1},{6,2},{7,3},{8,12},{9,13},{10,... | collective-permute-start | bytes 196616 | tf_op jit(solution)/shard_map/ppermute | solution.py:318
  6.8 3.9 %copy-start = (bf16[1,128,256]{2,1,0:T(8,128)(2,1)S(1)}, bf16[1,128,256]{2,1,0:T(8,128)(2,1)}, u32[]{:S(2)}) copy-start(bf16[1,128,256]{2,1,0:T(8,128)(2,1)} %refs_6_.1) | copy-start | bytes 196612
  6.8 11.2 %all-to-all-start = ((f32[32,2,128]{2,1,0:T(2,128)}), f32[32,2,128]{2,1,0:T(2,128)S(1)}, u32[]{:S(2)}, u32[]{:S(2)}) async-start(f32[32,2,128]{2,1,0:T(2,128)} %bitcast.2), calls=%async_computation | async-start | bytes 65536 | tf_op jit(solution)/shard_map/all_to_all | solution.py:305
  10.7 9.1 %collective-permute-start.3 = (bf16[2,128,256]{2,1,0:T(8,128)(2,1)S(1)}, bf16[2,128,256]{2,1,0:T(8,128)(2,1)S(1)}, u32[]{:S(2)}, u32[]{:S(2)}) collective-permute-start(bf16[2,128,256]{2,1,0:T(8,128)(2,1)S(1)} %pad_maximum_fusion.1), channel_id=1, source_target_pairs={{0,2},{1,3},{2,0},{3,1},{4,6},{5,7},{6,4},{7,5},{8,10},{9,11},{10,... | collective-permute-start | bytes 393224 | tf_op jit(solution)/shard_map/ppermute | solution.py:318
  12.5 16.4 %collective-permute-start.1 = (bf16[1024,128]{1,0:T(8,128)(2,1)S(1)}, bf16[1024,128]{1,0:T(8,128)(2,1)S(1)}, u32[]{:S(2)}, u32[]{:S(2)}) collective-permute-start(bf16[1024,128]{1,0:T(8,128)(2,1)S(1)} %get-tuple-element.23), channel_id=1, source_target_pairs={{2,0},{3,1},{4,2},{5,3},{6,4},{7,5},{10,8},{11,9},{12,10},{13,11},... | collective-permute-start | bytes 786440 | tf_op jit(solution)/shard_map/ppermute | solution.py:14
  18.4 7.4 %collective-permute-start = (f32[2,128,128]{2,1,0:T(8,128)S(1)}, f32[2,128,128]{2,1,0:T(8,128)S(1)}, u32[]{:S(2)}, u32[]{:S(2)}) collective-permute-start(f32[2,128,128]{2,1,0:T(8,128)S(1)} %get-tuple-element.18.own_gram_ref), channel_id=1, source_target_pairs={{2,0},{3,1},{4,2},{5,3},{6,4},{7,5},{10,8},{11,9},{12,10},{13,11},... | collective-permute-start | bytes 393224 | tf_op jit(solution)/shard_map/ppermute | solution.py:14
  19.8 6.0 %copy-start.1 = (f32[1,2,32,128]{3,2,1,0:T(8,128)S(1)}, f32[1,2,32,128]{3,2,1,0:T(8,128)}, u32[]{:S(2)}) copy-start(f32[1,2,32,128]{3,2,1,0:T(8,128)} %param.6) | copy-start | bytes 98308
  19.8 9.1 %collective-permute-start.4 = (bf16[4,128,256]{2,1,0:T(8,128)(2,1)S(1)}, bf16[4,128,256]{2,1,0:T(8,128)(2,1)S(1)}, u32[]{:S(2)}, u32[]{:S(2)}) collective-permute-start(bf16[4,128,256]{2,1,0:T(8,128)(2,1)S(1)} %pad_maximum_fusion), channel_id=1, source_target_pairs={{0,1},{1,0},{2,3},{3,2},{4,5},{5,4},{6,7},{7,6},{8,9},{9,8},{10,11... | collective-permute-start | bytes 786440 | tf_op jit(solution)/shard_map/ppermute | solution.py:318
  30.2 6.1 %collective-permute-start.7 = (bf16[192,128]{1,0:T(8,128)(2,1)S(1)}, bf16[192,128]{1,0:T(8,128)(2,1)S(1)}, u32[]{:S(2)}, u32[]{:S(2)}) collective-permute-start(bf16[192,128]{1,0:T(8,128)(2,1)S(1)} %get-tuple-element.27), channel_id=1, source_target_pairs={{0,6},{1,7},{2,4},{3,5},{4,2},{5,3},{6,0},{7,1},{8,14},{9,15},{10,... | collective-permute-start | bytes 147464 | tf_op jit(solution)/shard_map/ppermute | solution.py:346
  31.1 6.0 %collective-permute-start.6 = (bf16[192,128]{1,0:T(8,128)(2,1)S(1)}, bf16[192,128]{1,0:T(8,128)(2,1)S(1)}, u32[]{:S(2)}, u32[]{:S(2)}) collective-permute-start(bf16[192,128]{1,0:T(8,128)(2,1)S(1)} %get-tuple-element.26), channel_id=1, source_target_pairs={{0,4},{1,5},{2,6},{3,7},{4,0},{5,1},{6,2},{7,3},{8,12},{9,13},{10,... | collective-permute-start | bytes 147464 | tf_op jit(solution)/shard_map/ppermute | solution.py:346
  32.4 4.7 %collective-permute-start.5 = (bf16[192,128]{1,0:T(8,128)(2,1)S(1)}, bf16[192,128]{1,0:T(8,128)(2,1)S(1)}, u32[]{:S(2)}, u32[]{:S(2)}) collective-permute-start(bf16[192,128]{1,0:T(8,128)(2,1)S(1)} %get-tuple-element.25), channel_id=1, source_target_pairs={{0,2},{1,3},{2,0},{3,1},{4,6},{5,7},{6,4},{7,5},{8,10},{9,11},{10,... | collective-permute-start | bytes 147464 | tf_op jit(solution)/shard_map/ppermute | solution.py:346
  37.2 1.4 %collective-permute-start.8 = (bf16[4,128,128]{2,1,0:T(8,128)(2,1)S(1)}, bf16[4,128,128]{2,1,0:T(8,128)(2,1)S(1)}, u32[]{:S(2)}, u32[]{:S(2)}) collective-permute-start(bf16[4,128,128]{2,1,0:T(8,128)(2,1)S(1)} %pad_maximum_fusion.2), channel_id=1, source_target_pairs={{0,1},{1,0},{2,3},{3,2},{4,5},{5,4},{6,7},{7,6},{8,9},{9,8},{10,11... | collective-permute-start | bytes 393224 | tf_op jit(solution)/shard_map/ppermute | solution.py:348

commit v7 on v6

--- a/solution.py
+++ b/solution.py
@@ -151,7 +151,7 @@
 def patch_body(own_gram_ref, low_gram_ref, start_ref, temporal_ref, parts_ref, rounded_ref):
     patches = start_ref.shape[0]
     grams = [
-        jnp.concatenate(three_parts(own_gram_ref[p] + low_gram_ref[p]), 1) for p in range(patches)
+        jnp.concatenate(three_parts(own_gram_ref[p] + low_gram_ref[p]), 0) for p in range(patches)
     ]
     rank, frames = start_ref.shape[1], start_ref.shape[2]
     temporal = [start_ref[p] for p in range(patches)]
@@ -160,8 +160,8 @@
         rounded = [t.astype(jnp.bfloat16) for t in temporal]
         moved, inner = [], []
         for narrow, gram in zip(rounded, grams):
-            terms = jnp.dot(narrow, gram, preferred_element_type=jnp.float32)
-            image = terms[:, :frames] + terms[:, frames : 2 * frames] + terms[:, 2 * frames :]
+            repeated = jnp.concatenate([narrow] * 3, 1)
+            image = jnp.dot(repeated, gram, preferred_element_type=jnp.float32)
             terms = rows_dot(jnp.concatenate(three_parts(image), 0), narrow)
             moved.append(image)
             inner.append(terms[:rank] + terms[rank : 2 * rank] + terms[2 * rank :])
@@ -240,13 +240,20 @@
             reply_ref[2 * ranks :, :] = temporal_rounded
 
 
-def paired_trace_body(near_temporal_ref, *refs):
-    own_refs, mate_ref, temporal_ref, traces_ref = refs[:-3], refs[-3], refs[-2], refs[-1]
+def direct_trace_body(*refs):
+    own_refs, traces_ref = refs[:-1], refs[-1]
+    ranks = own_refs[0].shape[0] // 3
+    coefficient = jnp.concatenate([r[0:ranks] for r in own_refs], 0)
+    temporal = jnp.concatenate([r[2 * ranks :] for r in own_refs], 0)
+    traces_ref[...] = columns_dot(coefficient, temporal)
+
+
+def mate_trace_body(near_temporal_ref, direct_ref, mate_ref, temporal_ref, traces_ref):
     temporal_ref[...] = near_temporal_ref[...]
-    ranks = own_refs[0].shape[0] // 3
-    coefficient = [r[0:ranks] for r in own_refs] + [mate_ref[i, 0:ranks] for i in range(len(own_refs))]
-    temporal = [r[2 * ranks :] for r in own_refs] + [mate_ref[i, ranks:] for i in range(len(own_refs))]
-    traces_ref[...] = 0.25 * columns_dot(jnp.concatenate(coefficient, 0), jnp.concatenate(temporal, 0))
+    count, ranks = mate_ref.shape[0], mate_ref.shape[1] // 2
+    coefficient = jnp.concatenate([mate_ref[i, 0:ranks] for i in range(count)], 0)
+    temporal = jnp.concatenate([mate_ref[i, ranks:] for i in range(count)], 0)
+    traces_ref[...] = 0.25 * (direct_ref[...] + columns_dot(coefficient, temporal))
 
 
 def trace_body(reply_ref, traces_ref):
@@ -346,13 +353,16 @@
             arrived.append(lax.ppermute(replies[offset], "tile", route))
         handed = jnp.stack([block[ranks:] for block in arrived])
         mate = lax.ppermute(handed, "tile", [(i, i ^ 1) for i in range(tile_count)])
+        direct = vmem_call(
+            direct_trace_body, shape((sources, frames), f32), "direct_traces", flops // 2, 1 << 18
+        )(*arrived)
         temporal, traces = vmem_call(
-            paired_trace_body,
+            mate_trace_body,
             [shape(temporal.shape, f32), shape((sources, frames), f32)],
             "source_traces",
-            flops,
-            1 << 19,
-        )(temporal, *arrived, mate)
+            flops // 2,
+            1 << 18,
+        )(temporal, direct, mate)
     else:
         answers = lax.all_to_all(replies[0], "tile", 0, 0, tiled=True)
         traces = vmem_call(trace_body, shape((sources, frames), f32), "source_traces", flops, 2 * answers.size)(answers)

time: 39.7 us -> 39.7 us (level)
    pallas_call x1 -> x2, Pallas kernels: 0.86 us -> 1.03 us  [the longest x1 0.83 us: on_device(): vmem_call(mate_trace_body, [shape(temporal.shape, f32), shape((sources, f...]
  transfers between devices with their start and end apart: 10 -> 10, of which waited for: 5 -> 5; matrix products, arithmetic and copies ran while one was open for 0% -> 0% of each run, Pallas kernels for 14% -> 15%
where the time goes in v7:
time: 39.7 us; the launch traced here: 39.4 us
  starting transfers between devices  17 us (43%)
  waiting for transfers between devices  13.6 us (34%)
  Pallas kernels  7.84 us (20%)
  between operations  0.76 us (2%)
    ppermute x3, starting transfers between devices, on_device(): held.append(lax.ppermute(everything, 'tile', route))  6.12 us
    ppermute x2, waiting for transfers between devices, from_behind(): return lax.ppermute(block, axis, route)  5.82 us
    ppermute x3, starting transfers between devices, on_device(): arrived.append(lax.ppermute(replies[offset], 'tile', route))  4.45 us
    all_to_all x1, waiting for transfers between devices, on_device(): notes = lax.all_to_all(notes, ('plane', 'tile'), 0, 0, tiled=True)  4.14 us
    all_to_all x1, starting transfers between devices, on_device(): notes = lax.all_to_all(notes, ('plane', 'tile'), 0, 0, tiled=True)  3.83 us
    pallas_call x1, Pallas kernels, on_device(): vmem_call(patch_body, [shape((patches, rank, frames), f32), shape((2 * ra...  3.14 us
    ppermute x2, starting transfers between devices, from_behind(): return lax.ppermute(block, axis, route)  2.57 us
    ppermute x3, waiting for transfers between devices, on_device(): arrived.append(lax.ppermute(replies[offset], 'tile', route))  2.52 us
  transfers between devices with their start and end apart: 10, of which 5 were waited for; matrix products, arithmetic and copies ran while one was open for 0% of the time, Pallas kernels for 15%

profile of v7, /device:TPU:0, one launch (start us, length us, event | category | flops | bytes accessed | tf_op | source)
XLA Modules:
  0.0 39.4 jit_solution(12482839732245582281)
XLA Ops:
  0.6 4.1 %collective-permute-start.2 = (bf16[1,128,256]{2,1,0:T(8,128)(2,1)}, bf16[1,128,256]{2,1,0:T(8,128)(2,1)S(1)}, u32[]{:S(2)}, u32[]{:S(2)}) collective-permute-start(bf16[1,128,256]{2,1,0:T(8,128)(2,1)} %refs_6_.1), channel_id=1, source_target_pairs={{0,4},{1,5},{2,6},{3,7},{4,0},{5,1},{6,2},{7,3},{8,12},{9,13},{10,... | collective-permute-start | bytes 196616 | tf_op jit(solution)/shard_map/ppermute | solution.py:325
  4.7 2.1 %frame_sums.1 = (f32[64,128]{1,0:T(8,128)}, bf16[1024,128]{1,0:T(8,128)(2,1)S(1)}, bf16[3072,128]{1,0:T(8,128)(2,1)S(1)}) custom-call(bf16[3072,128]{1,0:T(8,128)(2,1)} %bitcast.20, s32[1,128]{1,0:T(1,128)} %bitcast.21, s32[1,128]{1,0:T(1,128)} %block_ref.1), custom_call_target="tpu_custom_call" | custom-call | flops 786432 | bytes 786432 | tf_op jit(solution)/shard_map/frame_sums/pallas_call | solution.py:294
  6.8 0.0 copy-start
  6.8 3.8 %all-to-all-start = ((f32[32,2,128]{2,1,0:T(2,128)}), f32[32,2,128]{2,1,0:T(2,128)S(1)}, u32[]{:S(2)}, u32[]{:S(2)}) async-start(f32[32,2,128]{2,1,0:T(2,128)} %bitcast.2), calls=%async_computation | async-start | bytes 65536 | tf_op jit(solution)/shard_map/all_to_all | solution.py:312
  10.6 0.0 collective-permute-done.2.refs_7_
  10.7 0.0 copy-done
  10.7 1.8 %collective-permute-start.3 = (bf16[2,128,256]{2,1,0:T(8,128)(2,1)S(1)}, bf16[2,128,256]{2,1,0:T(8,128)(2,1)S(1)}, u32[]{:S(2)}, u32[]{:S(2)}) collective-permute-start(bf16[2,128,256]{2,1,0:T(8,128)(2,1)S(1)} %pad_maximum_fusion.1), channel_id=1, source_target_pairs={{0,2},{1,3},{2,0},{3,1},{4,6},{5,7},{6,4},{7,5},{8,10},{9,11},{10,... | collective-permute-start | bytes 393224 | tf_op jit(solution)/shard_map/ppermute | solution.py:325
  12.5 1.3 %collective-permute-start.1 = (bf16[1024,128]{1,0:T(8,128)(2,1)S(1)}, bf16[1024,128]{1,0:T(8,128)(2,1)S(1)}, u32[]{:S(2)}, u32[]{:S(2)}) collective-permute-start(bf16[1024,128]{1,0:T(8,128)(2,1)S(1)} %get-tuple-element.23), channel_id=1, source_target_pairs={{2,0},{3,1},{4,2},{5,3},{6,4},{7,5},{10,8},{11,9},{12,10},{13,11},... | collective-permute-start | bytes 786440 | tf_op jit(solution)/shard_map/ppermute | solution.py:14
  13.8 4.1 %all-to-all-done = f32[32,2,128]{2,1,0:T(2,128)S(1)} async-done(((f32[32,2,128]{2,1,0:T(2,128)}), f32[32,2,128]{2,1,0:T(2,128)S(1)}, u32[]{:S(2)}, u32[]{:S(2)}) %all-to-all-start) | async-done | bytes 32800 | tf_op jit(solution)/shard_map/all_to_all | solution.py:312
  18.0 0.4 %own_grams.1 = (f32[2,128,128]{2,1,0:T(8,128)S(1)}, bf16[1024,128]{1,0:T(8,128)(2,1)S(1)}) custom-call(f32[64,128]{1,0:T(8,128)S(1)} %bitcast.17, bf16[3072,128]{1,0:T(8,128)(2,1)S(1)} %get-tuple-element.17.refs_1_), custom_call_target="tpu_custom_call" | custom-call | flops 100663296 | bytes 786432 | tf_op jit(solution)/shard_map/own_grams/pallas_call | solution.py:314
  18.4 1.3 %collective-permute-start = (f32[2,128,128]{2,1,0:T(8,128)S(1)}, f32[2,128,128]{2,1,0:T(8,128)S(1)}, u32[]{:S(2)}, u32[]{:S(2)}) collective-permute-start(f32[2,128,128]{2,1,0:T(8,128)S(1)} %get-tuple-element.18.own_gram_ref), channel_id=1, source_target_pairs={{2,0},{3,1},{4,2},{5,3},{6,4},{7,5},{10,8},{11,9},{12,10},{13,11},... | collective-permute-start | bytes 393224 | tf_op jit(solution)/shard_map/ppermute | solution.py:14
  19.7 0.1 pad_add_fusion.refs_0_
  19.8 0.0 copy-start.1
  19.8 0.0 collective-permute-done.3.refs_8_
  19.8 0.2 collective-permute-start.4
  20.0 5.8 %collective-permute-done.low_gram_ref = f32[2,128,128]{2,1,0:T(8,128)S(1)} collective-permute-done((f32[2,128,128]{2,1,0:T(8,128)S(1)}, f32[2,128,128]{2,1,0:T(8,128)S(1)}, u32[]{:S(2)}, u32[]{:S(2)}) %collective-permute-start) | collective-permute-done | bytes 131104 | tf_op jit(solution)/shard_map/ppermute | solution.py:14
  25.8 0.0 copy-done.1
  25.8 3.1 %patch_factors.1 = (f32[2,32,128]{2,1,0:T(8,128)S(1)}, bf16[128,128]{1,0:T(8,128)(2,1)S(1)}, bf16[64,128]{1,0:T(8,128)(2,1)S(1)}) custom-call(f32[2,128,128]{2,1,0:T(8,128)S(1)} %get-tuple-element.18.own_gram_ref, f32[2,128,128]{2,1,0:T(8,128)S(1)} %collective-permute-done.low_gram_ref, f32[2,32,128]{2,1,0:T(8,128)S(1)} %bitcast.19), custom_call_target="tpu_custom_call" | custom-call | flops 6000000000 | bytes 1048576 | tf_op jit(solution)/shard_map/patch_factors/pallas_call | solution.py:330
  28.9 0.0 collective-permute-done.1.refs_5_
  29.0 0.0 collective-permute-done.4.refs_9_
  29.0 1.2 %coefficients.1 = (bf16[192,128]{1,0:T(8,128)(2,1)S(1)}, bf16[192,128]{1,0:T(8,128)(2,1)S(1)}, bf16[192,128]{1,0:T(8,128)(2,1)S(1)}, bf16[192,128]{1,0:T(8,128)(2,1)S(1)}) custom-call(s32[2]{0:T(128)S(1)} %pad_add_fusion.refs_0_, bf16[128,128]{1,0:T(8,128)(2,1)S(1)} %get-tuple-element.20.refs_1_, bf16[64,128]{1,0:T(8,128)(2,1)S(1)} %get-tuple-element.21.refs_2_, ...), custom_call_target="tpu_custom_call" | custom-call | flops 268435456 | bytes 2097152 | tf_op jit(solution)/shard_map/coefficients/pallas_call | solution.py:339
  30.2 0.9 %collective-permute-start.7 = (bf16[192,128]{1,0:T(8,128)(2,1)S(1)}, bf16[192,128]{1,0:T(8,128)(2,1)S(1)}, u32[]{:S(2)}, u32[]{:S(2)}) collective-permute-start(bf16[192,128]{1,0:T(8,128)(2,1)S(1)} %get-tuple-element.27), channel_id=1, source_target_pairs={{0,6},{1,7},{2,4},{3,5},{4,2},{5,3},{6,0},{7,1},{8,14},{9,15},{10,... | collective-permute-start | bytes 147464 | tf_op jit(solution)/shard_map/ppermute | solution.py:353
  31.1 1.3 %collective-permute-start.6 = (bf16[192,128]{1,0:T(8,128)(2,1)S(1)}, bf16[192,128]{1,0:T(8,128)(2,1)S(1)}, u32[]{:S(2)}, u32[]{:S(2)}) collective-permute-start(bf16[192,128]{1,0:T(8,128)(2,1)S(1)} %get-tuple-element.26), channel_id=1, source_target_pairs={{0,4},{1,5},{2,6},{3,7},{4,0},{5,1},{6,2},{7,3},{8,12},{9,13},{10,... | collective-permute-start | bytes 147464 | tf_op jit(solution)/shard_map/ppermute | solution.py:353
  32.4 2.2 %collective-permute-start.5 = (bf16[192,128]{1,0:T(8,128)(2,1)S(1)}, bf16[192,128]{1,0:T(8,128)(2,1)S(1)}, u32[]{:S(2)}, u32[]{:S(2)}) collective-permute-start(bf16[192,128]{1,0:T(8,128)(2,1)S(1)} %get-tuple-element.25), channel_id=1, source_target_pairs={{0,2},{1,3},{2,0},{3,1},{4,6},{5,7},{6,4},{7,5},{8,10},{9,11},{10,... | collective-permute-start | bytes 147464 | tf_op jit(solution)/shard_map/ppermute | solution.py:353
  34.6 1.6 %collective-permute-done.7.refs_3_ = bf16[192,128]{1,0:T(8,128)(2,1)S(1)} collective-permute-done((bf16[192,128]{1,0:T(8,128)(2,1)S(1)}, bf16[192,128]{1,0:T(8,128)(2,1)S(1)}, u32[]{:S(2)}, u32[]{:S(2)}) %collective-permute-start.7) | collective-permute-done | bytes 49184 | tf_op jit(solution)/shard_map/ppermute | solution.py:353
  36.2 0.9 %collective-permute-done.6.refs_2_ = bf16[192,128]{1,0:T(8,128)(2,1)S(1)} collective-permute-done((bf16[192,128]{1,0:T(8,128)(2,1)S(1)}, bf16[192,128]{1,0:T(8,128)(2,1)S(1)}, u32[]{:S(2)}, u32[]{:S(2)}) %collective-permute-start.6) | collective-permute-done | bytes 49184 | tf_op jit(solution)/shard_map/ppermute | solution.py:353
  37.2 0.0 collective-permute-done.5.refs_1_
  37.2 0.1 collective-permute-start.8
  37.3 0.2 direct_traces.1.direct_ref
  37.5 1.1 %collective-permute-done.8.mate_ref = bf16[4,128,128]{2,1,0:T(8,128)(2,1)S(1)} collective-permute-done((bf16[4,128,128]{2,1,0:T(8,128)(2,1)S(1)}, bf16[4,128,128]{2,1,0:T(8,128)(2,1)S(1)}, u32[]{:S(2)}, u32[]{:S(2)}) %collective-permute-start.8) | collective-permute-done | bytes 131104 | tf_op jit(solution)/shard_map/ppermute | solution.py:355
  38.6 0.8 %source_traces.1 = (f32[2,32,128]{2,1,0:T(8,128)}, f32[128,128]{1,0:T(8,128)}) custom-call(f32[2,32,128]{2,1,0:T(8,128)S(1)} %get-tuple-element.19.near_temporal_ref, f32[128,128]{1,0:T(8,128)S(1)} %direct_traces.1.direct_ref, bf16[4,128,128]{2,1,0:T(8,128)(2,1)S(1)} %collective-permute-done.8.mate_ref), custom_call_target="tpu_custom_call" | custom-call | flops 8388608 | bytes 262144 | tf_op jit(solution)/shard_map/source_traces/pallas_call | solution.py:359
  (7 shorter events, 0.1 us)
Async XLA Ops:
  0.6 10.0 %collective-permute-start.2 = (bf16[1,128,256]{2,1,0:T(8,128)(2,1)}, bf16[1,128,256]{2,1,0:T(8,128)(2,1)S(1)}, u32[]{:S(2)}, u32[]{:S(2)}) collective-permute-start(bf16[1,128,256]{2,1,0:T(8,128)(2,1)} %refs_6_.1), channel_id=1, source_target_pairs={{0,4},{1,5},{2,6},{3,7},{4,0},{5,1},{6,2},{7,3},{8,12},{9,13},{10,... | collective-permute-start | bytes 196616 | tf_op jit(solution)/shard_map/ppermute | solution.py:325
  6.8 3.9 %copy-start = (bf16[1,128,256]{2,1,0:T(8,128)(2,1)S(1)}, bf16[1,128,256]{2,1,0:T(8,128)(2,1)}, u32[]{:S(2)}) copy-start(bf16[1,128,256]{2,1,0:T(8,128)(2,1)} %refs_6_.1) | copy-start | bytes 196612
  6.8 11.2 %all-to-all-start = ((f32[32,2,128]{2,1,0:T(2,128)}), f32[32,2,128]{2,1,0:T(2,128)S(1)}, u32[]{:S(2)}, u32[]{:S(2)}) async-start(f32[32,2,128]{2,1,0:T(2,128)} %bitcast.2), calls=%async_computation | async-start | bytes 65536 | tf_op jit(solution)/shard_map/all_to_all | solution.py:312
  10.7 9.1 %collective-permute-start.3 = (bf16[2,128,256]{2,1,0:T(8,128)(2,1)S(1)}, bf16[2,128,256]{2,1,0:T(8,128)(2,1)S(1)}, u32[]{:S(2)}, u32[]{:S(2)}) collective-permute-start(bf16[2,128,256]{2,1,0:T(8,128)(2,1)S(1)} %pad_maximum_fusion.1), channel_id=1, source_target_pairs={{0,2},{1,3},{2,0},{3,1},{4,6},{5,7},{6,4},{7,5},{8,10},{9,11},{10,... | collective-permute-start | bytes 393224 | tf_op jit(solution)/shard_map/ppermute | solution.py:325
  12.5 16.4 %collective-permute-start.1 = (bf16[1024,128]{1,0:T(8,128)(2,1)S(1)}, bf16[1024,128]{1,0:T(8,128)(2,1)S(1)}, u32[]{:S(2)}, u32[]{:S(2)}) collective-permute-start(bf16[1024,128]{1,0:T(8,128)(2,1)S(1)} %get-tuple-element.23), channel_id=1, source_target_pairs={{2,0},{3,1},{4,2},{5,3},{6,4},{7,5},{10,8},{11,9},{12,10},{13,11},... | collective-permute-start | bytes 786440 | tf_op jit(solution)/shard_map/ppermute | solution.py:14
  18.4 7.4 %collective-permute-start = (f32[2,128,128]{2,1,0:T(8,128)S(1)}, f32[2,128,128]{2,1,0:T(8,128)S(1)}, u32[]{:S(2)}, u32[]{:S(2)}) collective-permute-start(f32[2,128,128]{2,1,0:T(8,128)S(1)} %get-tuple-element.18.own_gram_ref), channel_id=1, source_target_pairs={{2,0},{3,1},{4,2},{5,3},{6,4},{7,5},{10,8},{11,9},{12,10},{13,11},... | collective-permute-start | bytes 393224 | tf_op jit(solution)/shard_map/ppermute | solution.py:14
  19.8 6.0 %copy-start.1 = (f32[1,2,32,128]{3,2,1,0:T(8,128)S(1)}, f32[1,2,32,128]{3,2,1,0:T(8,128)}, u32[]{:S(2)}) copy-start(f32[1,2,32,128]{3,2,1,0:T(8,128)} %param.6) | copy-start | bytes 98308
  19.8 9.1 %collective-permute-start.4 = (bf16[4,128,256]{2,1,0:T(8,128)(2,1)S(1)}, bf16[4,128,256]{2,1,0:T(8,128)(2,1)S(1)}, u32[]{:S(2)}, u32[]{:S(2)}) collective-permute-start(bf16[4,128,256]{2,1,0:T(8,128)(2,1)S(1)} %pad_maximum_fusion), channel_id=1, source_target_pairs={{0,1},{1,0},{2,3},{3,2},{4,5},{5,4},{6,7},{7,6},{8,9},{9,8},{10,11... | collective-permute-start | bytes 786440 | tf_op jit(solution)/shard_map/ppermute | solution.py:325
  30.2 6.1 %collective-permute-start.7 = (bf16[192,128]{1,0:T(8,128)(2,1)S(1)}, bf16[192,128]{1,0:T(8,128)(2,1)S(1)}, u32[]{:S(2)}, u32[]{:S(2)}) collective-permute-start(bf16[192,128]{1,0:T(8,128)(2,1)S(1)} %get-tuple-element.27), channel_id=1, source_target_pairs={{0,6},{1,7},{2,4},{3,5},{4,2},{5,3},{6,0},{7,1},{8,14},{9,15},{10,... | collective-permute-start | bytes 147464 | tf_op jit(solution)/shard_map/ppermute | solution.py:353
  31.1 6.0 %collective-permute-start.6 = (bf16[192,128]{1,0:T(8,128)(2,1)S(1)}, bf16[192,128]{1,0:T(8,128)(2,1)S(1)}, u32[]{:S(2)}, u32[]{:S(2)}) collective-permute-start(bf16[192,128]{1,0:T(8,128)(2,1)S(1)} %get-tuple-element.26), channel_id=1, source_target_pairs={{0,4},{1,5},{2,6},{3,7},{4,0},{5,1},{6,2},{7,3},{8,12},{9,13},{10,... | collective-permute-start | bytes 147464 | tf_op jit(solution)/shard_map/ppermute | solution.py:353
  32.4 4.7 %collective-permute-start.5 = (bf16[192,128]{1,0:T(8,128)(2,1)S(1)}, bf16[192,128]{1,0:T(8,128)(2,1)S(1)}, u32[]{:S(2)}, u32[]{:S(2)}) collective-permute-start(bf16[192,128]{1,0:T(8,128)(2,1)S(1)} %get-tuple-element.25), channel_id=1, source_target_pairs={{0,2},{1,3},{2,0},{3,1},{4,6},{5,7},{6,4},{7,5},{8,10},{9,11},{10,... | collective-permute-start | bytes 147464 | tf_op jit(solution)/shard_map/ppermute | solution.py:353
  37.2 1.4 %collective-permute-start.8 = (bf16[4,128,128]{2,1,0:T(8,128)(2,1)S(1)}, bf16[4,128,128]{2,1,0:T(8,128)(2,1)S(1)}, u32[]{:S(2)}, u32[]{:S(2)}) collective-permute-start(bf16[4,128,128]{2,1,0:T(8,128)(2,1)S(1)} %pad_maximum_fusion.2), channel_id=1, source_target_pairs={{0,1},{1,0},{2,3},{3,2},{4,5},{5,4},{6,7},{7,6},{8,9},{9,8},{10,11... | collective-permute-start | bytes 393224 | tf_op jit(solution)/shard_map/ppermute | solution.py:355
